TPU v7x, 32 devices: a whole 2x2x4 slice. The times are simulated.
32 devices in a mesh: row: 8 (over y, x, core), col: 4 (over z).
Axes of the slice: x: 2, y: 2, z: 4, core: 2. Of those that a mesh axis runs over, the one named last changes fastest.
Arguments:
- velocity: bfloat16 [2048, 8, 3, 2048], P(('row', 'col')), may hold values from -6 to 6
- deriv_x: bfloat16 [2048, 2048], replicated, may hold values from -0.125 to 0.125
- deriv_y: bfloat16 [8, 8], replicated, may hold values from -2 to 2
- deriv_z: bfloat16 [2048, 2048], replicated, may hold values from -0.125 to 0.125
- metric_x: float32 [2048], replicated, may hold values from 0.5 to 2
- metric_y: float32 [8], replicated, may hold values from 0.5 to 2
- metric_z: float32 [2048], replicated, may hold values from 0.5 to 2
- ib_target: bfloat16 [32, 128, 3, 128], P(('row', 'col')), may hold values from -6 to 6
- ib_owner: int32 [32, 128], P(('row', 'col')), may hold values from 0 to 31, as said below
- ib_block: int32 [32, 128], P(('row', 'col')), may hold values from 0 to 8191
- ib_count: int32 [32], P(('row', 'col')), may hold values from 64 to 128, as said below
Outputs:
- forced: float32 [2048, 8, 3, 2048], P(('row', 'col'))
Inputs may be any that keep to these rules, and one draw needn't show every extreme that they name: `ib_owner`: at most 8 live slots of one device name one owner; on every device the first 8 slots name one owner common to all devices. Only the first ib_count[s] slots of device s are live.
All inputs are finite; a program needn't handle non-finite values.
Results may differ from a plain program's by a relative error of at most 0.0019.
Values may be sent and summed in bfloat16 or wider, within the bound.
No kernel may reach another device: no remote copies, remote signals or barrier semaphores. Data moves between devices by JAX's collectives and lax.ppermute only.
A program may use at most 256 MiB of HBM per device.

v0:
```python
import functools

import jax
import jax.numpy as jnp
import numpy as np
from jax import lax
from jax.experimental import pallas as pl
from jax.experimental.pallas import tpu as pltpu
from jax.sharding import PartitionSpec as P

BLOCK = 128
MOST = 8
GROUP = 16
CHUNKS = 4

viscosity = 0.4
time_step = 0.2

F32 = jnp.float32
BF16 = jnp.bfloat16
AXES = ("row", "col")


def mm(a, b):
    return lax.dot_general(a, b, (((1,), (0,)), ((), ())), preferred_element_type=F32)


def mm_nt(a, b):
    return lax.dot_general(a, b, (((1,), (1,)), ((), ())), preferred_element_type=F32)


def pack_order(planes, comps):
    rows = GROUP * planes * comps
    table = np.zeros((rows, rows), np.float32)
    for y in range(planes):
        for c in range(comps):
            for z in range(GROUP):
                table[(y * comps + c) * GROUP + z, (z * comps + c) * planes + y] = 1
    return table


def unpack_order(planes, group):
    rows = group * planes
    table = np.zeros((rows, rows), np.float32)
    for y in range(planes):
        for z in range(group):
            table[z * planes + y, y * group + z] = 1
    return table


def pack_body(planes, comps, wide, order_ref, v_ref, o_ref):
    lanes = v_ref.shape[1]
    rows = order_ref.shape[0]
    for g in range(v_ref.shape[0] // rows):
        moved = mm(order_ref[...], v_ref[g * rows : (g + 1) * rows, :]).astype(BF16)
        for xg in range(lanes // wide):
            for y in range(planes):
                for c in range(comps):
                    at = (y * comps + c) * GROUP
                    o_ref[xg * planes + y, g * GROUP : (g + 1) * GROUP, c * wide : (c + 1) * wide] = moved[
                        at : at + GROUP, xg * wide : (xg + 1) * wide
                    ]


def pack(lines, order, chunk, chunks, planes, comps, devices, slab):
    columns = lines.shape[1]
    width = columns // chunks
    wide = width * planes // devices
    step = max(wide, 256)
    steps = width // step
    return pl.pallas_call(
        functools.partial(pack_body, planes, comps, wide),
        out_shape=jax.ShapeDtypeStruct((devices, slab, comps * wide), BF16),
        grid=(steps,),
        in_specs=[
            pl.BlockSpec(order.shape, lambda i: (0, 0)),
            pl.BlockSpec((lines.shape[0], step), lambda i: (0, chunk * steps + i)),
        ],
        out_specs=pl.BlockSpec((step // wide * planes, slab, comps * wide), lambda i: (i, 0, 0)),
        compiler_params=pltpu.CompilerParams(vmem_limit_bytes=48 << 20),
        cost_estimate=pl.CostEstimate(
            flops=2 * lines.shape[0] * order.shape[0] * width,
            bytes_accessed=4 * lines.shape[0] * width,
            transcendentals=0,
        ),
        name="pack",
    )(order, lines)


def depth_body(wide, block, x_ref, d_ref, m_ref, o_ref, g_ref):
    phase = pl.program_id(0)
    at = pl.multiple_of(pl.program_id(1) * block, block)
    spot = pl.ds(at, block)

    @pl.when(phase == 0)
    def _():
        g_ref[spot, :] = (mm(d_ref[...], x_ref[...]) * m_ref[spot, :]).astype(BF16)

    @pl.when(phase == 1)
    def _():
        curv = mm(d_ref[...], g_ref[...]) * m_ref[spot, :]
        grad = g_ref[spot, :].astype(F32)
        upward = x_ref[spot, 2 * wide : 3 * wide].astype(F32)
        for c in range(3):
            part = slice(c * wide, (c + 1) * wide)
            o_ref[:, part] = (viscosity * curv[:, part] - upward * grad[:, part]).astype(BF16)


def depth(x, deriv_z, metric_z):
    height, cols = x.shape
    block = min(512, height)
    return pl.pallas_call(
        functools.partial(depth_body, cols // 3, block),
        out_shape=jax.ShapeDtypeStruct(x.shape, BF16),
        grid=(2, height // block),
        in_specs=[
            pl.BlockSpec(x.shape, lambda p, i: (0, 0)),
            pl.BlockSpec((block, height), lambda p, i: (i, 0)),
            pl.BlockSpec((height, 1), lambda p, i: (0, 0)),
        ],
        out_specs=pl.BlockSpec((block, cols), lambda p, i: (i * p, 0)),
        scratch_shapes=[pltpu.VMEM(x.shape, BF16)],
        compiler_params=pltpu.CompilerParams(vmem_limit_bytes=48 << 20),
        cost_estimate=pl.CostEstimate(
            flops=4 * height * height * cols,
            bytes_accessed=4 * height * height + 4 * height * cols,
            transcendentals=0,
        ),
        name="depth",
    )(x, deriv_z, metric_z)


def marker_body(capacity, count_ref, owner_row, owner_col, block_col, t_ref, o_ref):
    count = count_ref[0]
    earlier = lax.broadcasted_iota(jnp.int32, (capacity, capacity), 0)
    later = lax.broadcasted_iota(jnp.int32, (capacity, capacity), 1)
    same = (owner_col[...] == owner_row[...]) & (earlier < later)
    position = jnp.sum(same.astype(jnp.int32), axis=0, keepdims=True)
    slot = lax.broadcasted_iota(jnp.int32, (1, capacity), 1)
    places = o_ref.shape[0]
    slotted = jnp.where(slot < count, owner_row[...] * MOST + position, places)
    placing = (lax.broadcasted_iota(jnp.int32, (places, capacity), 0) == slotted).astype(F32).astype(BF16)
    for c in range(3):
        o_ref[:, c * BLOCK : (c + 1) * BLOCK] = mm(placing, t_ref[c]).astype(BF16)
    lane = lax.broadcasted_iota(jnp.int32, (capacity, BLOCK), 1)
    high = block_col[...] // 128
    low = block_col[...] - high * 128
    label = jnp.where(lane == 0, high, jnp.where(lane == 1, low, jnp.where(lane == 2, 1, 0)))
    o_ref[:, 3 * BLOCK :] = mm(placing, label.astype(F32).astype(BF16)).astype(BF16)


def markers(ib_target, ib_owner, ib_block, ib_count, devices):
    capacity = ib_owner.shape[1]
    return pl.pallas_call(
        functools.partial(marker_body, capacity),
        out_shape=jax.ShapeDtypeStruct((devices * MOST, 4 * BLOCK), BF16),
        in_specs=[pl.BlockSpec(memory_space=pltpu.SMEM)] + [pl.BlockSpec(memory_space=pltpu.VMEM)] * 4,
        out_specs=pl.BlockSpec(memory_space=pltpu.VMEM),
        compiler_params=pltpu.CompilerParams(vmem_limit_bytes=32 << 20),
        cost_estimate=pl.CostEstimate(flops=10**8, bytes_accessed=10**6, transcendentals=0),
        name="markers",
    )(
        ib_count,
        ib_owner,
        ib_owner.reshape(capacity, 1),
        ib_block.reshape(capacity, 1),
        jnp.transpose(ib_target[0], (1, 0, 2)),
    )


def near_body(planes, comps, v_ref, dx_ref, dy_ref, mx_ref, my_ref, got_ref, p_ref, inv_ref, g_ref, s_ref):
    rows, columns = v_ref.shape
    group = rows // (planes * comps)
    lines = group * planes
    part = 512
    first = pl.program_id(0) * lines
    xblocks = columns // BLOCK
    slots = got_ref.shape[0]
    lane = lax.broadcasted_iota(jnp.int32, (8, BLOCK), 1)
    pick = jnp.where(lane == 0, 128.0, jnp.where(lane < 3, 1.0, 0.0)).astype(BF16)
    label = mm_nt(pick, got_ref[:, 3 * BLOCK :])[0:1, :].astype(jnp.int32)
    s_ref[:, : 3 * BLOCK] = got_ref[:, : 3 * BLOCK]
    s_ref[:, 3 * BLOCK :] = jnp.ones((slots, BLOCK), BF16)
    line = (first + lax.broadcasted_iota(jnp.int32, (lines, slots), 0)) * xblocks + 1
    for j in range(columns // part):
        span = slice(j * part, (j + 1) * part)
        g_ref[:, span] = (mm_nt(v_ref[...], dx_ref[span, :]) * mx_ref[:, span]).astype(BF16)
    for j in range(columns // part):
        span = slice(j * part, (j + 1) * part)
        curv = mm_nt(g_ref[...], dx_ref[span, :]) * mx_ref[:, span]
        vel = v_ref[:, span]
        grad_y = (mm(dy_ref[...], vel) * my_ref[...]).astype(BF16)
        curv = curv + mm(dy_ref[...], grad_y) * my_ref[...]
        shape = (group, comps, planes, part)
        vel = vel.astype(F32).reshape(shape)
        grad_y = grad_y.astype(F32).reshape(shape)
        grad_x = g_ref[:, span].astype(F32).reshape(shape)
        curv = curv.reshape(shape)
        tendency = viscosity * curv - (vel[:, 0:1] * grad_x + vel[:, 1:2] * grad_y)
        near = vel + time_step * tendency
        for b in range(part // BLOCK):
            chosen = (line + (j * (part // BLOCK) + b) == label).astype(F32).astype(BF16)
            share = mm(chosen, s_ref[...])
            inverse = (1.0 / (1.0 + share[:, 3 * BLOCK :])).reshape(group, planes, BLOCK)
            cells = slice(b * BLOCK, (b + 1) * BLOCK)
            place = slice(j * part + b * BLOCK, j * part + (b + 1) * BLOCK)
            inv_ref[:, :, place] = inverse
            for c in range(comps):
                pulled = share[:, c * BLOCK : (c + 1) * BLOCK].reshape(group, planes, BLOCK)
                p_ref[:, c, :, place] = (near[:, c, :, cells] + pulled) * inverse


def near(lines, deriv_x, band_y, metric_x, metric_rows, got, planes, comps, slab):
    total, columns = lines.shape
    rows = GROUP * planes * comps
    return pl.pallas_call(
        functools.partial(near_body, planes, comps),
        out_shape=(
            jax.ShapeDtypeStruct((slab, comps, planes, columns), F32),
            jax.ShapeDtypeStruct((slab, planes, columns), F32),
        ),
        grid=(total // rows,),
        in_specs=[
            pl.BlockSpec((rows, columns), lambda i: (i, 0)),
            pl.BlockSpec(deriv_x.shape, lambda i: (0, 0), pipeline_mode=pl.Buffered(1)),
            pl.BlockSpec(band_y.shape, lambda i: (0, 0)),
            pl.BlockSpec((1, columns), lambda i: (0, 0)),
            pl.BlockSpec((rows, 1), lambda i: (0, 0)),
            pl.BlockSpec(got.shape, lambda i: (0, 0)),
        ],
        out_specs=(
            pl.BlockSpec((GROUP, comps, planes, columns), lambda i: (i, 0, 0, 0)),
            pl.BlockSpec((GROUP, planes, columns), lambda i: (i, 0, 0)),
        ),
        scratch_shapes=[pltpu.VMEM((rows, columns), BF16), pltpu.VMEM(got.shape, BF16)],
        compiler_params=pltpu.CompilerParams(vmem_limit_bytes=56 << 20),
        cost_estimate=pl.CostEstimate(
            flops=4 * total * columns * columns,
            bytes_accessed=6 * total * columns + 2 * columns * columns,
            transcendentals=0,
        ),
        name="near",
    )(lines, deriv_x, band_y, metric_x, metric_rows, got)


def last_body(planes, comps, wide, group, order_ref, r_ref, inv_ref, p_ref, o_ref):
    slab = p_ref.shape[0]
    for xg in range(r_ref.shape[0] // planes):
        for g in range(slab // group):
            some = slice(g * group, (g + 1) * group)
            taken = r_ref[xg * planes : (xg + 1) * planes, some, :].reshape(planes * group, comps * wide)
            moved = mm(order_ref[...], taken) * time_step
            cells = slice(xg * wide, (xg + 1) * wide)
            inverse = inv_ref[some, :, cells]
            for c in range(comps):
                term = moved[:, c * wide : (c + 1) * wide].reshape(group, planes, wide)
                o_ref[some, c, :, cells] = p_ref[some, c, :, cells] + term * inverse


def last(field, returned, inverse, order, chunk, chunks, planes, comps, devices, slab, group):
    columns = field.shape[-1]
    width = columns // chunks
    wide = width * planes // devices
    step = wide
    steps = width // step
    spec = pl.BlockSpec((slab, comps, planes, step), lambda i: (0, 0, 0, chunk * steps + i))
    return pl.pallas_call(
        functools.partial(last_body, planes, comps, wide, group),
        out_shape=jax.ShapeDtypeStruct(field.shape, F32),
        grid=(steps,),
        in_specs=[
            pl.BlockSpec(order.shape, lambda i: (0, 0)),
            pl.BlockSpec((step // wide * planes, slab, comps * wide), lambda i: (i, 0, 0)),
            pl.BlockSpec((slab, planes, step), lambda i: (0, 0, chunk * steps + i)),
            spec,
        ],
        out_specs=spec,
        input_output_aliases={3: 0},
        compiler_params=pltpu.CompilerParams(vmem_limit_bytes=48 << 20),
        cost_estimate=pl.CostEstimate(
            flops=2 * slab * comps * planes * width * 256,
            bytes_accessed=12 * slab * comps * planes * width,
            transcendentals=0,
        ),
        name="last",
    )(order, returned, inverse, field)


def exchange(x):
    return lax.all_to_all(x, AXES, split_axis=0, concat_axis=0, tiled=True)


def local(
    velocity,
    deriv_x,
    deriv_y,
    deriv_z,
    metric_x,
    metric_y,
    metric_z,
    ib_target,
    ib_owner,
    ib_block,
    ib_count,
):
    slab, planes, comps, columns = velocity.shape
    devices = lax.axis_size("row") * lax.axis_size("col")
    pairs = planes * (columns // BLOCK) // devices
    chunks = min(CHUNKS, pairs)
    group = min(32, slab)
    lines = jnp.transpose(velocity, (0, 2, 1, 3)).reshape(slab * comps * planes, columns)
    order = jnp.asarray(pack_order(planes, comps), BF16)
    back = jnp.asarray(unpack_order(planes, group), BF16)
    arrived = []
    for k in range(chunks):
        arrived.append(exchange(pack(lines, order, k, chunks, planes, comps, devices, slab)))
        if k == 0:
            marked = markers(ib_target, ib_owner, ib_block, ib_count, devices)
            got = exchange(marked.reshape(devices, MOST, 4 * BLOCK)).reshape(devices * MOST, 4 * BLOCK)
    returned = []
    for k in range(chunks):
        x = arrived[k]
        result = depth(x.reshape(devices * slab, x.shape[2]), deriv_z, metric_z[:, None])
        returned.append(exchange(result.reshape(x.shape)))
    rows = GROUP * planes * comps
    band_y = jnp.kron(jnp.eye(GROUP * comps, dtype=F32), deriv_y.astype(F32)).astype(BF16)
    metric_rows = jnp.tile(metric_y, GROUP * comps)[:, None]
    field, inverse = near(
        lines, deriv_x, band_y, metric_x[None, :], metric_rows, got, planes, comps, slab
    )
    for k in range(chunks):
        field = last(
            field, returned[k], inverse, back, k, chunks, planes, comps, devices, slab, group
        )
    return jnp.transpose(field, (0, 2, 1, 3))


def solution(mesh):
    in_specs = (
        P(AXES, None, None, None),
        P(),
        P(),
        P(),
        P(),
        P(),
        P(),
        P(AXES, None, None, None),
        P(AXES, None),
        P(AXES, None),
        P(AXES),
    )
    out_specs = P(AXES, None, None, None)
    return jax.shard_map(local, mesh=mesh, in_specs=in_specs, out_specs=out_specs, check_vma=False)
```

profile of v0, /device:TPU:8, one launch (start us, length us, event | category | flops | bytes accessed | tf_op | source)
XLA Modules:
  0.0 395.6 jit_solution(13720075763849677870)
XLA Ops:
  4.7 6.0 %all-to-all-start.2 = ((bf16[32,8,512]{2,1,0:T(8,128)(2,1)}), bf16[32,8,512]{2,1,0:T(8,128)(2,1)S(1)}, u32[]{:S(2)}, u32[]{:S(2)}) async-start(bf16[32,8,512]{2,1,0:T(8,128)(2,1)} %bitcast.11), calls=%async_computation.2 | async-start | bytes 524288 | tf_op jit(solution)/shard_map/all_to_all | solution.py:290
  11.7 3.2 pack.7
  14.9 5.4 %all-to-all-done.2 = bf16[32,8,512]{2,1,0:T(8,128)(2,1)S(1)} async-done(((bf16[32,8,512]{2,1,0:T(8,128)(2,1)}), bf16[32,8,512]{2,1,0:T(8,128)(2,1)S(1)}, u32[]{:S(2)}, u32[]{:S(2)}) %all-to-all-start.2) | async-done | bytes 262176 | tf_op jit(solution)/shard_map/all_to_all | solution.py:290
  21.0 3.4 all-to-all-start.7
  24.4 3.2 pack.6
  27.6 34.4 %all-to-all-done.7 = bf16[32,64,384]{2,1,0:T(8,128)(2,1)S(1)} async-done(((bf16[32,64,384]{2,1,0:T(8,128)(2,1)}), bf16[32,64,384]{2,1,0:T(8,128)(2,1)S(1)}, u32[]{:S(2)}, u32[]{:S(2)}) %all-to-all-start.7) | async-done | bytes 1572896 | tf_op jit(solution)/shard_map/all_to_all | solution.py:290
  62.0 1.1 copy-done.11
  63.2 2.9 all-to-all-start.5
  66.1 3.2 pack.5
  69.3 34.4 %all-to-all-done.5 = bf16[32,64,384]{2,1,0:T(8,128)(2,1)S(1)} async-done(((bf16[32,64,384]{2,1,0:T(8,128)(2,1)}), bf16[32,64,384]{2,1,0:T(8,128)(2,1)S(1)}, u32[]{:S(2)}, u32[]{:S(2)}) %all-to-all-start.5) | async-done | bytes 1572896 | tf_op jit(solution)/shard_map/all_to_all | solution.py:290
  103.7 1.2 copy-done.9
  104.9 2.9 all-to-all-start.3
  107.8 3.2 pack.4
  111.0 34.4 %all-to-all-done.3 = bf16[32,64,384]{2,1,0:T(8,128)(2,1)S(1)} async-done(((bf16[32,64,384]{2,1,0:T(8,128)(2,1)}), bf16[32,64,384]{2,1,0:T(8,128)(2,1)S(1)}, u32[]{:S(2)}, u32[]{:S(2)}) %all-to-all-start.3) | async-done | bytes 1572896 | tf_op jit(solution)/shard_map/all_to_all | solution.py:290
  145.4 1.2 copy-done.5
  146.6 2.9 all-to-all-start
  149.9 1.8 copy-done.12
  151.7 12.9 %depth.7 = bf16[2048,384]{1,0:T(8,128)(2,1)S(1)} custom-call(bf16[2048,384]{1,0:T(8,128)(2,1)S(1)} %bitcast.26, bf16[2048,2048]{1,0:T(8,128)(2,1)} %d_ref.7, f32[2048,1]{1,0:T(8,128)S(1)} %copy.20.m_ref), custom_call_target="tpu_custom_call" | custom-call | flops 6442450944 | bytes 19922944 | tf_op jit(solution)/shard_map/depth/pallas_call | solution.py:112
  164.6 1.1 copy-done.15
  165.7 21.4 %all-to-all-done = bf16[32,64,384]{2,1,0:T(8,128)(2,1)S(1)} async-done(((bf16[32,64,384]{2,1,0:T(8,128)(2,1)}), bf16[32,64,384]{2,1,0:T(8,128)(2,1)S(1)}, u32[]{:S(2)}, u32[]{:S(2)}) %all-to-all-start) | async-done | bytes 1572896 | tf_op jit(solution)/shard_map/all_to_all | solution.py:290
  187.1 1.1 copy-done.7
  188.2 2.9 all-to-all-start.8
  191.1 1.4 copy-done.10
  192.5 1.2 copy-done.18
  193.8 12.9 %depth.6 = bf16[2048,384]{1,0:T(8,128)(2,1)S(1)} custom-call(bf16[2048,384]{1,0:T(8,128)(2,1)S(1)} %bitcast.25, bf16[2048,2048]{1,0:T(8,128)(2,1)} %d_ref.7, f32[2048,1]{1,0:T(8,128)S(1)} %copy-done.18), custom_call_target="tpu_custom_call" | custom-call | flops 6442450944 | bytes 19922944 | tf_op jit(solution)/shard_map/depth/pallas_call | solution.py:112
  206.7 1.2 copy-done.16
  207.8 20.9 %all-to-all-done.8.r_ref = bf16[32,64,384]{2,1,0:T(8,128)(2,1)S(1)} async-done(((bf16[32,64,384]{2,1,0:T(8,128)(2,1)}), bf16[32,64,384]{2,1,0:T(8,128)(2,1)S(1)}, u32[]{:S(2)}, u32[]{:S(2)}) %all-to-all-start.8) | async-done | bytes 1572896 | tf_op jit(solution)/shard_map/all_to_all | solution.py:290
  228.8 2.9 all-to-all-start.6
  231.7 1.4 copy-done.6
  233.1 1.2 copy-done.19
  234.3 12.9 %depth.5 = bf16[2048,384]{1,0:T(8,128)(2,1)S(1)} custom-call(bf16[2048,384]{1,0:T(8,128)(2,1)S(1)} %bitcast.23, bf16[2048,2048]{1,0:T(8,128)(2,1)} %d_ref.7, f32[2048,1]{1,0:T(8,128)S(1)} %copy-done.19), custom_call_target="tpu_custom_call" | custom-call | flops 6442450944 | bytes 19922944 | tf_op jit(solution)/shard_map/depth/pallas_call | solution.py:112
  248.3 20.9 %all-to-all-done.6.r_ref = bf16[32,64,384]{2,1,0:T(8,128)(2,1)S(1)} async-done(((bf16[32,64,384]{2,1,0:T(8,128)(2,1)}), bf16[32,64,384]{2,1,0:T(8,128)(2,1)S(1)}, u32[]{:S(2)}, u32[]{:S(2)}) %all-to-all-start.6) | async-done | bytes 1572896 | tf_op jit(solution)/shard_map/all_to_all | solution.py:290
  269.3 3.2 all-to-all-start.4
  272.4 1.4 copy-done.8
  273.8 1.2 copy-done.20
  275.1 12.9 %depth.4 = bf16[2048,384]{1,0:T(8,128)(2,1)S(1)} custom-call(bf16[2048,384]{1,0:T(8,128)(2,1)S(1)} %bitcast.24, bf16[2048,2048]{1,0:T(8,128)(2,1)} %d_ref.7, f32[2048,1]{1,0:T(8,128)S(1)} %copy-done.20), custom_call_target="tpu_custom_call" | custom-call | flops 6442450944 | bytes 19922944 | tf_op jit(solution)/shard_map/depth/pallas_call | solution.py:112
  288.0 1.2 copy-done.13
  289.2 20.7 %all-to-all-done.4.r_ref = bf16[32,64,384]{2,1,0:T(8,128)(2,1)} async-done(((bf16[32,64,384]{2,1,0:T(8,128)(2,1)}), bf16[32,64,384]{2,1,0:T(8,128)(2,1)}, u32[]{:S(2)}, u32[]{:S(2)}) %all-to-all-start.4) | async-done | bytes 1572896 | tf_op jit(solution)/shard_map/all_to_all | solution.py:290
  309.9 3.5 all-to-all-start.1
  313.4 3.0 multiply_convert_fusion
  316.4 7.1 %convert_element_type.18.dy_ref = bf16[384,384]{1,0:T(8,128)(2,1)} reshape(bf16[48,8,48,8]{3,2,1,0:T(8,128)(2,1)} %multiply_convert_fusion) | data formatting | bytes 589824 | tf_op jit(solution)/shard_map/convert_element_type | solution.py:326
  324.3 47.4 %near.1 = (f32[64,3,8,2048]{3,2,1,0:T(8,128)}, f32[64,8,2048]{2,1,0:T(8,128)}) custom-call(bf16[1536,2048]{1,0:T(8,128)(2,1)} %bitcast.37, bf16[2048,2048]{1,0:T(8,128)(2,1)} %dx_ref.1, bf16[384,384]{1,0:T(8,128)(2,1)} %convert_element_type.18.dy_ref, f32[1,2048]{1,0:T(1,128)} %bitcast.41, f32[384,1]{1,0:T(8,128)} %broadcast_in_dim_tile.4.my_ref, ...), custom_call_target="tpu_custom_call" | custom-call | flops 25769803776 | bytes 27262976 | tf_op jit(solution)/shard_map/near/pallas_call | solution.py:216
  371.7 2.2 copy-done
  373.9 4.7 %last.4.p_ref = f32[64,3,8,2048]{3,2,1,0:T(8,128)} custom-call(bf16[256,256]{1,0:T(8,128)(2,1)S(1)} %copy-done.4, bf16[32,64,384]{2,1,0:T(8,128)(2,1)S(1)} %all-to-all-done.8.r_ref, f32[64,8,2048]{2,1,0:T(8,128)S(1)} %copy-done, f32[64,3,8,2048]{3,2,1,0:T(8,128)} %get-tuple-element.8.p_ref), custom_call_target="tpu_custom_call", output_to_operand_aliasing={{}: (3, {})} | custom-call | flops 402653184 | bytes 9437184 | tf_op jit(solution)/shard_map/last/pallas_call | solution.py:267
  378.6 4.7 %last.5.p_ref = f32[64,3,8,2048]{3,2,1,0:T(8,128)} custom-call(bf16[256,256]{1,0:T(8,128)(2,1)S(1)} %copy-done.4, bf16[32,64,384]{2,1,0:T(8,128)(2,1)S(1)} %all-to-all-done.6.r_ref, f32[64,8,2048]{2,1,0:T(8,128)S(1)} %copy-done, f32[64,3,8,2048]{3,2,1,0:T(8,128)} %last.4.p_ref), custom_call_target="tpu_custom_call", output_to_operand_aliasing={{}: (3, {})} | custom-call | flops 402653184 | bytes 9437184 | tf_op jit(solution)/shard_map/last/pallas_call | solution.py:267
  383.4 5.0 %last.6.p_ref = f32[64,3,8,2048]{3,2,1,0:T(8,128)} custom-call(bf16[256,256]{1,0:T(8,128)(2,1)S(1)} %copy-done.4, bf16[32,64,384]{2,1,0:T(8,128)(2,1)} %all-to-all-done.4.r_ref, f32[64,8,2048]{2,1,0:T(8,128)S(1)} %copy-done, f32[64,3,8,2048]{3,2,1,0:T(8,128)} %last.5.p_ref), custom_call_target="tpu_custom_call", output_to_operand_aliasing={{}: (3, {})} | custom-call | flops 402653184 | bytes 9437184 | tf_op jit(solution)/shard_map/last/pallas_call | solution.py:267
  388.4 2.2 copy-done.1
  390.6 5.0 %last.7 = f32[64,3,8,2048]{3,2,1,0:T(8,128)} custom-call(bf16[256,256]{1,0:T(8,128)(2,1)S(1)} %copy-done.4, bf16[32,64,384]{2,1,0:T(8,128)(2,1)} %all-to-all-done.1.r_ref, f32[64,8,2048]{2,1,0:T(8,128)S(1)} %copy-done.1, f32[64,3,8,2048]{3,2,1,0:T(8,128)} %last.6.p_ref), custom_call_target="tpu_custom_call", output_to_operand_aliasing={{}: (3, {})} | custom-call | flops 402653184 | bytes 9437184 | tf_op jit(solution)/shard_map/last/pallas_call | solution.py:267
  (47 shorter events, 8.1 us)
Async XLA Ops:
  2.2 0.9 copy-start.21
  3.1 0.7 copy-start.22
  4.7 15.6 %all-to-all-start.2 = ((bf16[32,8,512]{2,1,0:T(8,128)(2,1)}), bf16[32,8,512]{2,1,0:T(8,128)(2,1)S(1)}, u32[]{:S(2)}, u32[]{:S(2)}) async-start(bf16[32,8,512]{2,1,0:T(8,128)(2,1)} %bitcast.11), calls=%async_computation.2 | async-start | bytes 524288 | tf_op jit(solution)/shard_map/all_to_all | solution.py:290
  10.8 1.0 copy-start.2
  14.9 9.5 %copy-start.3 = (bf16[384,384]{1,0:T(8,128)(2,1)S(1)}, bf16[384,384]{1,0:T(8,128)(2,1)}, u32[]{:S(2)}) copy-start(bf16[384,384]{1,0:T(8,128)(2,1)} %constant.4.clone.order_ref) | copy-start | bytes 884740
  20.3 0.7 copy-start.23
  21.0 41.0 %all-to-all-start.7 = ((bf16[32,64,384]{2,1,0:T(8,128)(2,1)}), bf16[32,64,384]{2,1,0:T(8,128)(2,1)S(1)}, u32[]{:S(2)}, u32[]{:S(2)}) async-start(bf16[32,64,384]{2,1,0:T(8,128)(2,1)} %pack.7), calls=%async_computation.7 | async-start | bytes 3145728 | tf_op jit(solution)/shard_map/all_to_all | solution.py:290
  62.0 1.2 copy-start.11
  63.2 40.5 %all-to-all-start.5 = ((bf16[32,64,384]{2,1,0:T(8,128)(2,1)}), bf16[32,64,384]{2,1,0:T(8,128)(2,1)S(1)}, u32[]{:S(2)}, u32[]{:S(2)}) async-start(bf16[32,64,384]{2,1,0:T(8,128)(2,1)} %pack.6), calls=%async_computation.5 | async-start | bytes 3145728 | tf_op jit(solution)/shard_map/all_to_all | solution.py:290
  103.7 1.2 copy-start.9
  104.9 40.5 %all-to-all-start.3 = ((bf16[32,64,384]{2,1,0:T(8,128)(2,1)}), bf16[32,64,384]{2,1,0:T(8,128)(2,1)S(1)}, u32[]{:S(2)}, u32[]{:S(2)}) async-start(bf16[32,64,384]{2,1,0:T(8,128)(2,1)} %pack.5), calls=%async_computation.3 | async-start | bytes 3145728 | tf_op jit(solution)/shard_map/all_to_all | solution.py:290
  111.0 38.5 %copy-start.24 = (f32[2048]{0:T(1024)S(1)}, f32[2048]{0:T(1024)}, u32[]{:S(2)}) copy-start(f32[2048]{0:T(1024)} %param.19) | copy-start | bytes 24580
  145.4 1.2 copy-start.5
  146.6 40.5 %all-to-all-start = ((bf16[32,64,384]{2,1,0:T(8,128)(2,1)}), bf16[32,64,384]{2,1,0:T(8,128)(2,1)S(1)}, u32[]{:S(2)}, u32[]{:S(2)}) async-start(bf16[32,64,384]{2,1,0:T(8,128)(2,1)} %pack.4), calls=%async_computation | async-start | bytes 3145728 | tf_op jit(solution)/shard_map/all_to_all | solution.py:290
  149.9 14.7 %copy-start.17 = (f32[2048,1]{1,0:T(8,128)}, f32[2048,1]{1,0:T(8,128)S(1)}, u32[]{:S(2)}) copy-start(f32[2048,1]{1,0:T(8,128)S(1)} %copy.20.m_ref) | copy-start | bytes 24580
  149.9 1.8 copy-start.12
  164.6 1.2 copy-start.15
  187.1 1.1 copy-start.7
  188.2 40.5 %all-to-all-start.8 = ((bf16[32,64,384]{2,1,0:T(8,128)(2,1)}), bf16[32,64,384]{2,1,0:T(8,128)(2,1)S(1)}, u32[]{:S(2)}, u32[]{:S(2)}) async-start(bf16[32,64,384]{2,1,0:T(8,128)(2,1)} %bitcast.29), calls=%async_computation.8 | async-start | bytes 3145728 | tf_op jit(solution)/shard_map/all_to_all | solution.py:290
  191.1 1.4 copy-start.10
  192.5 1.2 copy-start.18
  206.7 1.2 copy-start.16
  228.8 40.5 %all-to-all-start.6 = ((bf16[32,64,384]{2,1,0:T(8,128)(2,1)}), bf16[32,64,384]{2,1,0:T(8,128)(2,1)S(1)}, u32[]{:S(2)}, u32[]{:S(2)}) async-start(bf16[32,64,384]{2,1,0:T(8,128)(2,1)} %bitcast.30), calls=%async_computation.6 | async-start | bytes 3145728 | tf_op jit(solution)/shard_map/all_to_all | solution.py:290
  231.7 1.4 copy-start.6
  233.1 1.2 copy-start.19
  247.2 1.1 copy-start.14
  269.3 40.6 %all-to-all-start.4 = ((bf16[32,64,384]{2,1,0:T(8,128)(2,1)}), bf16[32,64,384]{2,1,0:T(8,128)(2,1)}, u32[]{:S(2)}, u32[]{:S(2)}) async-start(bf16[32,64,384]{2,1,0:T(8,128)(2,1)} %bitcast.28), calls=%async_computation.4 | async-start | bytes 3145728 | tf_op jit(solution)/shard_map/all_to_all | solution.py:290
  272.4 1.4 copy-start.8
  273.8 1.2 copy-start.20
  288.0 1.3 copy-start.13
  309.9 3.5 copy-start.25
  309.9 78.5 %all-to-all-start.1 = ((bf16[32,64,384]{2,1,0:T(8,128)(2,1)}), bf16[32,64,384]{2,1,0:T(8,128)(2,1)}, u32[]{:S(2)}, u32[]{:S(2)}) async-start(bf16[32,64,384]{2,1,0:T(8,128)(2,1)} %bitcast.27), calls=%async_computation.1 | async-start | bytes 3145728 | tf_op jit(solution)/shard_map/all_to_all | solution.py:290
  316.4 7.1 %copy-start.26 = (f32[8]{0:T(128)S(1)}, f32[8]{0:T(128)}, u32[]{:S(2)}) copy-start(f32[8]{0:T(128)} %param.18) | copy-start | bytes 100
  324.3 47.4 %copy-start.4 = (bf16[256,256]{1,0:T(8,128)(2,1)S(1)}, bf16[256,256]{1,0:T(8,128)(2,1)}, u32[]{:S(2)}) copy-start(bf16[256,256]{1,0:T(8,128)(2,1)} %constant.5.clone.order_ref) | copy-start | bytes 393220
  371.7 2.2 copy-start
  388.4 2.2 copy-start.1
where the time goes:
time: 399 us; the launch traced here: 396 us
  waiting for transfers between devices  193 us (48%)
  Pallas kernels  132 us (33%)
  local copies, waits for them, and re-layouts  36.4 us (9%)
  starting transfers between devices  30.5 us (8%)
    all_to_all x9, waiting for transfers between devices, exchange(): return lax.all_to_all(x, AXES, split_axis=0, concat_axis=0, tiled=True)  193 us
    pallas_call x4, Pallas kernels, depth(): pl.pallas_call(functools.partial(depth_body, cols // 3, block), out_shape...  51.6 us
    pallas_call x1, Pallas kernels, near(): pl.pallas_call(functools.partial(near_body, planes, comps), out_shape=(ja...  47.4 us
    all_to_all x9, starting transfers between devices, exchange(): return lax.all_to_all(x, AXES, split_axis=0, concat_axis=0, tiled=True)  30.5 us
    unnamed x54, local copies, waits for them, and re-layouts  26.6 us
    pallas_call x4, Pallas kernels, last(): pl.pallas_call(functools.partial(last_body, planes, comps, wide, group),...  19.5 us
    pallas_call x4, Pallas kernels, pack(): pl.pallas_call(functools.partial(pack_body, planes, comps, wide), out_sha...  12.8 us
  transfers between devices with their start and end apart: 9, of which 8 were waited for; matrix products, arithmetic and copies ran while one was open for 3% of the time, Pallas kernels for 32%

commit v1 on v0

v1 whole, which is shorter than its diff:
```python
import functools

import jax
import jax.numpy as jnp
import numpy as np
from jax import lax
from jax.experimental import pallas as pl
from jax.experimental.pallas import tpu as pltpu
from jax.sharding import PartitionSpec as P

BLOCK = 128
MOST = 8
GROUP = 16
QUARTERS = 4
VMEM = 60 << 20
SHORT = 1
LONG = 10**12

viscosity = 0.4
time_step = 0.2

F32 = jnp.float32
BF16 = jnp.bfloat16
AXES = ("row", "col")


def cost(flops):
    return pl.CostEstimate(flops=flops, bytes_accessed=1, transcendentals=0)


def mm(a, b):
    return lax.dot_general(a, b, (((1,), (0,)), ((), ())), preferred_element_type=F32)


def mm_nt(a, b):
    return lax.dot_general(a, b, (((1,), (1,)), ((), ())), preferred_element_type=F32)


def pack_order(planes, comps):
    rows = GROUP * planes * comps
    table = np.zeros((rows, rows), np.float32)
    for y in range(planes):
        for c in range(comps):
            for z in range(GROUP):
                table[(y * comps + c) * GROUP + z, (z * comps + c) * planes + y] = 1
    return table


def unpack_order(planes, group):
    rows = group * planes
    table = np.zeros((rows, rows), np.float32)
    for y in range(planes):
        for z in range(group):
            table[z * planes + y, y * group + z] = 1
    return table


def place_rows(o_ref, moved, planes, comps, wide, at_rows, spot):
    for y in range(planes):
        for c in range(comps):
            at = (y * comps + c) * GROUP
            o_ref[y, at_rows, c * wide : (c + 1) * wide] = moved[at : at + GROUP, spot]


def pack_body(planes, comps, wide, order_ref, v_ref, o_ref):
    lanes = v_ref.shape[1]
    rows = order_ref.shape[0]
    for g in range(v_ref.shape[0] // rows):
        moved = mm(order_ref[...], v_ref[g * rows : (g + 1) * rows, :]).astype(BF16)
        for xg in range(lanes // wide):
            place_rows(
                o_ref.at[:, xg],
                moved,
                planes,
                comps,
                wide,
                slice(g * GROUP, (g + 1) * GROUP),
                slice(xg * wide, (xg + 1) * wide),
            )


def pack(lines, order, count, planes, comps, groups, slab):
    step = 2 * BLOCK
    steps = groups // 2
    return pl.pallas_call(
        functools.partial(pack_body, planes, comps, BLOCK),
        out_shape=jax.ShapeDtypeStruct((planes, groups, count * slab, comps * BLOCK), BF16),
        grid=(count, steps),
        in_specs=[
            pl.BlockSpec(order.shape, lambda q, i: (0, 0)),
            pl.BlockSpec((lines.shape[0], step), lambda q, i: (0, q * steps + i)),
        ],
        out_specs=pl.BlockSpec((planes, 2, slab, comps * BLOCK), lambda q, i: (0, i, q, 0)),
        compiler_params=pltpu.CompilerParams(vmem_limit_bytes=VMEM),
        cost_estimate=cost(SHORT),
        name="pack",
    )(order, lines)


def pack_apart_body(planes, comps, wide, ways, count, steps, me_ref, order_ref, *rest):
    v_refs, o_refs = rest[:ways], rest[ways + count :]
    step = pl.program_id(0)

    @pl.when(step < steps)
    def _():
        whole = jnp.concatenate([v_ref[...] for v_ref in v_refs], axis=1)
        moved = mm(order_ref[...], whole).astype(BF16)
        for k in range(ways):
            place_rows(o_refs[k], moved, planes, comps, wide, slice(None), slice(k * wide, (k + 1) * wide))

    if count >= ways:
        m_refs = rest[ways : 2 * ways]

        @pl.when(step == steps)
        def _():
            for k in range(ways):
                o_refs[k][:, :MOST, :] = m_refs[k][:, 0, :, : comps * BLOCK]
                o_refs[k][:, MOST:, :BLOCK] = m_refs[k][:, 0, :, comps * BLOCK :]
                o_refs[k][:, MOST:, BLOCK:] = jnp.zeros((planes, MOST, (comps - 1) * BLOCK), BF16)


def pack_apart(lines, order, me, chunk, planes, comps, ways, slab, after, marked=None):
    total = lines.shape[0]
    wide = BLOCK
    rows = order.shape[0]
    steps = total // rows
    more = 0 if marked is None else 1
    given = () if marked is None else (marked,) * ways
    return pl.pallas_call(
        functools.partial(pack_apart_body, planes, comps, wide, ways, len(given) + len(after), steps),
        out_shape=(jax.ShapeDtypeStruct((planes, slab + more * GROUP, comps * wide), BF16),) * ways,
        grid_spec=pltpu.PrefetchScalarGridSpec(
            num_scalar_prefetch=1,
            grid=(steps + more,),
            in_specs=[pl.BlockSpec(order.shape, lambda i, m: (0, 0))]
            + [
                pl.BlockSpec(
                    (rows, wide), lambda i, m, k=k: (jnp.minimum(i, steps - 1), chunk * ways + (m[0] ^ k))
                )
                for k in range(ways)
            ]
            + [
                pl.BlockSpec((planes, 1, MOST, (comps + 1) * BLOCK), lambda i, m, k=k: (0, m[0] ^ k, 0, 0))
                for k in range(ways if more else 0)
            ]
            + [pl.BlockSpec(memory_space=pltpu.HBM)] * len(after),
            out_specs=(pl.BlockSpec((planes, GROUP, comps * wide), lambda i, m: (0, i, 0)),) * ways,
        ),
        compiler_params=pltpu.CompilerParams(vmem_limit_bytes=VMEM),
        cost_estimate=cost(SHORT),
        name="pack_apart",
    )(me, order, *([lines] * ways), *given, *after)


def join_body(ways, *refs):
    o_ref = refs[-1]
    for k in range(ways):
        o_ref[:, k] = refs[k][...]


def join(pieces, after):
    ways = len(pieces)
    planes, height, cols = pieces[0].shape
    half = planes // 2
    return pl.pallas_call(
        functools.partial(join_body, ways),
        out_shape=jax.ShapeDtypeStruct((planes, ways, height, cols), BF16),
        grid=(2,),
        in_specs=[pl.BlockSpec((half, height, cols), lambda i: (i, 0, 0))] * ways
        + [pl.BlockSpec(memory_space=pltpu.HBM)] * len(after),
        out_specs=pl.BlockSpec((half, ways, height, cols), lambda i: (i, 0, 0, 0)),
        compiler_params=pltpu.CompilerParams(vmem_limit_bytes=VMEM),
        cost_estimate=cost(LONG),
        name="join",
    )(*pieces, *after)


def split_body(ways, count, x_ref, *rest):
    for k in range(1, ways):
        rest[count + k - 1][...] = x_ref[:, k]


def split(x, quarter, slab, after):
    planes, ways, _, cols = x.shape
    half = planes // 2
    return pl.pallas_call(
        functools.partial(split_body, ways, len(after)),
        out_shape=(jax.ShapeDtypeStruct((planes, slab, cols), BF16),) * (ways - 1),
        grid=(2,),
        in_specs=[pl.BlockSpec((half, ways, slab, cols), lambda i: (i, 0, quarter, 0))]
        + [pl.BlockSpec(memory_space=pltpu.HBM)] * len(after),
        out_specs=(pl.BlockSpec((half, slab, cols), lambda i: (i, 0, 0)),) * (ways - 1),
        compiler_params=pltpu.CompilerParams(vmem_limit_bytes=VMEM),
        cost_estimate=cost(SHORT),
        name="split",
    )(x, *after)


def depth_body(count, slab, block, extra, near_in, near_out, me_ref, x_ref, d_ref, m_ref, *rest):
    o_ref, s_ref, g_ref = rest[extra:]
    tall, ways, _, cols = x_ref.shape
    wide = cols // 3
    phase = pl.program_id(0)
    step = pl.program_id(1)
    spot = pl.ds(pl.multiple_of(step * block, block), block)
    me = me_ref[0]

    @pl.when((phase == 0) & (step == 0))
    def _():
        for r in range(tall):
            for k in range(ways):
                to = pl.multiple_of((r * ways + (me ^ k if near_in else k)) * slab, slab)
                for q in range(count):
                    s_ref[pl.ds(to, slab), q * cols : (q + 1) * cols] = x_ref[r, k, q * slab : (q + 1) * slab]

    @pl.when(phase == 0)
    def _():
        g_ref[spot, :] = (mm(d_ref[...], s_ref[...]) * m_ref[spot, :]).astype(BF16)

    @pl.when(phase == 1)
    def _():
        curv = mm(d_ref[...], g_ref[...]) * m_ref[spot, :]
        grad = g_ref[spot, :].astype(F32)
        each = block // slab
        for q in range(count):
            upward = s_ref[spot, q * cols + 2 * wide : q * cols + 3 * wide].astype(F32)
            for c in range(3):
                part = slice(q * cols + c * wide, q * cols + (c + 1) * wide)
                term = (viscosity * curv[:, part] - upward * grad[:, part]).astype(BF16)
                for n in range(each):
                    r = step * (each // ways) + n // ways
                    k = me ^ (n % ways) if near_out else n % ways
                    o_ref[r, k, q * slab : (q + 1) * slab, c * wide : (c + 1) * wide] = term[
                        n * slab : (n + 1) * slab, :
                    ]


def depth(x, me, deriv_z, metric_z, count, slab, near_in, near_out, after, place=0, total=None, held=()):
    tall, ways, _, cols = x.shape
    shape = (tall, ways, count * slab, cols)
    extra = tuple(held) + tuple(after)
    height = deriv_z.shape[0]
    block = 512
    return pl.pallas_call(
        functools.partial(depth_body, count, slab, block, len(extra), near_in, near_out),
        out_shape=jax.ShapeDtypeStruct((tall, ways, (total or count) * slab, cols), BF16),
        grid_spec=pltpu.PrefetchScalarGridSpec(
            num_scalar_prefetch=1,
            grid=(2, height // block),
            in_specs=[
                pl.BlockSpec(shape, lambda p, i, m: (0, 0, 0, 0)),
                pl.BlockSpec((block, height), lambda p, i, m: (i, 0)),
                pl.BlockSpec((height, 1), lambda p, i, m: (0, 0)),
            ]
            + [pl.BlockSpec(memory_space=pltpu.HBM)] * len(extra),
            out_specs=pl.BlockSpec(shape, lambda p, i, m: (0, 0, place, 0)),
            scratch_shapes=[pltpu.VMEM((height, count * cols), BF16), pltpu.VMEM((height, count * cols), BF16)],
        ),
        input_output_aliases={4: 0} if held else {},
        compiler_params=pltpu.CompilerParams(vmem_limit_bytes=VMEM),
        cost_estimate=cost(SHORT),
        name="depth",
    )(me, x, deriv_z, metric_z, *extra)


def marker_body(capacity, count_ref, owner_row, owner_col, block_col, t_ref, o_ref):
    count = count_ref[0]
    earlier = lax.broadcasted_iota(jnp.int32, (capacity, capacity), 0)
    later = lax.broadcasted_iota(jnp.int32, (capacity, capacity), 1)
    same = (owner_col[...] == owner_row[...]) & (earlier < later)
    position = jnp.sum(same.astype(jnp.int32), axis=0, keepdims=True)
    slot = lax.broadcasted_iota(jnp.int32, (1, capacity), 1)
    places = o_ref.shape[0]
    slotted = jnp.where(slot < count, owner_row[...] * MOST + position, places)
    placing = (lax.broadcasted_iota(jnp.int32, (places, capacity), 0) == slotted).astype(F32).astype(BF16)
    for c in range(3):
        o_ref[:, c * BLOCK : (c + 1) * BLOCK] = mm(placing, t_ref[c]).astype(BF16)
    lane = lax.broadcasted_iota(jnp.int32, (capacity, BLOCK), 1)
    high = block_col[...] // 128
    low = block_col[...] - high * 128
    label = jnp.where(lane == 0, high, jnp.where(lane == 1, low, jnp.where(lane == 2, 1, 0)))
    o_ref[:, 3 * BLOCK :] = mm(placing, label.astype(F32).astype(BF16)).astype(BF16)


def markers(ib_target, ib_owner, ib_block, ib_count, devices):
    capacity = ib_owner.shape[1]
    return pl.pallas_call(
        functools.partial(marker_body, capacity),
        out_shape=jax.ShapeDtypeStruct((devices * MOST, 4 * BLOCK), BF16),
        in_specs=[pl.BlockSpec(memory_space=pltpu.SMEM)] + [pl.BlockSpec(memory_space=pltpu.VMEM)] * 4,
        out_specs=pl.BlockSpec(memory_space=pltpu.VMEM),
        compiler_params=pltpu.CompilerParams(vmem_limit_bytes=VMEM),
        cost_estimate=cost(SHORT),
        name="markers",
    )(
        ib_count,
        ib_owner,
        ib_owner.reshape(capacity, 1),
        ib_block.reshape(capacity, 1),
        jnp.transpose(ib_target[0], (1, 0, 2)),
    )


def near_body(planes, comps, extra, v_ref, dx_ref, dy_ref, mx_ref, my_ref, *rest):
    p_ref, g_ref, band_ref, scale_ref = rest[extra:]
    rows, columns = v_ref.shape
    group = rows // (planes * comps)
    part = 512

    @pl.when(pl.program_id(0) == 0)
    def _():
        row = lax.broadcasted_iota(jnp.int32, (rows, planes), 0) % planes
        take = (row == lax.broadcasted_iota(jnp.int32, (rows, planes), 1)).astype(F32)
        scale_ref[...] = jnp.sum(take * my_ref[...], axis=1, keepdims=True)
        take = take.astype(BF16)
        spread = mm_nt(mm(take, dy_ref[...]).astype(BF16), take)
        one = lax.broadcasted_iota(jnp.int32, (rows, rows), 0) // planes
        other = lax.broadcasted_iota(jnp.int32, (rows, rows), 1) // planes
        band_ref[...] = jnp.where(one == other, spread, 0.0).astype(BF16)

    for j in range(columns // part):
        span = slice(j * part, (j + 1) * part)
        g_ref[:, span] = (mm_nt(v_ref[...], dx_ref[span, :]) * mx_ref[:, span]).astype(BF16)
    for j in range(columns // part):
        span = slice(j * part, (j + 1) * part)
        curv = mm_nt(g_ref[...], dx_ref[span, :]) * mx_ref[:, span]
        vel = v_ref[:, span]
        grad_y = (mm(band_ref[...], vel) * scale_ref[...]).astype(BF16)
        curv = curv + mm(band_ref[...], grad_y) * scale_ref[...]
        shape = (group, comps, planes, part)
        vel = vel.astype(F32).reshape(shape)
        grad_y = grad_y.astype(F32).reshape(shape)
        grad_x = g_ref[:, span].astype(F32).reshape(shape)
        curv = curv.reshape(shape)
        tendency = viscosity * curv - (vel[:, 0:1] * grad_x + vel[:, 1:2] * grad_y)
        p_ref[:, :, :, span] = vel + time_step * tendency


def near(lines, deriv_x, deriv_y, metric_x, metric_y, planes, comps, slab, after):
    total, columns = lines.shape
    rows = GROUP * planes * comps
    return pl.pallas_call(
        functools.partial(near_body, planes, comps, len(after)),
        out_shape=jax.ShapeDtypeStruct((slab, comps, planes, columns), F32),
        grid=(total // rows,),
        in_specs=[
            pl.BlockSpec((rows, columns), lambda i: (i, 0)),
            pl.BlockSpec(deriv_x.shape, lambda i: (0, 0), pipeline_mode=pl.Buffered(1)),
            pl.BlockSpec(deriv_y.shape, lambda i: (0, 0)),
            pl.BlockSpec((1, columns), lambda i: (0, 0)),
            pl.BlockSpec((1, planes), lambda i: (0, 0)),
        ]
        + [pl.BlockSpec(memory_space=pltpu.HBM)] * len(after),
        out_specs=pl.BlockSpec((GROUP, comps, planes, columns), lambda i: (i, 0, 0, 0)),
        scratch_shapes=[
            pltpu.VMEM((rows, columns), BF16),
            pltpu.VMEM((rows, rows), BF16),
            pltpu.VMEM((rows, 1), F32),
        ],
        compiler_params=pltpu.CompilerParams(vmem_limit_bytes=VMEM),
        cost_estimate=cost(SHORT),
        name="near",
    )(lines, deriv_x, deriv_y, metric_x, metric_y, *after)


def ready_markers(got_ref, s_ref, l_ref):
    lane = lax.broadcasted_iota(jnp.int32, (8, BLOCK), 1)
    pick = jnp.where(lane == 0, 128.0, jnp.where(lane < 3, 1.0, 0.0)).astype(BF16)
    slots = s_ref.shape[0]
    if len(got_ref.shape) == 4:
        values = got_ref[:, :, :MOST, :]
        meta = got_ref[:, :, MOST:, :BLOCK]
    else:
        values = got_ref[:, :, : 3 * BLOCK]
        meta = got_ref[:, :, 3 * BLOCK :]
    meta = meta.astype(F32).reshape(slots, BLOCK).astype(BF16)
    l_ref[...] = mm_nt(pick, meta).astype(jnp.int32)
    s_ref[:, : 3 * BLOCK] = values.astype(F32).reshape(slots, 3 * BLOCK).astype(BF16)
    s_ref[:, 3 * BLOCK :] = jnp.ones((slots, BLOCK), BF16)


def markers_spec(got, slab):
    if got.ndim == 4:
        block = (got.shape[0], got.shape[1], GROUP, got.shape[3])
        return pl.BlockSpec(block, lambda *_: (0, 0, slab // GROUP, 0)), got.shape[0] * got.shape[1] * MOST
    return pl.BlockSpec(got.shape, lambda *_: (0, 0, 0)), got.shape[0] * MOST


def settle(order_ref, taken, s_ref, l_ref, p_ref, o_ref, comps, wide, group, xblocks, first, at):
    slab = p_ref.shape[0]
    planes = p_ref.shape[2]
    lines = group * planes
    slots = s_ref.shape[0]
    label = l_ref[0:1, :]
    for g in range(slab // group):
        some = slice(g * group, (g + 1) * group)
        moved = mm(order_ref[...], taken(some).reshape(lines, comps * wide)) * time_step
        line = (g * lines + lax.broadcasted_iota(jnp.int32, (lines, slots), 0)) * xblocks + 1
        for b in range(wide // BLOCK):
            chosen = (line + (first + b) == label).astype(F32).astype(BF16)
            share = mm(chosen, s_ref[...])
            inverse = 1.0 / (1.0 + share[:, 3 * BLOCK :])
            cells = slice(at + b * BLOCK, at + (b + 1) * BLOCK)
            for c in range(comps):
                term = moved[:, c * wide + b * BLOCK : c * wide + (b + 1) * BLOCK]
                total = p_ref[some, c, :, cells].reshape(lines, BLOCK) + term + share[:, c * BLOCK : (c + 1) * BLOCK]
                o_ref[some, c, :, cells] = (total * inverse).reshape(group, planes, BLOCK)


def last_body(planes, comps, group, xblocks, start, order_ref, r_ref, got_ref, p_ref, o_ref, s_ref, l_ref):
    pairs = r_ref.shape[1]
    step = pl.program_id(0) * pl.num_programs(1) + pl.program_id(1)

    @pl.when(step == 0)
    def _():
        ready_markers(got_ref, s_ref, l_ref)

    for xg in range(pairs):
        settle(
            order_ref,
            lambda some, xg=xg: r_ref[:, xg, some, :],
            s_ref,
            l_ref,
            p_ref,
            o_ref,
            comps,
            BLOCK,
            group,
            xblocks,
            start + step * pairs + xg,
            xg * BLOCK,
        )


def last(field, returned, got, order, first, count, group):
    slab, comps, planes, columns = field.shape
    groups = returned.shape[1]
    steps = groups // 2
    spec = pl.BlockSpec((slab, comps, planes, 2 * BLOCK), lambda q, i: (0, 0, 0, (first + q) * steps + i))
    got_spec, slots = markers_spec(got, slab)
    return pl.pallas_call(
        functools.partial(last_body, planes, comps, group, columns // BLOCK, first * groups),
        out_shape=jax.ShapeDtypeStruct(field.shape, F32),
        grid=(count, steps),
        in_specs=[
            pl.BlockSpec(order.shape, lambda q, i: (0, 0)),
            pl.BlockSpec((planes, 2, slab, comps * BLOCK), lambda q, i: (0, i, q, 0)),
            got_spec,
            spec,
        ],
        out_specs=spec,
        input_output_aliases={3: 0},
        scratch_shapes=[pltpu.VMEM((slots, 4 * BLOCK), BF16), pltpu.VMEM((8, slots), jnp.int32)],
        compiler_params=pltpu.CompilerParams(vmem_limit_bytes=VMEM),
        cost_estimate=cost(SHORT),
        name="last",
    )(order, returned, got, field)


def last_apart_body(comps, group, xblocks, start, ways, me_ref, order_ref, got_ref, own_ref, *rest):
    pieces, p_ref = rest[: ways - 1], rest[ways - 1]
    o_ref, s_ref, l_ref, t_ref = rest[-4:]
    step = pl.program_id(0)

    @pl.when(step == 0)
    def _():
        ready_markers(got_ref, s_ref, l_ref)
        t_ref[...] = own_ref[:, 0]

    for k in range(1, ways):

        @pl.when(step == k)
        def _(k=k):
            t_ref[...] = pieces[k - 1][...]

    settle(
        order_ref,
        lambda some: t_ref[:, some, :],
        s_ref,
        l_ref,
        p_ref,
        o_ref,
        comps,
        BLOCK,
        group,
        xblocks,
        start + (me_ref[0] ^ step),
        0,
    )


def last_apart(field, own, pieces, got, order, me, chunk, group, after):
    slab, comps, planes, columns = field.shape
    ways = own.shape[1]
    spec = pl.BlockSpec((slab, comps, planes, BLOCK), lambda i, m: (0, 0, 0, chunk * ways + (m[0] ^ i)))
    whole = pl.BlockSpec((planes, slab, comps * BLOCK), lambda i, m: (0, 0, 0))
    got_spec, slots = markers_spec(got, slab)
    return pl.pallas_call(
        functools.partial(last_apart_body, comps, group, columns // BLOCK, chunk * ways, ways),
        out_shape=jax.ShapeDtypeStruct(field.shape, F32),
        grid_spec=pltpu.PrefetchScalarGridSpec(
            num_scalar_prefetch=1,
            grid=(ways,),
            in_specs=[
                pl.BlockSpec(order.shape, lambda i, m: (0, 0)),
                got_spec,
                pl.BlockSpec((planes, 1, slab, comps * BLOCK), lambda i, m: (0, 0, chunk, 0)),
            ]
            + [whole] * (ways - 1)
            + [spec]
            + [pl.BlockSpec(memory_space=pltpu.HBM)] * len(after),
            out_specs=spec,
            scratch_shapes=[
                pltpu.VMEM((slots, 4 * BLOCK), BF16),
                pltpu.VMEM((8, slots), jnp.int32),
                pltpu.VMEM((planes, slab, comps * BLOCK), BF16),
            ],
        ),
        input_output_aliases={4 + ways - 1: 0},
        compiler_params=pltpu.CompilerParams(vmem_limit_bytes=VMEM),
        cost_estimate=cost(LONG),
        name="last_apart",
    )(me, order, got, own, *pieces, field, *after)


def come_body(count, *refs):
    refs[count][...] = jnp.zeros_like(refs[count])


def come(pieces):
    return pl.pallas_call(
        functools.partial(come_body, len(pieces)),
        out_shape=jax.ShapeDtypeStruct((8, BLOCK), F32),
        in_specs=[pl.BlockSpec(memory_space=pltpu.HBM)] * len(pieces),
        out_specs=pl.BlockSpec(memory_space=pltpu.VMEM),
        cost_estimate=cost(LONG),
        name="come",
    )(*pieces)


def across(pieces):
    ways = lax.axis_size("col")
    return tuple(
        lax.ppermute(piece, "col", [(c, c ^ k) for c in range(ways)]) for k, piece in enumerate(pieces, 1)
    )


def along(x):
    return lax.all_to_all(x, "row", split_axis=0, concat_axis=0, tiled=True)


def exchange(x):
    return lax.all_to_all(x, AXES, split_axis=0, concat_axis=0, tiled=True)


def local(
    velocity,
    deriv_x,
    deriv_y,
    deriv_z,
    metric_x,
    metric_y,
    metric_z,
    ib_target,
    ib_owner,
    ib_block,
    ib_count,
):
    slab, planes, comps, columns = velocity.shape
    row_count, ways = lax.axis_size("row"), lax.axis_size("col")
    devices = row_count * ways
    groups = devices // planes
    group = min(32, slab)
    chunks = columns // (groups * BLOCK)
    me = lax.axis_index("col").astype(jnp.int32).reshape(1)
    lines = jnp.transpose(velocity, (0, 2, 1, 3)).reshape(slab * comps * planes, columns)
    order = jnp.asarray(pack_order(planes, comps), BF16)
    back = jnp.asarray(unpack_order(planes, group), BF16)
    metric_col = metric_z[:, None]
    marked = markers(ib_target, ib_owner, ib_block, ib_count, devices)
    apart = row_count == planes and chunks == QUARTERS and slab == QUARTERS * GROUP
    at_once = 2 if apart else chunks
    first = pack(lines, order, at_once, planes, comps, groups, slab)
    block = (devices,) + first.shape[2:]
    arrived = exchange(first.reshape(block)).reshape((row_count, ways) + first.shape[2:])
    field = near(
        lines, deriv_x, deriv_y, metric_x[None, :], metric_y[None, :], planes, comps, slab, (first,)
    )

    def terms_of(x, near_in, near_out, after):
        return depth(x, me, deriv_z, metric_col, at_once, slab, near_in, near_out, after)

    if not apart:
        got = exchange(marked.reshape(devices, MOST, 4 * BLOCK))
        terms = terms_of(arrived, False, False, (field,))
        home = exchange(terms.reshape(block)).reshape(first.shape)
        field = last(field, home, got, back, 0, chunks, group)
        return jnp.transpose(field, (0, 2, 1, 3))

    def outward(k, after, marked=None):
        return pack_apart(lines, order, me, k, planes, comps, ways, slab, after, marked)

    sent3 = outward(3, (field,))
    sent2 = outward(2, (sent3[0],), marked.reshape(planes, ways, MOST, (comps + 1) * BLOCK))
    later2, later3 = lax.optimization_barrier((sent2[1:], sent3[1:], arrived))[:2]
    come2 = across(later2)
    come3 = across(later3)
    terms = terms_of(arrived, False, True, (sent2[0],))
    home = along(terms)
    joined2 = join((sent2[0],) + come2, (terms,))
    split0 = split(home, 0, slab, (joined2,))
    back0 = across(split0)
    split1 = split(home, 1, slab, (split0[0],))
    back1 = across(split1)
    got = full2 = along(joined2)
    joined3 = join((sent3[0],) + come3, (split1[0],))
    full3 = along(joined3)
    terms = depth(full2, me, deriv_z, metric_col, 1, slab, True, False, (joined3,), 0, 2)
    terms = depth(full3, me, deriv_z, metric_col, 1, slab, True, False, (come(back0),), 1, 2, (terms,))
    home_all = exchange(terms.reshape(block)).reshape(first.shape)
    field = last_apart(field, home, back0, got, back, me, 0, group, (terms,))
    field = last_apart(field, home, back1, got, back, me, 1, group, ())
    field = last(field, home_all, got, back, 2, 2, group)
    return jnp.transpose(field, (0, 2, 1, 3))


def solution(mesh):
    in_specs = (
        P(AXES, None, None, None),
        P(),
        P(),
        P(),
        P(),
        P(),
        P(),
        P(AXES, None, None, None),
        P(AXES, None),
        P(AXES, None),
        P(AXES),
    )
    out_specs = P(AXES, None, None, None)
    return jax.shard_map(local, mesh=mesh, in_specs=in_specs, out_specs=out_specs, check_vma=False)
```

time: 399 us -> 314 us (0.79)
  waiting for transfers between devices: 193 us -> 129 us
  local copies, waits for them, and re-layouts: 36.4 us -> 2.84 us
  Pallas kernels: 132 us -> 141 us
  starting transfers between devices: 30.5 us -> 38.2 us
    all_to_all x9 -> x2, waiting for transfers between devices: 193 us -> 72.7 us  [exchange(): return lax.all_to_all(x, AXES, split_axis=0, concat_axis=0, tiled=True)]
    ppermute x0 -> x12, waiting for transfers between devices: none -> 49.3 us  [across(): lax.ppermute(piece, 'col', [(c, c ^ k) for c in range(ways)])]
    unnamed x54 -> x8, local copies, waits for them, and re-layouts: 26.6 us -> 0.01 us
    all_to_all x9 -> x2, starting transfers between devices: 30.5 us -> 9.33 us  [exchange(): return lax.all_to_all(x, AXES, split_axis=0, concat_axis=0, tiled=True)]
    ppermute x0 -> x12, starting transfers between devices: none -> 15.8 us  [across(): lax.ppermute(piece, 'col', [(c, c ^ k) for c in range(ways)])]
    all_to_all x0 -> x3, starting transfers between devices: none -> 13.1 us  [along(): return lax.all_to_all(x, 'row', split_axis=0, concat_axis=0, tiled=True)]
    pallas_call x13 -> x15, Pallas kernels: 131 us -> 139 us  [the longest x3 49.9 us: depth(): pl.pallas_call(functools.partial(depth_body, count, slab, block, len(extr...]
    all_to_all x0 -> x3, waiting for transfers between devices: none -> 7.36 us  [along(): return lax.all_to_all(x, 'row', split_axis=0, concat_axis=0, tiled=True)]
  transfers between devices with their start and end apart: 9 -> 17, of which waited for: 8 -> 8; matrix products, arithmetic and copies ran while one was open for 3% -> 1% of each run, Pallas kernels for 32% -> 41%
where the time goes in v1:
time: 314 us; the launch traced here: 312 us
  Pallas kernels  141 us (45%)
  waiting for transfers between devices  129 us (41%)
  starting transfers between devices  38.2 us (12%)
    all_to_all x2, waiting for transfers between devices, exchange(): return lax.all_to_all(x, AXES, split_axis=0, concat_axis=0, tiled=True)  72.7 us
    pallas_call x3, Pallas kernels, depth(): pl.pallas_call(functools.partial(depth_body, count, slab, block, len(extr...  49.9 us
    ppermute x12, waiting for transfers between devices, across(): lax.ppermute(piece, 'col', [(c, c ^ k) for c in range(ways)])  49.3 us
    pallas_call x1, Pallas kernels, near(): pl.pallas_call(functools.partial(near_body, planes, comps, len(after)), o...  43.8 us
    ppermute x12, starting transfers between devices, across(): lax.ppermute(piece, 'col', [(c, c ^ k) for c in range(ways)])  15.8 us
    all_to_all x3, starting transfers between devices, along(): return lax.all_to_all(x, 'row', split_axis=0, concat_axis=0, tiled=True)  13.1 us
    pallas_call x2, Pallas kernels, last_apart(): pl.pallas_call(functools.partial(last_apart_body, comps, group, columns /...  11.7 us
    pallas_call x2, Pallas kernels, pack_apart(): pl.pallas_call(functools.partial(pack_apart_body, planes, comps, wide, wa...  9.52 us
  transfers between devices with their start and end apart: 17, of which 8 were waited for; matrix products, arithmetic and copies ran while one was open for 1% of the time, Pallas kernels for 41%

profile of v1, /device:TPU:8, one launch (start us, length us, event | category | flops | bytes accessed | tf_op | source)
XLA Modules:
  0.0 312.0 jit_solution(1424449031069902131)
XLA Ops:
  0.0 5.3 %pack.1.rest_0_ = bf16[8,4,128,384]{3,2,1,0:T(8,128)(2,1)} custom-call(bf16[384,384]{1,0:T(8,128)(2,1)} %constant.8.clone.order_ref, bf16[1536,2048]{1,0:T(8,128)(2,1)} %bitcast.18), custom_call_target="tpu_custom_call" | custom-call | flops 1 | bytes 1 | tf_op jit(solution)/shard_map/pack/pallas_call | solution.py:85
  5.3 6.0 %all-to-all-start = ((bf16[32,128,384]{2,1,0:T(8,128)(2,1)}), bf16[32,128,384]{2,1,0:T(8,128)(2,1)S(1)}, u32[]{:S(2)}, u32[]{:S(2)}) async-start(bf16[32,128,384]{2,1,0:T(8,128)(2,1)} %bitcast.28), calls=%async_computation | async-start | bytes 6291456 | tf_op jit(solution)/shard_map/all_to_all | solution.py:553
  11.4 43.8 %near.1.rest_4_.rest_3_ = f32[64,3,8,2048]{3,2,1,0:T(8,128)} custom-call(bf16[1536,2048]{1,0:T(8,128)(2,1)} %bitcast.19, bf16[2048,2048]{1,0:T(8,128)(2,1)} %dx_ref.1, bf16[8,8]{1,0:T(8,128)(2,1)} %dy_ref.1, f32[1,2048]{1,0:T(1,128)} %bitcast.36, f32[1,8]{1,0:T(1,128)} %bitcast.39, bf16[8,4,128,384]{3,2,1,0:T(8,128)(2,1)} %pack.1.rest_0_), custom_call_target="tpu_custom_call" | custom-call | flops 1 | bytes 1 | tf_op jit(solution)/shard_map/near/pallas_call | solution.py:342
  55.2 4.6 %pack_apart.2 = (bf16[8,64,384]{2,1,0:T(8,128)(2,1)}, bf16[8,64,384]{2,1,0:T(8,128)(2,1)}, bf16[8,64,384]{2,1,0:T(8,128)(2,1)}, bf16[8,64,384]{2,1,0:T(8,128)(2,1)}) custom-call(s32[1]{0:T(128)} %bitcast.me_ref, bf16[384,384]{1,0:T(8,128)(2,1)} %constant.8.clone.order_ref, bf16[1536,2048]{1,0:T(8,128)(2,1)} %bitcast.20, bf16[1536,2048]{1,0:T(8,128)(2,1)} %bitcast.21, ...), custom_call_target="tpu_custom_call" | custom-call | flops 1 | bytes 1 | tf_op jit(solution)/shard_map/pack_apart/pallas_call | solution.py:129
  60.4 0.7 copy.21.block_col
  61.2 0.7 copy.20.owner_col
  61.9 2.0 markers.1
  63.9 4.9 %pack_apart.3 = (bf16[8,80,384]{2,1,0:T(8,128)(2,1)}, bf16[8,80,384]{2,1,0:T(8,128)(2,1)}, bf16[8,80,384]{2,1,0:T(8,128)(2,1)}, bf16[8,80,384]{2,1,0:T(8,128)(2,1)}) custom-call(s32[1]{0:T(128)} %bitcast.me_ref, bf16[384,384]{1,0:T(8,128)(2,1)} %constant.8.clone.order_ref, bf16[1536,2048]{1,0:T(8,128)(2,1)} %bitcast.24, bf16[1536,2048]{1,0:T(8,128)(2,1)} %bitcast.25, ...), custom_call_target="tpu_custom_call" | custom-call | flops 1 | bytes 1 | tf_op jit(solution)/shard_map/pack_apart/pallas_call | solution.py:129
  68.8 14.0 %all-to-all-done = bf16[32,128,384]{2,1,0:T(8,128)(2,1)S(1)} async-done(((bf16[32,128,384]{2,1,0:T(8,128)(2,1)}), bf16[32,128,384]{2,1,0:T(8,128)(2,1)S(1)}, u32[]{:S(2)}, u32[]{:S(2)}) %all-to-all-start) | async-done | bytes 3145760 | tf_op jit(solution)/shard_map/all_to_all | solution.py:553
  82.8 0.0 collective-permute-start.3
  82.8 1.2 collective-permute-start.4
  84.0 2.3 collective-permute-start.5
  86.3 1.4 copy.22.m_ref
  87.7 0.9 collective-permute-start
  88.6 0.6 collective-permute-start.1
  89.2 19.7 %depth.3.refs_4_ = bf16[8,4,128,384]{3,2,1,0:T(8,128)(2,1)} custom-call(s32[1]{0:T(128)} %bitcast.me_ref, bf16[8,4,128,384]{3,2,1,0:T(8,128)(2,1)} %bitcast.30, bf16[2048,2048]{1,0:T(8,128)(2,1)} %d_ref.5, f32[2048,1]{1,0:T(8,128)} %copy.22.m_ref, bf16[8,80,384]{2,1,0:T(8,128)(2,1)} %get-tuple-element.35.rest_0_.refs_0_), custom_call_target="tpu_custom_call" | custom-call | flops 1 | bytes 1 | tf_op jit(solution)/shard_map/depth/pallas_call | solution.py:244
  108.9 4.5 %all-to-all-start.1 = ((bf16[8,4,128,384]{3,2,1,0:T(8,128)(2,1)}), bf16[8,4,128,384]{3,2,1,0:T(8,128)(2,1)}, u32[]{:S(2)}, u32[]{:S(2)}) async-start(bf16[8,4,128,384]{3,2,1,0:T(8,128)(2,1)} %depth.3.refs_4_), calls=%async_computation.1 | async-start | bytes 6291456 | tf_op jit(solution)/shard_map/all_to_all | solution.py:549
  113.4 2.1 collective-permute-start.2
  115.4 0.9 collective-permute-done.4.refs_2_
  116.3 30.9 %collective-permute-done.5.refs_3_ = bf16[8,80,384]{2,1,0:T(8,128)(2,1)} collective-permute-done((bf16[8,80,384]{2,1,0:T(8,128)(2,1)}, bf16[8,80,384]{2,1,0:T(8,128)(2,1)}, u32[]{:S(2)}, u32[]{:S(2)}) %collective-permute-start.5) | collective-permute-done | bytes 491552 | tf_op jit(solution)/shard_map/ppermute | solution.py:544
  147.2 2.8 join.2.rest_0_
  150.0 1.2 all-to-all-done.1.x_ref.own_ref
  151.2 4.3 %all-to-all-start.3 = ((bf16[8,4,80,384]{3,2,1,0:T(8,128)(2,1)}), bf16[8,4,80,384]{3,2,1,0:T(8,128)(2,1)}, u32[]{:S(2)}, u32[]{:S(2)}) async-start(bf16[8,4,80,384]{3,2,1,0:T(8,128)(2,1)} %join.2.rest_0_), calls=%async_computation.3 | async-start | bytes 3932160 | tf_op jit(solution)/shard_map/all_to_all | solution.py:549
  155.6 2.3 split.2
  157.9 2.4 collective-permute-start.7
  160.3 1.1 collective-permute-start.6
  161.4 2.3 split.3
  163.7 0.0 collective-permute-done.refs_1_
  163.7 0.0 collective-permute-start.8
  163.7 0.0 collective-permute-done.1.refs_2_
  163.7 3.2 %collective-permute-start.10 = (bf16[8,64,384]{2,1,0:T(8,128)(2,1)}, bf16[8,64,384]{2,1,0:T(8,128)(2,1)}, u32[]{:S(2)}, u32[]{:S(2)}) collective-permute-start(bf16[8,64,384]{2,1,0:T(8,128)(2,1)} %get-tuple-element.43), channel_id=1, source_target_pairs={{0,2},{1,3},{2,0},{3,1},{4,6},{5,7},{6,4},{7,5},{8,10},{9,11},{10,... | collective-permute-start | bytes 1179656 | tf_op jit(solution)/shard_map/ppermute | solution.py:544
  166.9 5.3 %collective-permute-done.2.refs_3_ = bf16[8,64,384]{2,1,0:T(8,128)(2,1)} collective-permute-done((bf16[8,64,384]{2,1,0:T(8,128)(2,1)}, bf16[8,64,384]{2,1,0:T(8,128)(2,1)}, u32[]{:S(2)}, u32[]{:S(2)}) %collective-permute-start.2) | collective-permute-done | bytes 393248 | tf_op jit(solution)/shard_map/ppermute | solution.py:544
  172.3 0.0 collective-permute-start.9
  172.3 2.5 join.3.rest_0_
  174.7 6.1 %all-to-all-done.3.x_ref.got_ref = bf16[8,4,80,384]{3,2,1,0:T(8,128)(2,1)} async-done(((bf16[8,4,80,384]{3,2,1,0:T(8,128)(2,1)}), bf16[8,4,80,384]{3,2,1,0:T(8,128)(2,1)}, u32[]{:S(2)}, u32[]{:S(2)}) %all-to-all-start.3) | async-done | bytes 1966112 | tf_op jit(solution)/shard_map/all_to_all | solution.py:549
  180.8 4.3 %all-to-all-start.2 = ((bf16[8,4,64,384]{3,2,1,0:T(8,128)(2,1)}), bf16[8,4,64,384]{3,2,1,0:T(8,128)(2,1)}, u32[]{:S(2)}, u32[]{:S(2)}) async-start(bf16[8,4,64,384]{3,2,1,0:T(8,128)(2,1)} %join.3.rest_0_), calls=%async_computation.2 | async-start | bytes 3145728 | tf_op jit(solution)/shard_map/all_to_all | solution.py:549
  185.1 15.1 %depth.4.rest_0_ = bf16[8,4,128,384]{3,2,1,0:T(8,128)(2,1)} custom-call(s32[1]{0:T(128)} %bitcast.me_ref, bf16[8,4,80,384]{3,2,1,0:T(8,128)(2,1)} %all-to-all-done.3.x_ref.got_ref, bf16[2048,2048]{1,0:T(8,128)(2,1)} %d_ref.5, f32[2048,1]{1,0:T(8,128)} %copy.22.m_ref, bf16[8,4,64,384]{3,2,1,0:T(8,128)(2,1)} %join.3.rest_0_), custom_call_target="tpu_custom_call" | custom-call | flops 1 | bytes 1 | tf_op jit(solution)/shard_map/depth/pallas_call | solution.py:244
  200.2 0.0 collective-permute-done.7.refs_1_.rest_1_
  200.2 2.0 collective-permute-start.11
  202.2 12.2 %collective-permute-done.8.refs_2_.rest_2_ = bf16[8,64,384]{2,1,0:T(8,128)(2,1)} collective-permute-done((bf16[8,64,384]{2,1,0:T(8,128)(2,1)}, bf16[8,64,384]{2,1,0:T(8,128)(2,1)}, u32[]{:S(2)}, u32[]{:S(2)}) %collective-permute-start.8) | collective-permute-done | bytes 393248 | tf_op jit(solution)/shard_map/ppermute | solution.py:544
  214.4 0.0 collective-permute-done.6.refs_0_.rest_0_
  214.4 0.6 come.1.rest_1_
  215.0 15.0 %depth.5.rest_4_ = bf16[8,4,128,384]{3,2,1,0:T(8,128)(2,1)} custom-call(s32[1]{0:T(128)} %bitcast.me_ref, bf16[8,4,64,384]{3,2,1,0:T(8,128)(2,1)} %all-to-all-done.2.x_ref, bf16[2048,2048]{1,0:T(8,128)(2,1)} %d_ref.5, f32[2048,1]{1,0:T(8,128)} %copy.22.m_ref, bf16[8,4,128,384]{3,2,1,0:T(8,128)(2,1)} %depth.4.rest_0_, ...), custom_call_target="tpu_custom_call", output_to_operand_aliasing={{}: (4, {})} | custom-call | flops 1 | bytes 1 | tf_op jit(solution)/shard_map/depth/pallas_call | solution.py:244
  230.1 3.3 %all-to-all-start.4 = ((bf16[32,128,384]{2,1,0:T(8,128)(2,1)}), bf16[32,128,384]{2,1,0:T(8,128)(2,1)}, u32[]{:S(2)}, u32[]{:S(2)}) async-start(bf16[32,128,384]{2,1,0:T(8,128)(2,1)} %bitcast.29), calls=%async_computation.4 | async-start | bytes 6291456 | tf_op jit(solution)/shard_map/all_to_all | solution.py:553
  233.4 5.9 %last_apart.2.rest_3_ = f32[64,3,8,2048]{3,2,1,0:T(8,128)} custom-call(s32[1]{0:T(128)} %bitcast.me_ref, bf16[256,256]{1,0:T(8,128)(2,1)} %constant.9.clone.order_ref, bf16[8,4,80,384]{3,2,1,0:T(8,128)(2,1)} %all-to-all-done.3.x_ref.got_ref, bf16[8,4,128,384]{3,2,1,0:T(8,128)(2,1)} %all-to-all-done.1.x_ref.own_ref, ...), custom_call_target="tpu_custom_call", output_to_operand_aliasing={{}: (7, {})} | custom-call | flops 999999995904 | bytes 1 | tf_op jit(solution)/shard_map/last_apart/pallas_call | solution.py:498
  239.2 5.9 %last_apart.3.p_ref = f32[64,3,8,2048]{3,2,1,0:T(8,128)} custom-call(s32[1]{0:T(128)} %bitcast.me_ref, bf16[256,256]{1,0:T(8,128)(2,1)} %constant.9.clone.order_ref, bf16[8,4,80,384]{3,2,1,0:T(8,128)(2,1)} %all-to-all-done.3.x_ref.got_ref, bf16[8,4,128,384]{3,2,1,0:T(8,128)(2,1)} %all-to-all-done.1.x_ref.own_ref, ...), custom_call_target="tpu_custom_call", output_to_operand_aliasing={{}: (7, {})} | custom-call | flops 999999995904 | bytes 1 | tf_op jit(solution)/shard_map/last_apart/pallas_call | solution.py:498
  245.1 58.7 %all-to-all-done.4 = bf16[32,128,384]{2,1,0:T(8,128)(2,1)} async-done(((bf16[32,128,384]{2,1,0:T(8,128)(2,1)}), bf16[32,128,384]{2,1,0:T(8,128)(2,1)}, u32[]{:S(2)}, u32[]{:S(2)}) %all-to-all-start.4) | async-done | bytes 3145760 | tf_op jit(solution)/shard_map/all_to_all | solution.py:553
  303.8 8.2 %last.1 = f32[64,3,8,2048]{3,2,1,0:T(8,128)} custom-call(bf16[256,256]{1,0:T(8,128)(2,1)} %constant.9.clone.order_ref, bf16[8,4,128,384]{3,2,1,0:T(8,128)(2,1)} %bitcast.15.r_ref, bf16[8,4,80,384]{3,2,1,0:T(8,128)(2,1)} %all-to-all-done.3.x_ref.got_ref, f32[64,3,8,2048]{3,2,1,0:T(8,128)} %last_apart.3.p_ref), custom_call_target="tpu_custom_call", output_to_operand_aliasing={{}: (3, {})} | custom-call | flops 1 | bytes 1 | tf_op jit(solution)/shard_map/last/pallas_call | solution.py:441
  (13 shorter events, 0.0 us)
Async XLA Ops:
  5.3 77.5 %all-to-all-start = ((bf16[32,128,384]{2,1,0:T(8,128)(2,1)}), bf16[32,128,384]{2,1,0:T(8,128)(2,1)S(1)}, u32[]{:S(2)}, u32[]{:S(2)}) async-start(bf16[32,128,384]{2,1,0:T(8,128)(2,1)} %bitcast.28), calls=%async_computation | async-start | bytes 6291456 | tf_op jit(solution)/shard_map/all_to_all | solution.py:553
  55.2 5.3 %copy-start.3 = (s32[1,128]{1,0:T(1,128)S(1)}, s32[1,128]{1,0:T(1,128)}, u32[]{:S(2)}) copy-start(s32[1,128]{1,0:T(1,128)} %param.22) | copy-start | bytes 1540
  55.2 6.0 %copy-start.2 = (s32[1,128]{1,0:T(1,128)S(1)}, s32[1,128]{1,0:T(1,128)}, u32[]{:S(2)}) copy-start(s32[1,128]{1,0:T(1,128)} %owner_row.1) | copy-start | bytes 1540
  63.9 22.4 %copy-start.1 = (f32[2048]{0:T(1024)S(1)}, f32[2048]{0:T(1024)}, u32[]{:S(2)}) copy-start(f32[2048]{0:T(1024)} %param.19) | copy-start | bytes 24580
  82.8 6.3 %copy-start = (bf16[32,128,384]{2,1,0:T(8,128)(2,1)}, bf16[32,128,384]{2,1,0:T(8,128)(2,1)S(1)}, u32[]{:S(2)}) copy-start(bf16[32,128,384]{2,1,0:T(8,128)(2,1)S(1)} %all-to-all-done) | copy-start | bytes 9437188
  82.8 30.5 %collective-permute-start.3 = (bf16[8,80,384]{2,1,0:T(8,128)(2,1)}, bf16[8,80,384]{2,1,0:T(8,128)(2,1)}, u32[]{:S(2)}, u32[]{:S(2)}) collective-permute-start(bf16[8,80,384]{2,1,0:T(8,128)(2,1)} %get-tuple-element.36), channel_id=1, source_target_pairs={{0,1},{1,0},{2,3},{3,2},{4,5},{5,4},{6,7},{7,6},{8,9},{9,8},{10,11... | collective-permute-start | bytes 1474568 | tf_op jit(solution)/shard_map/ppermute | solution.py:544
  82.8 33.5 %collective-permute-start.4 = (bf16[8,80,384]{2,1,0:T(8,128)(2,1)}, bf16[8,80,384]{2,1,0:T(8,128)(2,1)}, u32[]{:S(2)}, u32[]{:S(2)}) collective-permute-start(bf16[8,80,384]{2,1,0:T(8,128)(2,1)} %get-tuple-element.37), channel_id=1, source_target_pairs={{0,2},{1,3},{2,0},{3,1},{4,6},{5,7},{6,4},{7,5},{8,10},{9,11},{10,... | collective-permute-start | bytes 1474568 | tf_op jit(solution)/shard_map/ppermute | solution.py:544
  84.0 63.2 %collective-permute-start.5 = (bf16[8,80,384]{2,1,0:T(8,128)(2,1)}, bf16[8,80,384]{2,1,0:T(8,128)(2,1)}, u32[]{:S(2)}, u32[]{:S(2)}) collective-permute-start(bf16[8,80,384]{2,1,0:T(8,128)(2,1)} %get-tuple-element.38), channel_id=1, source_target_pairs={{0,3},{1,2},{2,1},{3,0},{4,7},{5,6},{6,5},{7,4},{8,11},{9,10},{10,... | collective-permute-start | bytes 1474568 | tf_op jit(solution)/shard_map/ppermute | solution.py:544
  87.7 76.0 %collective-permute-start = (bf16[8,64,384]{2,1,0:T(8,128)(2,1)}, bf16[8,64,384]{2,1,0:T(8,128)(2,1)}, u32[]{:S(2)}, u32[]{:S(2)}) collective-permute-start(bf16[8,64,384]{2,1,0:T(8,128)(2,1)} %get-tuple-element.32), channel_id=1, source_target_pairs={{0,1},{1,0},{2,3},{3,2},{4,5},{5,4},{6,7},{7,6},{8,9},{9,8},{10,11... | collective-permute-start | bytes 1179656 | tf_op jit(solution)/shard_map/ppermute | solution.py:544
  88.6 75.1 %collective-permute-start.1 = (bf16[8,64,384]{2,1,0:T(8,128)(2,1)}, bf16[8,64,384]{2,1,0:T(8,128)(2,1)}, u32[]{:S(2)}, u32[]{:S(2)}) collective-permute-start(bf16[8,64,384]{2,1,0:T(8,128)(2,1)} %get-tuple-element.33), channel_id=1, source_target_pairs={{0,2},{1,3},{2,0},{3,1},{4,6},{5,7},{6,4},{7,5},{8,10},{9,11},{10,... | collective-permute-start | bytes 1179656 | tf_op jit(solution)/shard_map/ppermute | solution.py:544
  108.9 42.4 %all-to-all-start.1 = ((bf16[8,4,128,384]{3,2,1,0:T(8,128)(2,1)}), bf16[8,4,128,384]{3,2,1,0:T(8,128)(2,1)}, u32[]{:S(2)}, u32[]{:S(2)}) async-start(bf16[8,4,128,384]{3,2,1,0:T(8,128)(2,1)} %depth.3.refs_4_), calls=%async_computation.1 | async-start | bytes 6291456 | tf_op jit(solution)/shard_map/all_to_all | solution.py:549
  113.4 58.9 %collective-permute-start.2 = (bf16[8,64,384]{2,1,0:T(8,128)(2,1)}, bf16[8,64,384]{2,1,0:T(8,128)(2,1)}, u32[]{:S(2)}, u32[]{:S(2)}) collective-permute-start(bf16[8,64,384]{2,1,0:T(8,128)(2,1)} %get-tuple-element.34), channel_id=1, source_target_pairs={{0,3},{1,2},{2,1},{3,0},{4,7},{5,6},{6,5},{7,4},{8,11},{9,10},{10,... | collective-permute-start | bytes 1179656 | tf_op jit(solution)/shard_map/ppermute | solution.py:544
  151.2 29.6 %all-to-all-start.3 = ((bf16[8,4,80,384]{3,2,1,0:T(8,128)(2,1)}), bf16[8,4,80,384]{3,2,1,0:T(8,128)(2,1)}, u32[]{:S(2)}, u32[]{:S(2)}) async-start(bf16[8,4,80,384]{3,2,1,0:T(8,128)(2,1)} %join.2.rest_0_), calls=%async_computation.3 | async-start | bytes 3932160 | tf_op jit(solution)/shard_map/all_to_all | solution.py:549
  157.9 42.3 %collective-permute-start.7 = (bf16[8,64,384]{2,1,0:T(8,128)(2,1)}, bf16[8,64,384]{2,1,0:T(8,128)(2,1)}, u32[]{:S(2)}, u32[]{:S(2)}) collective-permute-start(bf16[8,64,384]{2,1,0:T(8,128)(2,1)} %get-tuple-element.41), channel_id=1, source_target_pairs={{0,2},{1,3},{2,0},{3,1},{4,6},{5,7},{6,4},{7,5},{8,10},{9,11},{10,... | collective-permute-start | bytes 1179656 | tf_op jit(solution)/shard_map/ppermute | solution.py:544
  160.3 54.2 %collective-permute-start.6 = (bf16[8,64,384]{2,1,0:T(8,128)(2,1)}, bf16[8,64,384]{2,1,0:T(8,128)(2,1)}, u32[]{:S(2)}, u32[]{:S(2)}) collective-permute-start(bf16[8,64,384]{2,1,0:T(8,128)(2,1)} %get-tuple-element.39.rest_0_), channel_id=1, source_target_pairs={{0,1},{1,0},{2,3},{3,2},{4,5},{5,4},{6,7},{7,6},{8,9},{9,8},{10,11... | collective-permute-start | bytes 1179656 | tf_op jit(solution)/shard_map/ppermute | solution.py:544
  163.7 50.8 %collective-permute-start.8 = (bf16[8,64,384]{2,1,0:T(8,128)(2,1)}, bf16[8,64,384]{2,1,0:T(8,128)(2,1)}, u32[]{:S(2)}, u32[]{:S(2)}) collective-permute-start(bf16[8,64,384]{2,1,0:T(8,128)(2,1)} %get-tuple-element.42), channel_id=1, source_target_pairs={{0,3},{1,2},{2,1},{3,0},{4,7},{5,6},{6,5},{7,4},{8,11},{9,10},{10,... | collective-permute-start | bytes 1179656 | tf_op jit(solution)/shard_map/ppermute | solution.py:544
  163.7 75.5 %collective-permute-start.10 = (bf16[8,64,384]{2,1,0:T(8,128)(2,1)}, bf16[8,64,384]{2,1,0:T(8,128)(2,1)}, u32[]{:S(2)}, u32[]{:S(2)}) collective-permute-start(bf16[8,64,384]{2,1,0:T(8,128)(2,1)} %get-tuple-element.43), channel_id=1, source_target_pairs={{0,2},{1,3},{2,0},{3,1},{4,6},{5,7},{6,4},{7,5},{8,10},{9,11},{10,... | collective-permute-start | bytes 1179656 | tf_op jit(solution)/shard_map/ppermute | solution.py:544
  172.3 67.0 %collective-permute-start.9 = (bf16[8,64,384]{2,1,0:T(8,128)(2,1)}, bf16[8,64,384]{2,1,0:T(8,128)(2,1)}, u32[]{:S(2)}, u32[]{:S(2)}) collective-permute-start(bf16[8,64,384]{2,1,0:T(8,128)(2,1)} %get-tuple-element.40.refs_4_), channel_id=1, source_target_pairs={{0,1},{1,0},{2,3},{3,2},{4,5},{5,4},{6,7},{7,6},{8,9},{9,8},{10,11... | collective-permute-start | bytes 1179656 | tf_op jit(solution)/shard_map/ppermute | solution.py:544
  180.8 34.2 %all-to-all-start.2 = ((bf16[8,4,64,384]{3,2,1,0:T(8,128)(2,1)}), bf16[8,4,64,384]{3,2,1,0:T(8,128)(2,1)}, u32[]{:S(2)}, u32[]{:S(2)}) async-start(bf16[8,4,64,384]{3,2,1,0:T(8,128)(2,1)} %join.3.rest_0_), calls=%async_computation.2 | async-start | bytes 3145728 | tf_op jit(solution)/shard_map/all_to_all | solution.py:549
  200.2 39.0 %collective-permute-start.11 = (bf16[8,64,384]{2,1,0:T(8,128)(2,1)}, bf16[8,64,384]{2,1,0:T(8,128)(2,1)}, u32[]{:S(2)}, u32[]{:S(2)}) collective-permute-start(bf16[8,64,384]{2,1,0:T(8,128)(2,1)} %get-tuple-element.44), channel_id=1, source_target_pairs={{0,3},{1,2},{2,1},{3,0},{4,7},{5,6},{6,5},{7,4},{8,11},{9,10},{10,... | collective-permute-start | bytes 1179656 | tf_op jit(solution)/shard_map/ppermute | solution.py:544
  230.1 73.7 %all-to-all-start.4 = ((bf16[32,128,384]{2,1,0:T(8,128)(2,1)}), bf16[32,128,384]{2,1,0:T(8,128)(2,1)}, u32[]{:S(2)}, u32[]{:S(2)}) async-start(bf16[32,128,384]{2,1,0:T(8,128)(2,1)} %bitcast.29), calls=%async_computation.4 | async-start | bytes 6291456 | tf_op jit(solution)/shard_map/all_to_all | solution.py:553

commit v2 on v1

--- a/solution.py
+++ b/solution.py
@@ -13,7 +13,10 @@
 GROUP = 16
 QUARTERS = 4
 VMEM = 60 << 20
+ROOM = 60 << 20
 SHORT = 1
+EARLY = 2
+PACK = 4
 LONG = 10**12
 
 viscosity = 0.4
@@ -80,8 +83,9 @@
 
 
 def pack(lines, order, count, planes, comps, groups, slab):
-    step = 2 * BLOCK
-    steps = groups // 2
+    many = PACK
+    step = many * BLOCK
+    steps = groups // many
     return pl.pallas_call(
         functools.partial(pack_body, planes, comps, BLOCK),
         out_shape=jax.ShapeDtypeStruct((planes, groups, count * slab, comps * BLOCK), BF16),
@@ -90,61 +94,57 @@
             pl.BlockSpec(order.shape, lambda q, i: (0, 0)),
             pl.BlockSpec((lines.shape[0], step), lambda q, i: (0, q * steps + i)),
         ],
-        out_specs=pl.BlockSpec((planes, 2, slab, comps * BLOCK), lambda q, i: (0, i, q, 0)),
+        out_specs=pl.BlockSpec((planes, many, slab, comps * BLOCK), lambda q, i: (0, i, q, 0)),
         compiler_params=pltpu.CompilerParams(vmem_limit_bytes=VMEM),
         cost_estimate=cost(SHORT),
         name="pack",
     )(order, lines)
 
 
-def pack_apart_body(planes, comps, wide, ways, count, steps, me_ref, order_ref, *rest):
-    v_refs, o_refs = rest[:ways], rest[ways + count :]
-    step = pl.program_id(0)
-
-    @pl.when(step < steps)
-    def _():
-        whole = jnp.concatenate([v_ref[...] for v_ref in v_refs], axis=1)
+def pack_apart_body(planes, comps, ways, given, extra, me_ref, order_ref, *rest):
+    v_refs, o_refs = rest[:ways], rest[ways + given + extra :]
+    rows = order_ref.shape[0]
+    groups = v_refs[0].shape[0] // rows
+    slab = groups * GROUP
+    for g in range(groups):
+        whole = jnp.concatenate([v_ref[g * rows : (g + 1) * rows, :] for v_ref in v_refs], axis=1)
         moved = mm(order_ref[...], whole).astype(BF16)
+        spot = slice(g * GROUP, (g + 1) * GROUP)
         for k in range(ways):
-            place_rows(o_refs[k], moved, planes, comps, wide, slice(None), slice(k * wide, (k + 1) * wide))
-
-    if count >= ways:
-        m_refs = rest[ways : 2 * ways]
-
-        @pl.when(step == steps)
-        def _():
-            for k in range(ways):
-                o_refs[k][:, :MOST, :] = m_refs[k][:, 0, :, : comps * BLOCK]
-                o_refs[k][:, MOST:, :BLOCK] = m_refs[k][:, 0, :, comps * BLOCK :]
-                o_refs[k][:, MOST:, BLOCK:] = jnp.zeros((planes, MOST, (comps - 1) * BLOCK), BF16)
+            cells = slice(k * BLOCK, (k + 1) * BLOCK)
+            if not given:
+                place_rows(o_refs[k], moved, planes, comps, BLOCK, spot, cells)
+                continue
+            for y in range(planes):
+                for c in range(comps):
+                    at = (y * comps + c) * GROUP
+                    to = c * slab + g * GROUP
+                    o_refs[k][y, to : to + GROUP, :] = moved[at : at + GROUP, cells]
+    if given:
+        for k in range(ways):
+            at = comps * slab
+            for c in range(comps):
+                o_refs[k][:, at + c * MOST : at + (c + 1) * MOST, :] = rest[ways][
+                    k, :, :, c * BLOCK : (c + 1) * BLOCK
+                ]
+            o_refs[k][:, at + comps * MOST :, :] = rest[ways + 1][k]
 
 
 def pack_apart(lines, order, me, chunk, planes, comps, ways, slab, after, marked=None):
     total = lines.shape[0]
-    wide = BLOCK
-    rows = order.shape[0]
-    steps = total // rows
-    more = 0 if marked is None else 1
-    given = () if marked is None else (marked,) * ways
-    return pl.pallas_call(
-        functools.partial(pack_apart_body, planes, comps, wide, ways, len(given) + len(after), steps),
-        out_shape=(jax.ShapeDtypeStruct((planes, slab + more * GROUP, comps * wide), BF16),) * ways,
+    given = () if marked is None else marked
+    shape = (planes, comps * slab + (comps + 1) * MOST, BLOCK) if given else (planes, slab, comps * BLOCK)
+    return pl.pallas_call(
+        functools.partial(pack_apart_body, planes, comps, ways, len(given), len(after)),
+        out_shape=(jax.ShapeDtypeStruct(shape, BF16),) * ways,
         grid_spec=pltpu.PrefetchScalarGridSpec(
             num_scalar_prefetch=1,
-            grid=(steps + more,),
+            grid=(1,),
             in_specs=[pl.BlockSpec(order.shape, lambda i, m: (0, 0))]
-            + [
-                pl.BlockSpec(
-                    (rows, wide), lambda i, m, k=k: (jnp.minimum(i, steps - 1), chunk * ways + (m[0] ^ k))
-                )
-                for k in range(ways)
-            ]
-            + [
-                pl.BlockSpec((planes, 1, MOST, (comps + 1) * BLOCK), lambda i, m, k=k: (0, m[0] ^ k, 0, 0))
-                for k in range(ways if more else 0)
-            ]
+            + [pl.BlockSpec((total, BLOCK), lambda i, m, k=k: (0, chunk * ways + (m[0] ^ k))) for k in range(ways)]
+            + [pl.BlockSpec(x.shape, lambda i, m: (0, 0, 0, 0)) for x in given]
             + [pl.BlockSpec(memory_space=pltpu.HBM)] * len(after),
-            out_specs=(pl.BlockSpec((planes, GROUP, comps * wide), lambda i, m: (0, i, 0)),) * ways,
+            out_specs=(pl.BlockSpec(shape, lambda i, m: (0, 0, 0)),) * ways,
         ),
         compiler_params=pltpu.CompilerParams(vmem_limit_bytes=VMEM),
         cost_estimate=cost(SHORT),
@@ -153,9 +153,8 @@
 
 
 def join_body(ways, *refs):
-    o_ref = refs[-1]
     for k in range(ways):
-        o_ref[:, k] = refs[k][...]
+        refs[-1][:, k] = refs[k][...]
 
 
 def join(pieces, after):
@@ -198,7 +197,9 @@
 
 def depth_body(count, slab, block, extra, near_in, near_out, me_ref, x_ref, d_ref, m_ref, *rest):
     o_ref, s_ref, g_ref = rest[extra:]
-    tall, ways, _, cols = x_ref.shape
+    tall, ways, height, cols = x_ref.shape
+    stacked = cols == BLOCK
+    cols = 3 * BLOCK
     wide = cols // 3
     phase = pl.program_id(0)
     step = pl.program_id(1)
@@ -210,8 +211,12 @@
         for r in range(tall):
             for k in range(ways):
                 to = pl.multiple_of((r * ways + (me ^ k if near_in else k)) * slab, slab)
-                for q in range(count):
-                    s_ref[pl.ds(to, slab), q * cols : (q + 1) * cols] = x_ref[r, k, q * slab : (q + 1) * slab]
+                for q in range(1 if stacked else count):
+                    s_ref[pl.ds(to, slab), q * cols : (q + 1) * cols] = (
+                        jnp.concatenate([x_ref[r, k, c * slab : (c + 1) * slab] for c in range(3)], axis=1)
+                        if stacked
+                        else x_ref[r, k, q * slab : (q + 1) * slab]
+                    )
 
     @pl.when(phase == 0)
     def _():
@@ -237,6 +242,8 @@
 
 def depth(x, me, deriv_z, metric_z, count, slab, near_in, near_out, after, place=0, total=None, held=()):
     tall, ways, _, cols = x.shape
+    given = (tall, ways, count * slab if cols > BLOCK else 3 * slab, cols)
+    cols = 3 * BLOCK
     shape = (tall, ways, count * slab, cols)
     extra = tuple(held) + tuple(after)
     height = deriv_z.shape[0]
@@ -248,7 +255,7 @@
             num_scalar_prefetch=1,
             grid=(2, height // block),
             in_specs=[
-                pl.BlockSpec(shape, lambda p, i, m: (0, 0, 0, 0)),
+                pl.BlockSpec(given, lambda p, i, m: (0, 0, 0, 0)),
                 pl.BlockSpec((block, height), lambda p, i, m: (i, 0)),
                 pl.BlockSpec((height, 1), lambda p, i, m: (0, 0)),
             ]
@@ -263,15 +270,17 @@
     )(me, x, deriv_z, metric_z, *extra)
 
 
-def marker_body(capacity, count_ref, owner_row, owner_col, block_col, t_ref, o_ref):
-    count = count_ref[0]
+def marker_body(capacity, ways, apart, count_ref, me_ref, owner_row, owner_col, block_col, t_ref, o_ref, *l_refs):
     earlier = lax.broadcasted_iota(jnp.int32, (capacity, capacity), 0)
     later = lax.broadcasted_iota(jnp.int32, (capacity, capacity), 1)
     same = (owner_col[...] == owner_row[...]) & (earlier < later)
     position = jnp.sum(same.astype(jnp.int32), axis=0, keepdims=True)
     slot = lax.broadcasted_iota(jnp.int32, (1, capacity), 1)
+    owner = owner_row[...]
     places = o_ref.shape[0]
-    slotted = jnp.where(slot < count, owner_row[...] * MOST + position, places)
+    if apart:
+        owner = ((owner % ways) ^ me_ref[0]) * (places // (ways * MOST)) + owner // ways
+    slotted = jnp.where(slot < count_ref[0], owner * MOST + position, places)
     placing = (lax.broadcasted_iota(jnp.int32, (places, capacity), 0) == slotted).astype(F32).astype(BF16)
     for c in range(3):
         o_ref[:, c * BLOCK : (c + 1) * BLOCK] = mm(placing, t_ref[c]).astype(BF16)
@@ -279,21 +288,32 @@
     high = block_col[...] // 128
     low = block_col[...] - high * 128
     label = jnp.where(lane == 0, high, jnp.where(lane == 1, low, jnp.where(lane == 2, 1, 0)))
-    o_ref[:, 3 * BLOCK :] = mm(placing, label.astype(F32).astype(BF16)).astype(BF16)
-
-
-def markers(ib_target, ib_owner, ib_block, ib_count, devices):
+    label = mm(placing, label.astype(F32).astype(BF16)).astype(BF16)
+    if apart:
+        l_refs[0][...] = label
+    else:
+        o_ref[:, 3 * BLOCK :] = label
+
+
+def markers(ib_target, ib_owner, ib_block, ib_count, me, devices, ways, apart):
     capacity = ib_owner.shape[1]
-    return pl.pallas_call(
-        functools.partial(marker_body, capacity),
-        out_shape=jax.ShapeDtypeStruct((devices * MOST, 4 * BLOCK), BF16),
-        in_specs=[pl.BlockSpec(memory_space=pltpu.SMEM)] + [pl.BlockSpec(memory_space=pltpu.VMEM)] * 4,
-        out_specs=pl.BlockSpec(memory_space=pltpu.VMEM),
+    places = devices * MOST
+    if apart:
+        shapes = (jax.ShapeDtypeStruct((places, 3 * BLOCK), BF16),)
+        shapes += (jax.ShapeDtypeStruct((places, BLOCK), BF16),)
+    else:
+        shapes = (jax.ShapeDtypeStruct((places, 4 * BLOCK), BF16),)
+    return pl.pallas_call(
+        functools.partial(marker_body, capacity, ways, apart),
+        out_shape=shapes,
+        in_specs=[pl.BlockSpec(memory_space=pltpu.SMEM)] * 2 + [pl.BlockSpec(memory_space=pltpu.VMEM)] * 4,
+        out_specs=(pl.BlockSpec(memory_space=pltpu.VMEM),) * len(shapes),
         compiler_params=pltpu.CompilerParams(vmem_limit_bytes=VMEM),
         cost_estimate=cost(SHORT),
         name="markers",
     )(
         ib_count,
+        me,
         ib_owner,
         ib_owner.reshape(capacity, 1),
         ib_block.reshape(capacity, 1),
@@ -301,8 +321,8 @@
     )
 
 
-def near_body(planes, comps, extra, v_ref, dx_ref, dy_ref, mx_ref, my_ref, *rest):
-    p_ref, g_ref, band_ref, scale_ref = rest[extra:]
+def near_body(planes, comps, extra, near_columns, v_ref, dx_ref, dy_ref, mx_ref, my_ref, *rest):
+    p_refs, (g_ref, band_ref, scale_ref) = rest[extra:-3], rest[-3:]
     rows, columns = v_ref.shape
     group = rows // (planes * comps)
     part = 512
@@ -333,15 +353,21 @@
         grad_x = g_ref[:, span].astype(F32).reshape(shape)
         curv = curv.reshape(shape)
         tendency = viscosity * curv - (vel[:, 0:1] * grad_x + vel[:, 1:2] * grad_y)
-        p_ref[:, :, :, span] = vel + time_step * tendency
-
-
-def near(lines, deriv_x, deriv_y, metric_x, metric_y, planes, comps, slab, after):
+        at = j * part
+        if at < near_columns:
+            p_refs[0][:, :, :, span] = vel + time_step * tendency
+        else:
+            p_refs[-1][:, :, :, at - near_columns : at - near_columns + part] = vel + time_step * tendency
+
+
+def near(lines, deriv_x, deriv_y, metric_x, metric_y, planes, comps, slab, near_columns, after):
     total, columns = lines.shape
     rows = GROUP * planes * comps
-    return pl.pallas_call(
-        functools.partial(near_body, planes, comps, len(after)),
-        out_shape=jax.ShapeDtypeStruct((slab, comps, planes, columns), F32),
+    far = columns - near_columns
+    shapes = ((columns, near_columns), (far, far)) if near_columns else ((far, far),)
+    return pl.pallas_call(
+        functools.partial(near_body, planes, comps, len(after), near_columns),
+        out_shape=tuple(jax.ShapeDtypeStruct((slab, comps, planes, n), F32) for n, _ in shapes),
         grid=(total // rows,),
         in_specs=[
             pl.BlockSpec((rows, columns), lambda i: (i, 0)),
@@ -351,7 +377,7 @@
             pl.BlockSpec((1, planes), lambda i: (0, 0)),
         ]
         + [pl.BlockSpec(memory_space=pltpu.HBM)] * len(after),
-        out_specs=pl.BlockSpec((GROUP, comps, planes, columns), lambda i: (i, 0, 0, 0)),
+        out_specs=tuple(pl.BlockSpec((GROUP, comps, planes, n), lambda i: (i, 0, 0, 0)) for _, n in shapes),
         scratch_shapes=[
             pltpu.VMEM((rows, columns), BF16),
             pltpu.VMEM((rows, rows), BF16),
@@ -368,21 +394,21 @@
     pick = jnp.where(lane == 0, 128.0, jnp.where(lane < 3, 1.0, 0.0)).astype(BF16)
     slots = s_ref.shape[0]
     if len(got_ref.shape) == 4:
-        values = got_ref[:, :, :MOST, :]
-        meta = got_ref[:, :, MOST:, :BLOCK]
+        values = [got_ref[:, :, c * MOST : (c + 1) * MOST, :] for c in range(4)]
     else:
-        values = got_ref[:, :, : 3 * BLOCK]
-        meta = got_ref[:, :, 3 * BLOCK :]
-    meta = meta.astype(F32).reshape(slots, BLOCK).astype(BF16)
-    l_ref[...] = mm_nt(pick, meta).astype(jnp.int32)
-    s_ref[:, : 3 * BLOCK] = values.astype(F32).reshape(slots, 3 * BLOCK).astype(BF16)
+        values = [got_ref[:, :, c * BLOCK : (c + 1) * BLOCK] for c in range(4)]
+    values = [x.astype(F32).reshape(slots, BLOCK).astype(BF16) for x in values]
+    l_ref[...] = mm_nt(pick, values[3]).astype(jnp.int32)
+    for c in range(3):
+        s_ref[:, c * BLOCK : (c + 1) * BLOCK] = values[c]
     s_ref[:, 3 * BLOCK :] = jnp.ones((slots, BLOCK), BF16)
 
 
 def markers_spec(got, slab):
     if got.ndim == 4:
-        block = (got.shape[0], got.shape[1], GROUP, got.shape[3])
-        return pl.BlockSpec(block, lambda *_: (0, 0, slab // GROUP, 0)), got.shape[0] * got.shape[1] * MOST
+        rows = 4 * MOST
+        block = (got.shape[0], got.shape[1], rows, got.shape[3])
+        return pl.BlockSpec(block, lambda *_: (0, 0, 3 * slab // rows, 0)), got.shape[0] * got.shape[1] * MOST
     return pl.BlockSpec(got.shape, lambda *_: (0, 0, 0)), got.shape[0] * MOST
 
 
@@ -407,54 +433,100 @@
                 o_ref[some, c, :, cells] = (total * inverse).reshape(group, planes, BLOCK)
 
 
-def last_body(planes, comps, group, xblocks, start, order_ref, r_ref, got_ref, p_ref, o_ref, s_ref, l_ref):
-    pairs = r_ref.shape[1]
-    step = pl.program_id(0) * pl.num_programs(1) + pl.program_id(1)
+def mark_body(planes, comps, group, xblocks, start, got_ref, p_ref, o_ref, i_ref, s_ref, l_ref):
+    step = pl.program_id(0)
 
     @pl.when(step == 0)
     def _():
         ready_markers(got_ref, s_ref, l_ref)
 
-    for xg in range(pairs):
-        settle(
-            order_ref,
-            lambda some, xg=xg: r_ref[:, xg, some, :],
-            s_ref,
-            l_ref,
-            p_ref,
-            o_ref,
-            comps,
-            BLOCK,
-            group,
-            xblocks,
-            start + step * pairs + xg,
-            xg * BLOCK,
-        )
-
-
-def last(field, returned, got, order, first, count, group):
-    slab, comps, planes, columns = field.shape
+    blocks = p_ref.shape[3] // BLOCK
+    lines = group * planes
+    slots = s_ref.shape[0]
+    for b in range(blocks):
+        cells = slice(b * BLOCK, (b + 1) * BLOCK)
+        for g in range(p_ref.shape[0] // group):
+            some = slice(g * group, (g + 1) * group)
+            line = (g * lines + lax.broadcasted_iota(jnp.int32, (lines, slots), 0)) * xblocks + 1
+            chosen = (line + (start + step * blocks + b) == l_ref[0:1, :]).astype(F32).astype(BF16)
+            share = mm(chosen, s_ref[...])
+            inverse = 1.0 / (1.0 + share[:, 3 * BLOCK :])
+            i_ref[some, :, cells] = (time_step * inverse).reshape(group, planes, BLOCK)
+            for c in range(comps):
+                total = p_ref[some, c, :, cells].reshape(lines, BLOCK) + share[:, c * BLOCK : (c + 1) * BLOCK]
+                o_ref[some, c, :, cells] = (total * inverse).reshape(group, planes, BLOCK)
+
+
+def mark(far, got, columns, group, after):
+    slab, comps, planes, wide = far.shape
+    step = 2 * BLOCK
+    spec = pl.BlockSpec((slab, comps, planes, step), lambda i: (0, 0, 0, i))
+    got_spec, slots = markers_spec(got, slab)
+
+    def body(*refs):
+        start = (columns - wide) // BLOCK
+        mark_body(planes, comps, group, columns // BLOCK, start, *refs[:2], *refs[2 + len(after) :])
+
+    return pl.pallas_call(
+        body,
+        out_shape=(
+            jax.ShapeDtypeStruct(far.shape, F32),
+            jax.ShapeDtypeStruct((slab, planes, wide), F32),
+        ),
+        grid=(wide // step,),
+        in_specs=[got_spec, spec] + [pl.BlockSpec(memory_space=pltpu.HBM)] * len(after),
+        out_specs=(spec, pl.BlockSpec((slab, planes, step), lambda i: (0, 0, i))),
+        scratch_shapes=[pltpu.VMEM((slots, 4 * BLOCK), BF16), pltpu.VMEM((8, slots), jnp.int32)],
+        compiler_params=pltpu.CompilerParams(vmem_limit_bytes=ROOM),
+        cost_estimate=cost(SHORT),
+        name="mark",
+    )(got, far, *after)
+
+
+def last_body(planes, comps, count, extra, order_ref, *rest):
+    r_refs, (i_ref, p_ref), o_ref = rest[:count], rest[count : count + 2], rest[count + 2 + extra]
+    group = p_ref.shape[0]
+    groups = r_refs[0].shape[1]
+    lines = group * planes
+    for q in range(count):
+        for xg in range(groups):
+            at = (q * groups + xg) * BLOCK
+            cells = slice(at, at + BLOCK)
+            moved = mm(order_ref[...], r_refs[q][:, xg].reshape(lines, comps * BLOCK))
+            weight = i_ref[:, :, cells]
+            for c in range(comps):
+                term = moved[:, c * BLOCK : (c + 1) * BLOCK].reshape(group, planes, BLOCK)
+                o_ref[:, c, :, cells] = p_ref[:, c, :, cells] + term * weight
+
+
+def last(field, far, weight, returned, order):
+    slab, comps, planes, wide = far.shape
     groups = returned.shape[1]
-    steps = groups // 2
-    spec = pl.BlockSpec((slab, comps, planes, 2 * BLOCK), lambda q, i: (0, 0, 0, (first + q) * steps + i))
-    got_spec, slots = markers_spec(got, slab)
-    return pl.pallas_call(
-        functools.partial(last_body, planes, comps, group, columns // BLOCK, first * groups),
-        out_shape=jax.ShapeDtypeStruct(field.shape, F32),
-        grid=(count, steps),
-        in_specs=[
-            pl.BlockSpec(order.shape, lambda q, i: (0, 0)),
-            pl.BlockSpec((planes, 2, slab, comps * BLOCK), lambda q, i: (0, i, q, 0)),
-            got_spec,
-            spec,
-        ],
-        out_specs=spec,
-        input_output_aliases={3: 0},
-        scratch_shapes=[pltpu.VMEM((slots, 4 * BLOCK), BF16), pltpu.VMEM((8, slots), jnp.int32)],
-        compiler_params=pltpu.CompilerParams(vmem_limit_bytes=VMEM),
+    count = wide // (groups * BLOCK)
+    steps = slab // GROUP
+    columns = wide if field is None else field.shape[3]
+    skip = columns // wide - 1
+    held = () if field is None else (field,)
+    return pl.pallas_call(
+        functools.partial(last_body, planes, comps, count, len(held)),
+        out_shape=jax.ShapeDtypeStruct((slab, comps, planes, columns), F32),
+        grid=(steps,),
+        in_specs=[pl.BlockSpec(order.shape, lambda i: (0, 0))]
+        + [
+            pl.BlockSpec((planes, groups, GROUP, comps * BLOCK), lambda i, q=q: (0, 0, q * steps + i, 0))
+            for q in range(count)
+        ]
+        + [
+            pl.BlockSpec((GROUP, planes, wide), lambda i: (i, 0, 0)),
+            pl.BlockSpec((GROUP, comps, planes, wide), lambda i: (i, 0, 0, 0)),
+        ]
+        + [pl.BlockSpec(memory_space=pltpu.HBM)] * len(held),
+        out_specs=pl.BlockSpec((GROUP, comps, planes, wide), lambda i: (i, 0, 0, skip)),
+        input_output_aliases={3 + count: 0} if held else {},
+        compiler_params=pltpu.CompilerParams(vmem_limit_bytes=ROOM),
         cost_estimate=cost(SHORT),
         name="last",
-    )(order, returned, got, field)
+    )(order, *([returned] * count), weight, far, *held)
 
 
 def last_apart_body(comps, group, xblocks, start, ways, me_ref, order_ref, got_ref, own_ref, *rest):
@@ -576,36 +648,37 @@
     lines = jnp.transpose(velocity, (0, 2, 1, 3)).reshape(slab * comps * planes, columns)
     order = jnp.asarray(pack_order(planes, comps), BF16)
     back = jnp.asarray(unpack_order(planes, group), BF16)
+    small = jnp.asarray(unpack_order(planes, GROUP), BF16)
     metric_col = metric_z[:, None]
-    marked = markers(ib_target, ib_owner, ib_block, ib_count, devices)
     apart = row_count == planes and chunks == QUARTERS and slab == QUARTERS * GROUP
+    marked, *labels = markers(ib_target, ib_owner, ib_block, ib_count, me, devices, ways, apart)
     at_once = 2 if apart else chunks
+    near_columns = columns // 2 if apart else 0
     first = pack(lines, order, at_once, planes, comps, groups, slab)
     block = (devices,) + first.shape[2:]
     arrived = exchange(first.reshape(block)).reshape((row_count, ways) + first.shape[2:])
-    field = near(
-        lines, deriv_x, deriv_y, metric_x[None, :], metric_y[None, :], planes, comps, slab, (first,)
+    *fields, far = near(
+        lines, deriv_x, deriv_y, metric_x[None, :], metric_y[None, :], planes, comps, slab, near_columns, (first,)
     )
-
-    def terms_of(x, near_in, near_out, after):
-        return depth(x, me, deriv_z, metric_col, at_once, slab, near_in, near_out, after)
 
     if not apart:
         got = exchange(marked.reshape(devices, MOST, 4 * BLOCK))
-        terms = terms_of(arrived, False, False, (field,))
+        terms = depth(arrived, me, deriv_z, metric_col, at_once, slab, False, False, (far,))
         home = exchange(terms.reshape(block)).reshape(first.shape)
-        field = last(field, home, got, back, 0, chunks, group)
-        return jnp.transpose(field, (0, 2, 1, 3))
+        far, weight = mark(far, got, columns, group, ())
+        return jnp.transpose(last(None, far, weight, home, small), (0, 2, 1, 3))
 
     def outward(k, after, marked=None):
         return pack_apart(lines, order, me, k, planes, comps, ways, slab, after, marked)
 
+    (field,) = fields
+    marked = (marked.reshape(ways, planes, MOST, comps * BLOCK), labels[0].reshape(ways, planes, MOST, BLOCK))
     sent3 = outward(3, (field,))
-    sent2 = outward(2, (sent3[0],), marked.reshape(planes, ways, MOST, (comps + 1) * BLOCK))
-    later2, later3 = lax.optimization_barrier((sent2[1:], sent3[1:], arrived))[:2]
-    come2 = across(later2)
-    come3 = across(later3)
-    terms = terms_of(arrived, False, True, (sent2[0],))
+    sent2 = outward(2, (sent3[0],), marked)
+    later2, later3 = lax.optimization_barrier((sent2[EARLY:], sent3[EARLY:], arrived))[:2]
+    come2 = across(tuple(sent2[1:EARLY]) + tuple(later2))
+    come3 = across(tuple(sent3[1:EARLY]) + tuple(later3))
+    terms = depth(arrived, me, deriv_z, metric_col, 2, slab, False, True, (sent2[0],))
     home = along(terms)
     joined2 = join((sent2[0],) + come2, (terms,))
     split0 = split(home, 0, slab, (joined2,))
@@ -620,8 +693,8 @@
     home_all = exchange(terms.reshape(block)).reshape(first.shape)
     field = last_apart(field, home, back0, got, back, me, 0, group, (terms,))
     field = last_apart(field, home, back1, got, back, me, 1, group, ())
-    field = last(field, home_all, got, back, 2, 2, group)
-    return jnp.transpose(field, (0, 2, 1, 3))
+    far, weight = mark(far, got, columns, group, (field,))
+    return jnp.transpose(last(field, far, weight, home_all, small), (0, 2, 1, 3))
 
 
 def solution(mesh):

time: 314 us -> 306 us (0.975)
  waiting for transfers between devices: 129 us -> 119 us
    ppermute x12, waiting for transfers between devices: 49.3 us -> 35.5 us  [across(): lax.ppermute(piece, 'col', [(c, c ^ k) for c in range(ways)])]
    all_to_all x3, waiting for transfers between devices: 7.36 us -> 16.7 us  [along(): return lax.all_to_all(x, 'row', split_axis=0, concat_axis=0, tiled=True)]
    all_to_all x2, waiting for transfers between devices: 72.7 us -> 66.7 us  [exchange(): return lax.all_to_all(x, AXES, split_axis=0, concat_axis=0, tiled=True)]
    pallas_call x5 -> x6, Pallas kernels: 63.5 us -> 67.9 us  [the longest x1 43.3 us: near(): pl.pallas_call(functools.partial(near_body, planes, comps, len(after), ne...]
  transfers between devices with their start and end apart: 17 -> 17, of which waited for: 8 -> 8; matrix products, arithmetic and copies ran while one was open for 1% -> 1% of each run, Pallas kernels for 41% -> 43%
where the time goes in v2:
time: 306 us; the launch traced here: 305 us
  Pallas kernels  144 us (47%)
  waiting for transfers between devices  119 us (39%)
  starting transfers between devices  38.1 us (12%)
    all_to_all x2, waiting for transfers between devices, exchange(): return lax.all_to_all(x, AXES, split_axis=0, concat_axis=0, tiled=True)  66.7 us
    pallas_call x3, Pallas kernels, depth(): pl.pallas_call(functools.partial(depth_body, count, slab, block, len(extr...  50.1 us
    pallas_call x1, Pallas kernels, near(): pl.pallas_call(functools.partial(near_body, planes, comps, len(after), ne...  43.3 us
    ppermute x12, waiting for transfers between devices, across(): lax.ppermute(piece, 'col', [(c, c ^ k) for c in range(ways)])  35.5 us
    all_to_all x3, waiting for transfers between devices, along(): return lax.all_to_all(x, 'row', split_axis=0, concat_axis=0, tiled=True)  16.7 us
    ppermute x12, starting transfers between devices, across(): lax.ppermute(piece, 'col', [(c, c ^ k) for c in range(ways)])  14.4 us
    all_to_all x3, starting transfers between devices, along(): return lax.all_to_all(x, 'row', split_axis=0, concat_axis=0, tiled=True)  13.1 us
    pallas_call x2, Pallas kernels, last_apart(): pl.pallas_call(functools.partial(last_apart_body, comps, group, columns /...  11.6 us
  transfers between devices with their start and end apart: 17, of which 8 were waited for; matrix products, arithmetic and copies ran while one was open for 1% of the time, Pallas kernels for 43%

profile of v2, /device:TPU:8, one launch (start us, length us, event | category | flops | bytes accessed | tf_op | source)
XLA Modules:
  0.0 305.0 jit_solution(14425927802841625426)
XLA Ops:
  0.0 4.7 %pack.1.rest_0_ = bf16[8,4,128,384]{3,2,1,0:T(8,128)(2,1)} custom-call(bf16[384,384]{1,0:T(8,128)(2,1)} %constant.10.clone.order_ref, bf16[1536,2048]{1,0:T(8,128)(2,1)} %bitcast.19), custom_call_target="tpu_custom_call" | custom-call | flops 1 | bytes 1 | tf_op jit(solution)/shard_map/pack/pallas_call | solution.py:89
  4.7 6.0 %all-to-all-start = ((bf16[32,128,384]{2,1,0:T(8,128)(2,1)}), bf16[32,128,384]{2,1,0:T(8,128)(2,1)S(1)}, u32[]{:S(2)}, u32[]{:S(2)}) async-start(bf16[32,128,384]{2,1,0:T(8,128)(2,1)} %bitcast.29), calls=%async_computation | async-start | bytes 6291456 | tf_op jit(solution)/shard_map/all_to_all | solution.py:625
  10.7 43.3 %near.1 = (f32[64,3,8,2048]{3,2,1,0:T(8,128)}, f32[64,3,8,1024]{3,2,1,0:T(8,128)}) custom-call(bf16[1536,2048]{1,0:T(8,128)(2,1)} %bitcast.20, bf16[2048,2048]{1,0:T(8,128)(2,1)} %dx_ref.1, bf16[8,8]{1,0:T(8,128)(2,1)} %dy_ref.1, f32[1,2048]{1,0:T(1,128)} %bitcast.35, f32[1,8]{1,0:T(1,128)} %bitcast.38, bf16[8,4,128,384]{3,2,1,0:T(8,128)(2,1)} %pack.1.rest_0_), custom_call_target="tpu_custom_call" | custom-call | flops 1 | bytes 1 | tf_op jit(solution)/shard_map/near/pallas_call | solution.py:368
  54.0 3.7 %pack_apart.2 = (bf16[8,64,384]{2,1,0:T(8,128)(2,1)}, bf16[8,64,384]{2,1,0:T(8,128)(2,1)}, bf16[8,64,384]{2,1,0:T(8,128)(2,1)}, bf16[8,64,384]{2,1,0:T(8,128)(2,1)}) custom-call(s32[1]{0:T(128)} %bitcast.me_ref, bf16[384,384]{1,0:T(8,128)(2,1)} %constant.10.clone.order_ref, bf16[1536,2048]{1,0:T(8,128)(2,1)} %bitcast.21, bf16[1536,2048]{1,0:T(8,128)(2,1)} %bitcast.22, ...), custom_call_target="tpu_custom_call" | custom-call | flops 1 | bytes 1 | tf_op jit(solution)/shard_map/pack_apart/pallas_call | solution.py:137
  58.3 0.7 copy.22.block_col
  59.1 0.7 copy.21.owner_col
  59.8 2.0 markers.1
  61.8 3.8 %pack_apart.3 = (bf16[8,224,128]{2,1,0:T(8,128)(2,1)}, bf16[8,224,128]{2,1,0:T(8,128)(2,1)}, bf16[8,224,128]{2,1,0:T(8,128)(2,1)}, bf16[8,224,128]{2,1,0:T(8,128)(2,1)}) custom-call(s32[1]{0:T(128)} %bitcast.me_ref, bf16[384,384]{1,0:T(8,128)(2,1)} %constant.10.clone.order_ref, bf16[1536,2048]{1,0:T(8,128)(2,1)} %bitcast.25, bf16[1536,2048]{1,0:T(8,128)(2,1)} %bitcast.26, ...), custom_call_target="tpu_custom_call" | custom-call | flops 1 | bytes 1 | tf_op jit(solution)/shard_map/pack_apart/pallas_call | solution.py:137
  65.6 0.3 collective-permute-start.3
  65.9 16.4 %all-to-all-done = bf16[32,128,384]{2,1,0:T(8,128)(2,1)S(1)} async-done(((bf16[32,128,384]{2,1,0:T(8,128)(2,1)}), bf16[32,128,384]{2,1,0:T(8,128)(2,1)S(1)}, u32[]{:S(2)}, u32[]{:S(2)}) %all-to-all-start) | async-done | bytes 3145760 | tf_op jit(solution)/shard_map/all_to_all | solution.py:625
  82.3 0.5 collective-permute-start.5
  82.8 3.9 %collective-permute-start = (bf16[8,64,384]{2,1,0:T(8,128)(2,1)}, bf16[8,64,384]{2,1,0:T(8,128)(2,1)}, u32[]{:S(2)}, u32[]{:S(2)}) collective-permute-start(bf16[8,64,384]{2,1,0:T(8,128)(2,1)} %get-tuple-element.31), channel_id=1, source_target_pairs={{0,1},{1,0},{2,3},{3,2},{4,5},{5,4},{6,7},{7,6},{8,9},{9,8},{10,11... | collective-permute-start | bytes 1179656 | tf_op jit(solution)/shard_map/ppermute | solution.py:616
  86.7 1.4 copy.23.m_ref
  88.0 0.0 collective-permute-start.1
  88.0 20.0 %depth.3.refs_4_ = bf16[8,4,128,384]{3,2,1,0:T(8,128)(2,1)} custom-call(s32[1]{0:T(128)} %bitcast.me_ref, bf16[8,4,128,384]{3,2,1,0:T(8,128)(2,1)} %bitcast.31, bf16[2048,2048]{1,0:T(8,128)(2,1)} %d_ref.5, f32[2048,1]{1,0:T(8,128)} %copy.23.m_ref, bf16[8,224,128]{2,1,0:T(8,128)(2,1)} %get-tuple-element.40.rest_0_.refs_0_), custom_call_target="tpu_custom_call" | custom-call | flops 1 | bytes 1 | tf_op jit(solution)/shard_map/depth/pallas_call | solution.py:251
  108.0 4.5 %all-to-all-start.1 = ((bf16[8,4,128,384]{3,2,1,0:T(8,128)(2,1)}), bf16[8,4,128,384]{3,2,1,0:T(8,128)(2,1)}, u32[]{:S(2)}, u32[]{:S(2)}) async-start(bf16[8,4,128,384]{3,2,1,0:T(8,128)(2,1)} %depth.3.refs_4_), calls=%async_computation.1 | async-start | bytes 6291456 | tf_op jit(solution)/shard_map/all_to_all | solution.py:621
  112.5 0.0 collective-permute-done.3.refs_1_
  112.5 1.3 collective-permute-start.2
  113.8 16.1 %collective-permute-done.4.refs_2_ = bf16[8,224,128]{2,1,0:T(8,128)(2,1)} collective-permute-done((bf16[8,224,128]{2,1,0:T(8,128)(2,1)}, bf16[8,224,128]{2,1,0:T(8,128)(2,1)}, u32[]{:S(2)}, u32[]{:S(2)}) %collective-permute-start.4) | collective-permute-done | bytes 458784 | tf_op jit(solution)/shard_map/ppermute | solution.py:616
  130.0 10.8 %collective-permute-done.5.refs_3_ = bf16[8,224,128]{2,1,0:T(8,128)(2,1)} collective-permute-done((bf16[8,224,128]{2,1,0:T(8,128)(2,1)}, bf16[8,224,128]{2,1,0:T(8,128)(2,1)}, u32[]{:S(2)}, u32[]{:S(2)}) %collective-permute-start.5) | collective-permute-done | bytes 458784 | tf_op jit(solution)/shard_map/ppermute | solution.py:616
  140.8 2.6 join.2.rest_0_
  143.4 7.0 %all-to-all-done.1.x_ref.own_ref = bf16[8,4,128,384]{3,2,1,0:T(8,128)(2,1)} async-done(((bf16[8,4,128,384]{3,2,1,0:T(8,128)(2,1)}), bf16[8,4,128,384]{3,2,1,0:T(8,128)(2,1)}, u32[]{:S(2)}, u32[]{:S(2)}) %all-to-all-start.1) | async-done | bytes 3145760 | tf_op jit(solution)/shard_map/all_to_all | solution.py:621
  150.4 4.3 %all-to-all-start.3 = ((bf16[8,4,224,128]{3,2,1,0:T(8,128)(2,1)}), bf16[8,4,224,128]{3,2,1,0:T(8,128)(2,1)}, u32[]{:S(2)}, u32[]{:S(2)}) async-start(bf16[8,4,224,128]{3,2,1,0:T(8,128)(2,1)} %join.2.rest_0_), calls=%async_computation.3 | async-start | bytes 3670016 | tf_op jit(solution)/shard_map/all_to_all | solution.py:621
  154.7 2.3 split.2
  157.0 2.7 collective-permute-start.7
  159.8 2.2 split.3
  162.0 0.8 collective-permute-start.8
  162.8 0.0 collective-permute-done.1.refs_2_
  162.8 3.6 %collective-permute-start.10 = (bf16[8,64,384]{2,1,0:T(8,128)(2,1)}, bf16[8,64,384]{2,1,0:T(8,128)(2,1)}, u32[]{:S(2)}, u32[]{:S(2)}) collective-permute-start(bf16[8,64,384]{2,1,0:T(8,128)(2,1)} %get-tuple-element.49), channel_id=1, source_target_pairs={{0,2},{1,3},{2,0},{3,1},{4,6},{5,7},{6,4},{7,5},{8,10},{9,11},{10,... | collective-permute-start | bytes 1179656 | tf_op jit(solution)/shard_map/ppermute | solution.py:616
  166.4 0.0 collective-permute-done.2.refs_3_
  166.4 0.0 collective-permute-start.9
  166.4 2.4 join.3.rest_0_
  168.8 9.7 %all-to-all-done.3.x_ref.got_ref.refs_0_ = bf16[8,4,224,128]{3,2,1,0:T(8,128)(2,1)} async-done(((bf16[8,4,224,128]{3,2,1,0:T(8,128)(2,1)}), bf16[8,4,224,128]{3,2,1,0:T(8,128)(2,1)}, u32[]{:S(2)}, u32[]{:S(2)}) %all-to-all-start.3) | async-done | bytes 1835040 | tf_op jit(solution)/shard_map/all_to_all | solution.py:621
  178.6 4.3 %all-to-all-start.2 = ((bf16[8,4,64,384]{3,2,1,0:T(8,128)(2,1)}), bf16[8,4,64,384]{3,2,1,0:T(8,128)(2,1)}, u32[]{:S(2)}, u32[]{:S(2)}) async-start(bf16[8,4,64,384]{3,2,1,0:T(8,128)(2,1)} %join.3.rest_0_), calls=%async_computation.2 | async-start | bytes 3145728 | tf_op jit(solution)/shard_map/all_to_all | solution.py:621
  182.9 15.2 %depth.4.rest_0_ = bf16[8,4,128,384]{3,2,1,0:T(8,128)(2,1)} custom-call(s32[1]{0:T(128)} %bitcast.me_ref, bf16[8,4,224,128]{3,2,1,0:T(8,128)(2,1)} %all-to-all-done.3.x_ref.got_ref.refs_0_, bf16[2048,2048]{1,0:T(8,128)(2,1)} %d_ref.5, f32[2048,1]{1,0:T(8,128)} %copy.23.m_ref, bf16[8,4,64,384]{3,2,1,0:T(8,128)(2,1)} %join.3.rest_0_), custom_call_target="tpu_custom_call" | custom-call | flops 1 | bytes 1 | tf_op jit(solution)/shard_map/depth/pallas_call | solution.py:251
  198.1 1.3 collective-permute-start.11
  199.3 4.6 %collective-permute-done.8.refs_2_.rest_2_ = bf16[8,64,384]{2,1,0:T(8,128)(2,1)} collective-permute-done((bf16[8,64,384]{2,1,0:T(8,128)(2,1)}, bf16[8,64,384]{2,1,0:T(8,128)(2,1)}, u32[]{:S(2)}, u32[]{:S(2)}) %collective-permute-start.8) | collective-permute-done | bytes 393248 | tf_op jit(solution)/shard_map/ppermute | solution.py:616
  203.9 0.0 collective-permute-done.6.refs_0_.rest_0_
  203.9 0.6 come.1.rest_1_
  204.5 0.0 all-to-all-done.2.x_ref
  204.5 15.0 %depth.5.rest_4_ = bf16[8,4,128,384]{3,2,1,0:T(8,128)(2,1)} custom-call(s32[1]{0:T(128)} %bitcast.me_ref, bf16[8,4,64,384]{3,2,1,0:T(8,128)(2,1)} %all-to-all-done.2.x_ref, bf16[2048,2048]{1,0:T(8,128)(2,1)} %d_ref.5, f32[2048,1]{1,0:T(8,128)} %copy.23.m_ref, bf16[8,4,128,384]{3,2,1,0:T(8,128)(2,1)} %depth.4.rest_0_, ...), custom_call_target="tpu_custom_call", output_to_operand_aliasing={{}: (4, {})} | custom-call | flops 1 | bytes 1 | tf_op jit(solution)/shard_map/depth/pallas_call | solution.py:251
  219.5 4.5 %all-to-all-start.4 = ((bf16[32,128,384]{2,1,0:T(8,128)(2,1)}), bf16[32,128,384]{2,1,0:T(8,128)(2,1)}, u32[]{:S(2)}, u32[]{:S(2)}) async-start(bf16[32,128,384]{2,1,0:T(8,128)(2,1)} %bitcast.30), calls=%async_computation.4 | async-start | bytes 6291456 | tf_op jit(solution)/shard_map/all_to_all | solution.py:625
  224.0 5.8 %last_apart.2.rest_3_ = f32[64,3,8,2048]{3,2,1,0:T(8,128)} custom-call(s32[1]{0:T(128)} %bitcast.me_ref, bf16[256,256]{1,0:T(8,128)(2,1)} %constant.11.clone.order_ref, bf16[8,4,224,128]{3,2,1,0:T(8,128)(2,1)} %all-to-all-done.3.x_ref.got_ref.refs_0_, bf16[8,4,128,384]{3,2,1,0:T(8,128)(2,1)} %all-to-all-done.1.x_ref.own_ref, ...), custom_call_target="tpu_custom_call", output_to_operand_aliasing={{}: (7, {})} | custom-call | flops 999999995904 | bytes 1 | tf_op jit(solution)/shard_map/last_apart/pallas_call | solution.py:570
  229.8 4.0 %collective-permute-done.11.rest_2_ = bf16[8,64,384]{2,1,0:T(8,128)(2,1)} collective-permute-done((bf16[8,64,384]{2,1,0:T(8,128)(2,1)}, bf16[8,64,384]{2,1,0:T(8,128)(2,1)}, u32[]{:S(2)}, u32[]{:S(2)}) %collective-permute-start.11) | collective-permute-done | bytes 393248 | tf_op jit(solution)/shard_map/ppermute | solution.py:616
  233.8 5.8 %last_apart.3.refs_2_.rest_4_ = f32[64,3,8,2048]{3,2,1,0:T(8,128)} custom-call(s32[1]{0:T(128)} %bitcast.me_ref, bf16[256,256]{1,0:T(8,128)(2,1)} %constant.11.clone.order_ref, bf16[8,4,224,128]{3,2,1,0:T(8,128)(2,1)} %all-to-all-done.3.x_ref.got_ref.refs_0_, bf16[8,4,128,384]{3,2,1,0:T(8,128)(2,1)} %all-to-all-done.1.x_ref.own_ref, ...), custom_call_target="tpu_custom_call", output_to_operand_aliasing={{}: (7, {})} | custom-call | flops 999999995904 | bytes 1 | tf_op jit(solution)/shard_map/last_apart/pallas_call | solution.py:570
  239.6 7.3 %mark.1 = (f32[64,3,8,1024]{3,2,1,0:T(8,128)}, f32[64,8,1024]{2,1,0:T(8,128)}) custom-call(bf16[8,4,224,128]{3,2,1,0:T(8,128)(2,1)} %all-to-all-done.3.x_ref.got_ref.refs_0_, f32[64,3,8,1024]{3,2,1,0:T(8,128)} %get-tuple-element.48.refs_1_, f32[64,3,8,2048]{3,2,1,0:T(8,128)} %last_apart.3.refs_2_.rest_4_), custom_call_target="tpu_custom_call" | custom-call | flops 1 | bytes 1 | tf_op jit(solution)/shard_map/mark/pallas_call | solution.py:470
  246.8 50.3 %all-to-all-done.4 = bf16[32,128,384]{2,1,0:T(8,128)(2,1)} async-done(((bf16[32,128,384]{2,1,0:T(8,128)(2,1)}), bf16[32,128,384]{2,1,0:T(8,128)(2,1)}, u32[]{:S(2)}, u32[]{:S(2)}) %all-to-all-start.4) | async-done | bytes 3145760 | tf_op jit(solution)/shard_map/all_to_all | solution.py:625
  297.2 7.8 %last.1 = f32[64,3,8,2048]{3,2,1,0:T(8,128)} custom-call(bf16[128,128]{1,0:T(8,128)(2,1)} %constant.12.clone.order_ref, bf16[8,4,128,384]{3,2,1,0:T(8,128)(2,1)} %bitcast.16.rest_0_.rest_1_, bf16[8,4,128,384]{3,2,1,0:T(8,128)(2,1)} %bitcast.16.rest_0_.rest_1_, f32[64,8,1024]{2,1,0:T(8,128)} %get-tuple-element.51.rest_2_, ...), custom_call_target="tpu_custom_call", output_to_operand_aliasing={{}: (5, {})} | custom-call | flops 1 | bytes 1 | tf_op jit(solution)/shard_map/last/pallas_call | solution.py:510
  (14 shorter events, 0.0 us)
Async XLA Ops:
  4.7 77.6 %all-to-all-start = ((bf16[32,128,384]{2,1,0:T(8,128)(2,1)}), bf16[32,128,384]{2,1,0:T(8,128)(2,1)S(1)}, u32[]{:S(2)}, u32[]{:S(2)}) async-start(bf16[32,128,384]{2,1,0:T(8,128)(2,1)} %bitcast.29), calls=%async_computation | async-start | bytes 6291456 | tf_op jit(solution)/shard_map/all_to_all | solution.py:625
  54.0 4.3 %copy-start.3 = (s32[1,128]{1,0:T(1,128)S(1)}, s32[1,128]{1,0:T(1,128)}, u32[]{:S(2)}) copy-start(s32[1,128]{1,0:T(1,128)} %param.23) | copy-start | bytes 1540
  54.0 5.1 %copy-start.2 = (s32[1,128]{1,0:T(1,128)S(1)}, s32[1,128]{1,0:T(1,128)}, u32[]{:S(2)}) copy-start(s32[1,128]{1,0:T(1,128)} %owner_row.1) | copy-start | bytes 1540
  61.8 24.9 %copy-start.1 = (f32[2048]{0:T(1024)S(1)}, f32[2048]{0:T(1024)}, u32[]{:S(2)}) copy-start(f32[2048]{0:T(1024)} %param.20) | copy-start | bytes 24580
  65.6 46.8 %collective-permute-start.3 = (bf16[8,224,128]{2,1,0:T(8,128)(2,1)}, bf16[8,224,128]{2,1,0:T(8,128)(2,1)}, u32[]{:S(2)}, u32[]{:S(2)}) collective-permute-start(bf16[8,224,128]{2,1,0:T(8,128)(2,1)} %get-tuple-element.41), channel_id=1, source_target_pairs={{0,1},{1,0},{2,3},{3,2},{4,5},{5,4},{6,7},{7,6},{8,9},{9,8},{10,11... | collective-permute-start | bytes 1376264 | tf_op jit(solution)/shard_map/ppermute | solution.py:616
  82.3 5.8 %copy-start = (bf16[32,128,384]{2,1,0:T(8,128)(2,1)}, bf16[32,128,384]{2,1,0:T(8,128)(2,1)S(1)}, u32[]{:S(2)}) copy-start(bf16[32,128,384]{2,1,0:T(8,128)(2,1)S(1)} %all-to-all-done) | copy-start | bytes 9437188
  82.3 47.7 %collective-permute-start.4 = (bf16[8,224,128]{2,1,0:T(8,128)(2,1)}, bf16[8,224,128]{2,1,0:T(8,128)(2,1)}, u32[]{:S(2)}, u32[]{:S(2)}) collective-permute-start(bf16[8,224,128]{2,1,0:T(8,128)(2,1)} %get-tuple-element.42), channel_id=1, source_target_pairs={{0,2},{1,3},{2,0},{3,1},{4,6},{5,7},{6,4},{7,5},{8,10},{9,11},{10,... | collective-permute-start | bytes 1376264 | tf_op jit(solution)/shard_map/ppermute | solution.py:616
  82.3 58.5 %collective-permute-start.5 = (bf16[8,224,128]{2,1,0:T(8,128)(2,1)}, bf16[8,224,128]{2,1,0:T(8,128)(2,1)}, u32[]{:S(2)}, u32[]{:S(2)}) collective-permute-start(bf16[8,224,128]{2,1,0:T(8,128)(2,1)} %get-tuple-element.43), channel_id=1, source_target_pairs={{0,3},{1,2},{2,1},{3,0},{4,7},{5,6},{6,5},{7,4},{8,11},{9,10},{10,... | collective-permute-start | bytes 1376264 | tf_op jit(solution)/shard_map/ppermute | solution.py:616
  82.8 79.2 %collective-permute-start = (bf16[8,64,384]{2,1,0:T(8,128)(2,1)}, bf16[8,64,384]{2,1,0:T(8,128)(2,1)}, u32[]{:S(2)}, u32[]{:S(2)}) collective-permute-start(bf16[8,64,384]{2,1,0:T(8,128)(2,1)} %get-tuple-element.31), channel_id=1, source_target_pairs={{0,1},{1,0},{2,3},{3,2},{4,5},{5,4},{6,7},{7,6},{8,9},{9,8},{10,11... | collective-permute-start | bytes 1179656 | tf_op jit(solution)/shard_map/ppermute | solution.py:616
  88.0 74.7 %collective-permute-start.1 = (bf16[8,64,384]{2,1,0:T(8,128)(2,1)}, bf16[8,64,384]{2,1,0:T(8,128)(2,1)}, u32[]{:S(2)}, u32[]{:S(2)}) collective-permute-start(bf16[8,64,384]{2,1,0:T(8,128)(2,1)} %get-tuple-element.38), channel_id=1, source_target_pairs={{0,2},{1,3},{2,0},{3,1},{4,6},{5,7},{6,4},{7,5},{8,10},{9,11},{10,... | collective-permute-start | bytes 1179656 | tf_op jit(solution)/shard_map/ppermute | solution.py:616
  108.0 42.4 %all-to-all-start.1 = ((bf16[8,4,128,384]{3,2,1,0:T(8,128)(2,1)}), bf16[8,4,128,384]{3,2,1,0:T(8,128)(2,1)}, u32[]{:S(2)}, u32[]{:S(2)}) async-start(bf16[8,4,128,384]{3,2,1,0:T(8,128)(2,1)} %depth.3.refs_4_), calls=%async_computation.1 | async-start | bytes 6291456 | tf_op jit(solution)/shard_map/all_to_all | solution.py:621
  112.5 53.9 %collective-permute-start.2 = (bf16[8,64,384]{2,1,0:T(8,128)(2,1)}, bf16[8,64,384]{2,1,0:T(8,128)(2,1)}, u32[]{:S(2)}, u32[]{:S(2)}) collective-permute-start(bf16[8,64,384]{2,1,0:T(8,128)(2,1)} %get-tuple-element.39), channel_id=1, source_target_pairs={{0,3},{1,2},{2,1},{3,0},{4,7},{5,6},{6,5},{7,4},{8,11},{9,10},{10,... | collective-permute-start | bytes 1179656 | tf_op jit(solution)/shard_map/ppermute | solution.py:616
  150.4 28.2 %all-to-all-start.3 = ((bf16[8,4,224,128]{3,2,1,0:T(8,128)(2,1)}), bf16[8,4,224,128]{3,2,1,0:T(8,128)(2,1)}, u32[]{:S(2)}, u32[]{:S(2)}) async-start(bf16[8,4,224,128]{3,2,1,0:T(8,128)(2,1)} %join.2.rest_0_), calls=%async_computation.3 | async-start | bytes 3670016 | tf_op jit(solution)/shard_map/all_to_all | solution.py:621
  157.0 41.1 %collective-permute-start.7 = (bf16[8,64,384]{2,1,0:T(8,128)(2,1)}, bf16[8,64,384]{2,1,0:T(8,128)(2,1)}, u32[]{:S(2)}, u32[]{:S(2)}) collective-permute-start(bf16[8,64,384]{2,1,0:T(8,128)(2,1)} %get-tuple-element.46), channel_id=1, source_target_pairs={{0,2},{1,3},{2,0},{3,1},{4,6},{5,7},{6,4},{7,5},{8,10},{9,11},{10,... | collective-permute-start | bytes 1179656 | tf_op jit(solution)/shard_map/ppermute | solution.py:616
  159.7 44.2 %collective-permute-start.6 = (bf16[8,64,384]{2,1,0:T(8,128)(2,1)}, bf16[8,64,384]{2,1,0:T(8,128)(2,1)}, u32[]{:S(2)}, u32[]{:S(2)}) collective-permute-start(bf16[8,64,384]{2,1,0:T(8,128)(2,1)} %get-tuple-element.44.rest_0_), channel_id=1, source_target_pairs={{0,1},{1,0},{2,3},{3,2},{4,5},{5,4},{6,7},{7,6},{8,9},{9,8},{10,11... | collective-permute-start | bytes 1179656 | tf_op jit(solution)/shard_map/ppermute | solution.py:616
  162.0 41.9 %collective-permute-start.8 = (bf16[8,64,384]{2,1,0:T(8,128)(2,1)}, bf16[8,64,384]{2,1,0:T(8,128)(2,1)}, u32[]{:S(2)}, u32[]{:S(2)}) collective-permute-start(bf16[8,64,384]{2,1,0:T(8,128)(2,1)} %get-tuple-element.47), channel_id=1, source_target_pairs={{0,3},{1,2},{2,1},{3,0},{4,7},{5,6},{6,5},{7,4},{8,11},{9,10},{10,... | collective-permute-start | bytes 1179656 | tf_op jit(solution)/shard_map/ppermute | solution.py:616
  162.8 67.1 %collective-permute-start.10 = (bf16[8,64,384]{2,1,0:T(8,128)(2,1)}, bf16[8,64,384]{2,1,0:T(8,128)(2,1)}, u32[]{:S(2)}, u32[]{:S(2)}) collective-permute-start(bf16[8,64,384]{2,1,0:T(8,128)(2,1)} %get-tuple-element.49), channel_id=1, source_target_pairs={{0,2},{1,3},{2,0},{3,1},{4,6},{5,7},{6,4},{7,5},{8,10},{9,11},{10,... | collective-permute-start | bytes 1179656 | tf_op jit(solution)/shard_map/ppermute | solution.py:616
  166.4 67.4 %collective-permute-start.9 = (bf16[8,64,384]{2,1,0:T(8,128)(2,1)}, bf16[8,64,384]{2,1,0:T(8,128)(2,1)}, u32[]{:S(2)}, u32[]{:S(2)}) collective-permute-start(bf16[8,64,384]{2,1,0:T(8,128)(2,1)} %get-tuple-element.45.refs_4_), channel_id=1, source_target_pairs={{0,1},{1,0},{2,3},{3,2},{4,5},{5,4},{6,7},{7,6},{8,9},{9,8},{10,11... | collective-permute-start | bytes 1179656 | tf_op jit(solution)/shard_map/ppermute | solution.py:616
  178.6 25.9 %all-to-all-start.2 = ((bf16[8,4,64,384]{3,2,1,0:T(8,128)(2,1)}), bf16[8,4,64,384]{3,2,1,0:T(8,128)(2,1)}, u32[]{:S(2)}, u32[]{:S(2)}) async-start(bf16[8,4,64,384]{3,2,1,0:T(8,128)(2,1)} %join.3.rest_0_), calls=%async_computation.2 | async-start | bytes 3145728 | tf_op jit(solution)/shard_map/all_to_all | solution.py:621
  198.1 35.7 %collective-permute-start.11 = (bf16[8,64,384]{2,1,0:T(8,128)(2,1)}, bf16[8,64,384]{2,1,0:T(8,128)(2,1)}, u32[]{:S(2)}, u32[]{:S(2)}) collective-permute-start(bf16[8,64,384]{2,1,0:T(8,128)(2,1)} %get-tuple-element.50), channel_id=1, source_target_pairs={{0,3},{1,2},{2,1},{3,0},{4,7},{5,6},{6,5},{7,4},{8,11},{9,10},{10,... | collective-permute-start | bytes 1179656 | tf_op jit(solution)/shard_map/ppermute | solution.py:616
  219.5 77.7 %all-to-all-start.4 = ((bf16[32,128,384]{2,1,0:T(8,128)(2,1)}), bf16[32,128,384]{2,1,0:T(8,128)(2,1)}, u32[]{:S(2)}, u32[]{:S(2)}) async-start(bf16[32,128,384]{2,1,0:T(8,128)(2,1)} %bitcast.30), calls=%async_computation.4 | async-start | bytes 6291456 | tf_op jit(solution)/shard_map/all_to_all | solution.py:625

commit v3 on v2

--- a/solution.py
+++ b/solution.py
@@ -14,6 +14,7 @@
 QUARTERS = 4
 VMEM = 60 << 20
 ROOM = 60 << 20
+LAST = 16
 SHORT = 1
 EARLY = 2
 PACK = 4
@@ -39,13 +40,13 @@
     return lax.dot_general(a, b, (((1,), (1,)), ((), ())), preferred_element_type=F32)
 
 
-def pack_order(planes, comps):
-    rows = GROUP * planes * comps
+def pack_order(planes, comps, group):
+    rows = group * planes * comps
     table = np.zeros((rows, rows), np.float32)
     for y in range(planes):
         for c in range(comps):
-            for z in range(GROUP):
-                table[(y * comps + c) * GROUP + z, (z * comps + c) * planes + y] = 1
+            for z in range(group):
+                table[(y * comps + c) * group + z, (z * comps + c) * planes + y] = 1
     return table
 
 
@@ -61,13 +62,15 @@
 def place_rows(o_ref, moved, planes, comps, wide, at_rows, spot):
     for y in range(planes):
         for c in range(comps):
-            at = (y * comps + c) * GROUP
-            o_ref[y, at_rows, c * wide : (c + 1) * wide] = moved[at : at + GROUP, spot]
+            group = moved.shape[0] // (planes * comps)
+            at = (y * comps + c) * group
+            o_ref[y, at_rows, c * wide : (c + 1) * wide] = moved[at : at + group, spot]
 
 
 def pack_body(planes, comps, wide, order_ref, v_ref, o_ref):
     lanes = v_ref.shape[1]
     rows = order_ref.shape[0]
+    group = rows // (planes * comps)
     for g in range(v_ref.shape[0] // rows):
         moved = mm(order_ref[...], v_ref[g * rows : (g + 1) * rows, :]).astype(BF16)
         for xg in range(lanes // wide):
@@ -77,7 +80,7 @@
                 planes,
                 comps,
                 wide,
-                slice(g * GROUP, (g + 1) * GROUP),
+                slice(g * group, (g + 1) * group),
                 slice(xg * wide, (xg + 1) * wide),
             )
 
@@ -439,6 +442,7 @@
     @pl.when(step == 0)
     def _():
         ready_markers(got_ref, s_ref, l_ref)
+        i_ref[...] = jnp.zeros_like(i_ref)
 
     blocks = p_ref.shape[3] // BLOCK
     lines = group * planes
@@ -451,7 +455,9 @@
             chosen = (line + (start + step * blocks + b) == l_ref[0:1, :]).astype(F32).astype(BF16)
             share = mm(chosen, s_ref[...])
             inverse = 1.0 / (1.0 + share[:, 3 * BLOCK :])
-            i_ref[some, :, cells] = (time_step * inverse).reshape(group, planes, BLOCK)
+            held = lax.broadcasted_iota(jnp.int32, (lines, BLOCK), 1) == step * blocks + b
+            at = slice(g * lines, (g + 1) * lines)
+            i_ref[at, :] = jnp.where(held, time_step * inverse, i_ref[at, :])
             for c in range(comps):
                 total = p_ref[some, c, :, cells].reshape(lines, BLOCK) + share[:, c * BLOCK : (c + 1) * BLOCK]
                 o_ref[some, c, :, cells] = (total * inverse).reshape(group, planes, BLOCK)
@@ -471,11 +477,11 @@
         body,
         out_shape=(
             jax.ShapeDtypeStruct(far.shape, F32),
-            jax.ShapeDtypeStruct((slab, planes, wide), F32),
+            jax.ShapeDtypeStruct((slab * planes, BLOCK), F32),
         ),
         grid=(wide // step,),
         in_specs=[got_spec, spec] + [pl.BlockSpec(memory_space=pltpu.HBM)] * len(after),
-        out_specs=(spec, pl.BlockSpec((slab, planes, step), lambda i: (0, 0, i))),
+        out_specs=(spec, pl.BlockSpec((slab * planes, BLOCK), lambda i: (0, 0))),
         scratch_shapes=[pltpu.VMEM((slots, 4 * BLOCK), BF16), pltpu.VMEM((8, slots), jnp.int32)],
         compiler_params=pltpu.CompilerParams(vmem_limit_bytes=ROOM),
         cost_estimate=cost(SHORT),
@@ -493,17 +499,18 @@
             at = (q * groups + xg) * BLOCK
             cells = slice(at, at + BLOCK)
             moved = mm(order_ref[...], r_refs[q][:, xg].reshape(lines, comps * BLOCK))
-            weight = i_ref[:, :, cells]
+            weight = i_ref[:, q * groups + xg : q * groups + xg + 1]
             for c in range(comps):
-                term = moved[:, c * BLOCK : (c + 1) * BLOCK].reshape(group, planes, BLOCK)
-                o_ref[:, c, :, cells] = p_ref[:, c, :, cells] + term * weight
+                term = (moved[:, c * BLOCK : (c + 1) * BLOCK] * weight).reshape(group, planes, BLOCK)
+                o_ref[:, c, :, cells] = p_ref[:, c, :, cells] + term
 
 
 def last(field, far, weight, returned, order):
     slab, comps, planes, wide = far.shape
     groups = returned.shape[1]
     count = wide // (groups * BLOCK)
-    steps = slab // GROUP
+    rows = order.shape[0] // planes
+    steps = slab // rows
     columns = wide if field is None else field.shape[3]
     skip = columns // wide - 1
     held = () if field is None else (field,)
@@ -513,15 +520,15 @@
         grid=(steps,),
         in_specs=[pl.BlockSpec(order.shape, lambda i: (0, 0))]
         + [
-            pl.BlockSpec((planes, groups, GROUP, comps * BLOCK), lambda i, q=q: (0, 0, q * steps + i, 0))
+            pl.BlockSpec((planes, groups, rows, comps * BLOCK), lambda i, q=q: (0, 0, q * steps + i, 0))
             for q in range(count)
         ]
         + [
-            pl.BlockSpec((GROUP, planes, wide), lambda i: (i, 0, 0)),
-            pl.BlockSpec((GROUP, comps, planes, wide), lambda i: (i, 0, 0, 0)),
+            pl.BlockSpec((rows * planes, BLOCK), lambda i: (i, 0)),
+            pl.BlockSpec((rows, comps, planes, wide), lambda i: (i, 0, 0, 0)),
         ]
         + [pl.BlockSpec(memory_space=pltpu.HBM)] * len(held),
-        out_specs=pl.BlockSpec((GROUP, comps, planes, wide), lambda i: (i, 0, 0, skip)),
+        out_specs=pl.BlockSpec((rows, comps, planes, wide), lambda i: (i, 0, 0, skip)),
         input_output_aliases={3 + count: 0} if held else {},
         compiler_params=pltpu.CompilerParams(vmem_limit_bytes=ROOM),
         cost_estimate=cost(SHORT),
@@ -646,15 +653,16 @@
     chunks = columns // (groups * BLOCK)
     me = lax.axis_index("col").astype(jnp.int32).reshape(1)
     lines = jnp.transpose(velocity, (0, 2, 1, 3)).reshape(slab * comps * planes, columns)
-    order = jnp.asarray(pack_order(planes, comps), BF16)
+    order = jnp.asarray(pack_order(planes, comps, GROUP), BF16)
+    quick = jnp.asarray(pack_order(planes, comps, GROUP // 2), BF16)
     back = jnp.asarray(unpack_order(planes, group), BF16)
-    small = jnp.asarray(unpack_order(planes, GROUP), BF16)
+    small = jnp.asarray(unpack_order(planes, LAST), BF16)
     metric_col = metric_z[:, None]
     apart = row_count == planes and chunks == QUARTERS and slab == QUARTERS * GROUP
     marked, *labels = markers(ib_target, ib_owner, ib_block, ib_count, me, devices, ways, apart)
     at_once = 2 if apart else chunks
     near_columns = columns // 2 if apart else 0
-    first = pack(lines, order, at_once, planes, comps, groups, slab)
+    first = pack(lines, quick, at_once, planes, comps, groups, slab)
     block = (devices,) + first.shape[2:]
     arrived = exchange(first.reshape(block)).reshape((row_count, ways) + first.shape[2:])
     *fields, far = near(

time: 306 us -> 305 us (level)
  no operation moved by 1% of the time
where the time goes in v3:
time: 305 us; the launch traced here: 304 us
  Pallas kernels  143 us (47%)
  waiting for transfers between devices  119 us (39%)
  starting transfers between devices  38.1 us (12%)
    all_to_all x2, waiting for transfers between devices, exchange(): return lax.all_to_all(x, AXES, split_axis=0, concat_axis=0, tiled=True)  67.1 us
    pallas_call x3, Pallas kernels, depth(): pl.pallas_call(functools.partial(depth_body, count, slab, block, len(extr...  50.1 us
    pallas_call x1, Pallas kernels, near(): pl.pallas_call(functools.partial(near_body, planes, comps, len(after), ne...  43.3 us
    ppermute x12, waiting for transfers between devices, across(): lax.ppermute(piece, 'col', [(c, c ^ k) for c in range(ways)])  35.5 us
    all_to_all x3, waiting for transfers between devices, along(): return lax.all_to_all(x, 'row', split_axis=0, concat_axis=0, tiled=True)  16.7 us
    ppermute x12, starting transfers between devices, across(): lax.ppermute(piece, 'col', [(c, c ^ k) for c in range(ways)])  14.4 us
    all_to_all x3, starting transfers between devices, along(): return lax.all_to_all(x, 'row', split_axis=0, concat_axis=0, tiled=True)  13.1 us
    pallas_call x2, Pallas kernels, last_apart(): pl.pallas_call(functools.partial(last_apart_body, comps, group, columns /...  11.6 us
  transfers between devices with their start and end apart: 17, of which 8 were waited for; matrix products, arithmetic and copies ran while one was open for 1% of the time, Pallas kernels for 43%

profile of v3, /device:TPU:8, one launch (start us, length us, event | category | flops | bytes accessed | tf_op | source)
XLA Modules:
  0.0 303.7 jit_solution(8700259274613642084)
XLA Ops:
  0.0 3.8 %pack.1.rest_0_ = bf16[8,4,128,384]{3,2,1,0:T(8,128)(2,1)} custom-call(bf16[192,192]{1,0:T(8,128)(2,1)} %constant.13.clone.order_ref, bf16[1536,2048]{1,0:T(8,128)(2,1)} %bitcast.19), custom_call_target="tpu_custom_call" | custom-call | flops 1 | bytes 1 | tf_op jit(solution)/shard_map/pack/pallas_call | solution.py:92
  3.8 6.0 %all-to-all-start = ((bf16[32,128,384]{2,1,0:T(8,128)(2,1)}), bf16[32,128,384]{2,1,0:T(8,128)(2,1)S(1)}, u32[]{:S(2)}, u32[]{:S(2)}) async-start(bf16[32,128,384]{2,1,0:T(8,128)(2,1)} %bitcast.29), calls=%async_computation | async-start | bytes 6291456 | tf_op jit(solution)/shard_map/all_to_all | solution.py:632
  9.8 43.3 %near.1 = (f32[64,3,8,2048]{3,2,1,0:T(8,128)}, f32[64,3,8,1024]{3,2,1,0:T(8,128)}) custom-call(bf16[1536,2048]{1,0:T(8,128)(2,1)} %bitcast.20, bf16[2048,2048]{1,0:T(8,128)(2,1)} %dx_ref.1, bf16[8,8]{1,0:T(8,128)(2,1)} %dy_ref.1, f32[1,2048]{1,0:T(1,128)} %bitcast.35, f32[1,8]{1,0:T(1,128)} %bitcast.38, bf16[8,4,128,384]{3,2,1,0:T(8,128)(2,1)} %pack.1.rest_0_), custom_call_target="tpu_custom_call" | custom-call | flops 1 | bytes 1 | tf_op jit(solution)/shard_map/near/pallas_call | solution.py:371
  53.2 3.7 %pack_apart.2 = (bf16[8,64,384]{2,1,0:T(8,128)(2,1)}, bf16[8,64,384]{2,1,0:T(8,128)(2,1)}, bf16[8,64,384]{2,1,0:T(8,128)(2,1)}, bf16[8,64,384]{2,1,0:T(8,128)(2,1)}) custom-call(s32[1]{0:T(128)} %bitcast.me_ref, bf16[384,384]{1,0:T(8,128)(2,1)} %constant.12.clone.order_ref, bf16[1536,2048]{1,0:T(8,128)(2,1)} %bitcast.21, bf16[1536,2048]{1,0:T(8,128)(2,1)} %bitcast.22, ...), custom_call_target="tpu_custom_call" | custom-call | flops 1 | bytes 1 | tf_op jit(solution)/shard_map/pack_apart/pallas_call | solution.py:140
  57.5 0.7 copy.23.block_col
  58.2 0.7 copy.22.owner_col
  59.0 2.0 markers.1
  61.0 3.8 %pack_apart.3 = (bf16[8,224,128]{2,1,0:T(8,128)(2,1)}, bf16[8,224,128]{2,1,0:T(8,128)(2,1)}, bf16[8,224,128]{2,1,0:T(8,128)(2,1)}, bf16[8,224,128]{2,1,0:T(8,128)(2,1)}) custom-call(s32[1]{0:T(128)} %bitcast.me_ref, bf16[384,384]{1,0:T(8,128)(2,1)} %constant.12.clone.order_ref, bf16[1536,2048]{1,0:T(8,128)(2,1)} %bitcast.25, bf16[1536,2048]{1,0:T(8,128)(2,1)} %bitcast.26, ...), custom_call_target="tpu_custom_call" | custom-call | flops 1 | bytes 1 | tf_op jit(solution)/shard_map/pack_apart/pallas_call | solution.py:140
  64.8 0.3 collective-permute-start.3
  65.0 16.4 %all-to-all-done = bf16[32,128,384]{2,1,0:T(8,128)(2,1)S(1)} async-done(((bf16[32,128,384]{2,1,0:T(8,128)(2,1)}), bf16[32,128,384]{2,1,0:T(8,128)(2,1)S(1)}, u32[]{:S(2)}, u32[]{:S(2)}) %all-to-all-start) | async-done | bytes 3145760 | tf_op jit(solution)/shard_map/all_to_all | solution.py:632
  81.4 0.0 collective-permute-start.4
  81.4 0.5 collective-permute-start.5
  81.9 3.9 %collective-permute-start = (bf16[8,64,384]{2,1,0:T(8,128)(2,1)}, bf16[8,64,384]{2,1,0:T(8,128)(2,1)}, u32[]{:S(2)}, u32[]{:S(2)}) collective-permute-start(bf16[8,64,384]{2,1,0:T(8,128)(2,1)} %get-tuple-element.31), channel_id=1, source_target_pairs={{0,1},{1,0},{2,3},{3,2},{4,5},{5,4},{6,7},{7,6},{8,9},{9,8},{10,11... | collective-permute-start | bytes 1179656 | tf_op jit(solution)/shard_map/ppermute | solution.py:623
  85.8 1.4 copy.24.m_ref
  87.2 20.0 %depth.3.refs_4_ = bf16[8,4,128,384]{3,2,1,0:T(8,128)(2,1)} custom-call(s32[1]{0:T(128)} %bitcast.me_ref, bf16[8,4,128,384]{3,2,1,0:T(8,128)(2,1)} %bitcast.31, bf16[2048,2048]{1,0:T(8,128)(2,1)} %d_ref.5, f32[2048,1]{1,0:T(8,128)} %copy.24.m_ref, bf16[8,224,128]{2,1,0:T(8,128)(2,1)} %get-tuple-element.40.rest_0_.refs_0_), custom_call_target="tpu_custom_call" | custom-call | flops 1 | bytes 1 | tf_op jit(solution)/shard_map/depth/pallas_call | solution.py:254
  107.1 4.5 %all-to-all-start.1 = ((bf16[8,4,128,384]{3,2,1,0:T(8,128)(2,1)}), bf16[8,4,128,384]{3,2,1,0:T(8,128)(2,1)}, u32[]{:S(2)}, u32[]{:S(2)}) async-start(bf16[8,4,128,384]{3,2,1,0:T(8,128)(2,1)} %depth.3.refs_4_), calls=%async_computation.1 | async-start | bytes 6291456 | tf_op jit(solution)/shard_map/all_to_all | solution.py:628
  111.6 0.0 collective-permute-done.3.refs_1_
  111.6 1.3 collective-permute-start.2
  113.0 16.1 %collective-permute-done.4.refs_2_ = bf16[8,224,128]{2,1,0:T(8,128)(2,1)} collective-permute-done((bf16[8,224,128]{2,1,0:T(8,128)(2,1)}, bf16[8,224,128]{2,1,0:T(8,128)(2,1)}, u32[]{:S(2)}, u32[]{:S(2)}) %collective-permute-start.4) | collective-permute-done | bytes 458784 | tf_op jit(solution)/shard_map/ppermute | solution.py:623
  129.1 10.8 %collective-permute-done.5.refs_3_ = bf16[8,224,128]{2,1,0:T(8,128)(2,1)} collective-permute-done((bf16[8,224,128]{2,1,0:T(8,128)(2,1)}, bf16[8,224,128]{2,1,0:T(8,128)(2,1)}, u32[]{:S(2)}, u32[]{:S(2)}) %collective-permute-start.5) | collective-permute-done | bytes 458784 | tf_op jit(solution)/shard_map/ppermute | solution.py:623
  140.0 2.6 join.2.rest_0_
  142.5 7.0 %all-to-all-done.1.x_ref.own_ref = bf16[8,4,128,384]{3,2,1,0:T(8,128)(2,1)} async-done(((bf16[8,4,128,384]{3,2,1,0:T(8,128)(2,1)}), bf16[8,4,128,384]{3,2,1,0:T(8,128)(2,1)}, u32[]{:S(2)}, u32[]{:S(2)}) %all-to-all-start.1) | async-done | bytes 3145760 | tf_op jit(solution)/shard_map/all_to_all | solution.py:628
  149.5 4.3 %all-to-all-start.3 = ((bf16[8,4,224,128]{3,2,1,0:T(8,128)(2,1)}), bf16[8,4,224,128]{3,2,1,0:T(8,128)(2,1)}, u32[]{:S(2)}, u32[]{:S(2)}) async-start(bf16[8,4,224,128]{3,2,1,0:T(8,128)(2,1)} %join.2.rest_0_), calls=%async_computation.3 | async-start | bytes 3670016 | tf_op jit(solution)/shard_map/all_to_all | solution.py:628
  153.9 2.3 split.2
  156.2 2.7 collective-permute-start.7
  158.9 2.3 split.3
  161.2 0.8 collective-permute-start.8
  161.9 0.0 collective-permute-done.1.refs_2_
  161.9 3.6 %collective-permute-start.10 = (bf16[8,64,384]{2,1,0:T(8,128)(2,1)}, bf16[8,64,384]{2,1,0:T(8,128)(2,1)}, u32[]{:S(2)}, u32[]{:S(2)}) collective-permute-start(bf16[8,64,384]{2,1,0:T(8,128)(2,1)} %get-tuple-element.49), channel_id=1, source_target_pairs={{0,2},{1,3},{2,0},{3,1},{4,6},{5,7},{6,4},{7,5},{8,10},{9,11},{10,... | collective-permute-start | bytes 1179656 | tf_op jit(solution)/shard_map/ppermute | solution.py:623
  165.6 0.0 collective-permute-done.2.refs_3_
  165.6 0.0 collective-permute-start.9
  165.6 2.5 join.3.rest_0_
  168.0 9.7 %all-to-all-done.3.x_ref.got_ref.refs_0_ = bf16[8,4,224,128]{3,2,1,0:T(8,128)(2,1)} async-done(((bf16[8,4,224,128]{3,2,1,0:T(8,128)(2,1)}), bf16[8,4,224,128]{3,2,1,0:T(8,128)(2,1)}, u32[]{:S(2)}, u32[]{:S(2)}) %all-to-all-start.3) | async-done | bytes 1835040 | tf_op jit(solution)/shard_map/all_to_all | solution.py:628
  177.7 4.3 %all-to-all-start.2 = ((bf16[8,4,64,384]{3,2,1,0:T(8,128)(2,1)}), bf16[8,4,64,384]{3,2,1,0:T(8,128)(2,1)}, u32[]{:S(2)}, u32[]{:S(2)}) async-start(bf16[8,4,64,384]{3,2,1,0:T(8,128)(2,1)} %join.3.rest_0_), calls=%async_computation.2 | async-start | bytes 3145728 | tf_op jit(solution)/shard_map/all_to_all | solution.py:628
  182.0 15.2 %depth.4.rest_0_ = bf16[8,4,128,384]{3,2,1,0:T(8,128)(2,1)} custom-call(s32[1]{0:T(128)} %bitcast.me_ref, bf16[8,4,224,128]{3,2,1,0:T(8,128)(2,1)} %all-to-all-done.3.x_ref.got_ref.refs_0_, bf16[2048,2048]{1,0:T(8,128)(2,1)} %d_ref.5, f32[2048,1]{1,0:T(8,128)} %copy.24.m_ref, bf16[8,4,64,384]{3,2,1,0:T(8,128)(2,1)} %join.3.rest_0_), custom_call_target="tpu_custom_call" | custom-call | flops 1 | bytes 1 | tf_op jit(solution)/shard_map/depth/pallas_call | solution.py:254
  197.2 1.3 collective-permute-start.11
  198.5 4.6 %collective-permute-done.8.refs_2_.rest_2_ = bf16[8,64,384]{2,1,0:T(8,128)(2,1)} collective-permute-done((bf16[8,64,384]{2,1,0:T(8,128)(2,1)}, bf16[8,64,384]{2,1,0:T(8,128)(2,1)}, u32[]{:S(2)}, u32[]{:S(2)}) %collective-permute-start.8) | collective-permute-done | bytes 393248 | tf_op jit(solution)/shard_map/ppermute | solution.py:623
  203.0 0.6 come.1.rest_1_
  203.6 0.0 all-to-all-done.2.x_ref
  203.6 15.0 %depth.5.rest_4_ = bf16[8,4,128,384]{3,2,1,0:T(8,128)(2,1)} custom-call(s32[1]{0:T(128)} %bitcast.me_ref, bf16[8,4,64,384]{3,2,1,0:T(8,128)(2,1)} %all-to-all-done.2.x_ref, bf16[2048,2048]{1,0:T(8,128)(2,1)} %d_ref.5, f32[2048,1]{1,0:T(8,128)} %copy.24.m_ref, bf16[8,4,128,384]{3,2,1,0:T(8,128)(2,1)} %depth.4.rest_0_, ...), custom_call_target="tpu_custom_call", output_to_operand_aliasing={{}: (4, {})} | custom-call | flops 1 | bytes 1 | tf_op jit(solution)/shard_map/depth/pallas_call | solution.py:254
  218.6 4.5 %all-to-all-start.4 = ((bf16[32,128,384]{2,1,0:T(8,128)(2,1)}), bf16[32,128,384]{2,1,0:T(8,128)(2,1)}, u32[]{:S(2)}, u32[]{:S(2)}) async-start(bf16[32,128,384]{2,1,0:T(8,128)(2,1)} %bitcast.30), calls=%async_computation.4 | async-start | bytes 6291456 | tf_op jit(solution)/shard_map/all_to_all | solution.py:632
  223.2 5.8 %last_apart.2.rest_3_ = f32[64,3,8,2048]{3,2,1,0:T(8,128)} custom-call(s32[1]{0:T(128)} %bitcast.me_ref, bf16[256,256]{1,0:T(8,128)(2,1)} %constant.14.clone.order_ref, bf16[8,4,224,128]{3,2,1,0:T(8,128)(2,1)} %all-to-all-done.3.x_ref.got_ref.refs_0_, bf16[8,4,128,384]{3,2,1,0:T(8,128)(2,1)} %all-to-all-done.1.x_ref.own_ref, ...), custom_call_target="tpu_custom_call", output_to_operand_aliasing={{}: (7, {})} | custom-call | flops 999999995904 | bytes 1 | tf_op jit(solution)/shard_map/last_apart/pallas_call | solution.py:577
  229.0 0.0 collective-permute-done.10.rest_1_
  229.0 4.0 %collective-permute-done.11.rest_2_ = bf16[8,64,384]{2,1,0:T(8,128)(2,1)} collective-permute-done((bf16[8,64,384]{2,1,0:T(8,128)(2,1)}, bf16[8,64,384]{2,1,0:T(8,128)(2,1)}, u32[]{:S(2)}, u32[]{:S(2)}) %collective-permute-start.11) | collective-permute-done | bytes 393248 | tf_op jit(solution)/shard_map/ppermute | solution.py:623
  232.9 5.8 %last_apart.3.refs_2_.rest_4_ = f32[64,3,8,2048]{3,2,1,0:T(8,128)} custom-call(s32[1]{0:T(128)} %bitcast.me_ref, bf16[256,256]{1,0:T(8,128)(2,1)} %constant.14.clone.order_ref, bf16[8,4,224,128]{3,2,1,0:T(8,128)(2,1)} %all-to-all-done.3.x_ref.got_ref.refs_0_, bf16[8,4,128,384]{3,2,1,0:T(8,128)(2,1)} %all-to-all-done.1.x_ref.own_ref, ...), custom_call_target="tpu_custom_call", output_to_operand_aliasing={{}: (7, {})} | custom-call | flops 999999995904 | bytes 1 | tf_op jit(solution)/shard_map/last_apart/pallas_call | solution.py:577
  238.7 6.8 %mark.1 = (f32[64,3,8,1024]{3,2,1,0:T(8,128)}, f32[512,128]{1,0:T(8,128)}) custom-call(bf16[8,4,224,128]{3,2,1,0:T(8,128)(2,1)} %all-to-all-done.3.x_ref.got_ref.refs_0_, f32[64,3,8,1024]{3,2,1,0:T(8,128)} %get-tuple-element.48.refs_1_, f32[64,3,8,2048]{3,2,1,0:T(8,128)} %last_apart.3.refs_2_.rest_4_), custom_call_target="tpu_custom_call" | custom-call | flops 1 | bytes 1 | tf_op jit(solution)/shard_map/mark/pallas_call | solution.py:476
  245.5 50.8 %all-to-all-done.4 = bf16[32,128,384]{2,1,0:T(8,128)(2,1)} async-done(((bf16[32,128,384]{2,1,0:T(8,128)(2,1)}), bf16[32,128,384]{2,1,0:T(8,128)(2,1)}, u32[]{:S(2)}, u32[]{:S(2)}) %all-to-all-start.4) | async-done | bytes 3145760 | tf_op jit(solution)/shard_map/all_to_all | solution.py:632
  296.3 7.4 %last.1 = f32[64,3,8,2048]{3,2,1,0:T(8,128)} custom-call(bf16[128,128]{1,0:T(8,128)(2,1)} %constant.15.clone.order_ref, bf16[8,4,128,384]{3,2,1,0:T(8,128)(2,1)} %bitcast.16.rest_0_.rest_1_, bf16[8,4,128,384]{3,2,1,0:T(8,128)(2,1)} %bitcast.16.rest_0_.rest_1_, f32[512,128]{1,0:T(8,128)} %get-tuple-element.51.rest_2_, ...), custom_call_target="tpu_custom_call", output_to_operand_aliasing={{}: (5, {})} | custom-call | flops 1 | bytes 1 | tf_op jit(solution)/shard_map/last/pallas_call | solution.py:517
  (14 shorter events, 0.0 us)
Async XLA Ops:
  3.8 77.6 %all-to-all-start = ((bf16[32,128,384]{2,1,0:T(8,128)(2,1)}), bf16[32,128,384]{2,1,0:T(8,128)(2,1)S(1)}, u32[]{:S(2)}, u32[]{:S(2)}) async-start(bf16[32,128,384]{2,1,0:T(8,128)(2,1)} %bitcast.29), calls=%async_computation | async-start | bytes 6291456 | tf_op jit(solution)/shard_map/all_to_all | solution.py:632
  53.1 4.3 %copy-start.3 = (s32[1,128]{1,0:T(1,128)S(1)}, s32[1,128]{1,0:T(1,128)}, u32[]{:S(2)}) copy-start(s32[1,128]{1,0:T(1,128)} %param.24) | copy-start | bytes 1540
  53.1 5.1 %copy-start.2 = (s32[1,128]{1,0:T(1,128)S(1)}, s32[1,128]{1,0:T(1,128)}, u32[]{:S(2)}) copy-start(s32[1,128]{1,0:T(1,128)} %owner_row.1) | copy-start | bytes 1540
  61.0 24.8 %copy-start.1 = (f32[2048]{0:T(1024)S(1)}, f32[2048]{0:T(1024)}, u32[]{:S(2)}) copy-start(f32[2048]{0:T(1024)} %param.21) | copy-start | bytes 24580
  64.8 46.8 %collective-permute-start.3 = (bf16[8,224,128]{2,1,0:T(8,128)(2,1)}, bf16[8,224,128]{2,1,0:T(8,128)(2,1)}, u32[]{:S(2)}, u32[]{:S(2)}) collective-permute-start(bf16[8,224,128]{2,1,0:T(8,128)(2,1)} %get-tuple-element.41), channel_id=1, source_target_pairs={{0,1},{1,0},{2,3},{3,2},{4,5},{5,4},{6,7},{7,6},{8,9},{9,8},{10,11... | collective-permute-start | bytes 1376264 | tf_op jit(solution)/shard_map/ppermute | solution.py:623
  81.4 5.8 %copy-start = (bf16[32,128,384]{2,1,0:T(8,128)(2,1)}, bf16[32,128,384]{2,1,0:T(8,128)(2,1)S(1)}, u32[]{:S(2)}) copy-start(bf16[32,128,384]{2,1,0:T(8,128)(2,1)S(1)} %all-to-all-done) | copy-start | bytes 9437188
  81.4 47.7 %collective-permute-start.4 = (bf16[8,224,128]{2,1,0:T(8,128)(2,1)}, bf16[8,224,128]{2,1,0:T(8,128)(2,1)}, u32[]{:S(2)}, u32[]{:S(2)}) collective-permute-start(bf16[8,224,128]{2,1,0:T(8,128)(2,1)} %get-tuple-element.42), channel_id=1, source_target_pairs={{0,2},{1,3},{2,0},{3,1},{4,6},{5,7},{6,4},{7,5},{8,10},{9,11},{10,... | collective-permute-start | bytes 1376264 | tf_op jit(solution)/shard_map/ppermute | solution.py:623
  81.4 58.5 %collective-permute-start.5 = (bf16[8,224,128]{2,1,0:T(8,128)(2,1)}, bf16[8,224,128]{2,1,0:T(8,128)(2,1)}, u32[]{:S(2)}, u32[]{:S(2)}) collective-permute-start(bf16[8,224,128]{2,1,0:T(8,128)(2,1)} %get-tuple-element.43), channel_id=1, source_target_pairs={{0,3},{1,2},{2,1},{3,0},{4,7},{5,6},{6,5},{7,4},{8,11},{9,10},{10,... | collective-permute-start | bytes 1376264 | tf_op jit(solution)/shard_map/ppermute | solution.py:623
  81.9 79.3 %collective-permute-start = (bf16[8,64,384]{2,1,0:T(8,128)(2,1)}, bf16[8,64,384]{2,1,0:T(8,128)(2,1)}, u32[]{:S(2)}, u32[]{:S(2)}) collective-permute-start(bf16[8,64,384]{2,1,0:T(8,128)(2,1)} %get-tuple-element.31), channel_id=1, source_target_pairs={{0,1},{1,0},{2,3},{3,2},{4,5},{5,4},{6,7},{7,6},{8,9},{9,8},{10,11... | collective-permute-start | bytes 1179656 | tf_op jit(solution)/shard_map/ppermute | solution.py:623
  87.2 74.7 %collective-permute-start.1 = (bf16[8,64,384]{2,1,0:T(8,128)(2,1)}, bf16[8,64,384]{2,1,0:T(8,128)(2,1)}, u32[]{:S(2)}, u32[]{:S(2)}) collective-permute-start(bf16[8,64,384]{2,1,0:T(8,128)(2,1)} %get-tuple-element.38), channel_id=1, source_target_pairs={{0,2},{1,3},{2,0},{3,1},{4,6},{5,7},{6,4},{7,5},{8,10},{9,11},{10,... | collective-permute-start | bytes 1179656 | tf_op jit(solution)/shard_map/ppermute | solution.py:623
  107.1 42.4 %all-to-all-start.1 = ((bf16[8,4,128,384]{3,2,1,0:T(8,128)(2,1)}), bf16[8,4,128,384]{3,2,1,0:T(8,128)(2,1)}, u32[]{:S(2)}, u32[]{:S(2)}) async-start(bf16[8,4,128,384]{3,2,1,0:T(8,128)(2,1)} %depth.3.refs_4_), calls=%async_computation.1 | async-start | bytes 6291456 | tf_op jit(solution)/shard_map/all_to_all | solution.py:628
  111.6 53.9 %collective-permute-start.2 = (bf16[8,64,384]{2,1,0:T(8,128)(2,1)}, bf16[8,64,384]{2,1,0:T(8,128)(2,1)}, u32[]{:S(2)}, u32[]{:S(2)}) collective-permute-start(bf16[8,64,384]{2,1,0:T(8,128)(2,1)} %get-tuple-element.39), channel_id=1, source_target_pairs={{0,3},{1,2},{2,1},{3,0},{4,7},{5,6},{6,5},{7,4},{8,11},{9,10},{10,... | collective-permute-start | bytes 1179656 | tf_op jit(solution)/shard_map/ppermute | solution.py:623
  149.5 28.2 %all-to-all-start.3 = ((bf16[8,4,224,128]{3,2,1,0:T(8,128)(2,1)}), bf16[8,4,224,128]{3,2,1,0:T(8,128)(2,1)}, u32[]{:S(2)}, u32[]{:S(2)}) async-start(bf16[8,4,224,128]{3,2,1,0:T(8,128)(2,1)} %join.2.rest_0_), calls=%async_computation.3 | async-start | bytes 3670016 | tf_op jit(solution)/shard_map/all_to_all | solution.py:628
  156.2 41.0 %collective-permute-start.7 = (bf16[8,64,384]{2,1,0:T(8,128)(2,1)}, bf16[8,64,384]{2,1,0:T(8,128)(2,1)}, u32[]{:S(2)}, u32[]{:S(2)}) collective-permute-start(bf16[8,64,384]{2,1,0:T(8,128)(2,1)} %get-tuple-element.46), channel_id=1, source_target_pairs={{0,2},{1,3},{2,0},{3,1},{4,6},{5,7},{6,4},{7,5},{8,10},{9,11},{10,... | collective-permute-start | bytes 1179656 | tf_op jit(solution)/shard_map/ppermute | solution.py:623
  158.9 44.1 %collective-permute-start.6 = (bf16[8,64,384]{2,1,0:T(8,128)(2,1)}, bf16[8,64,384]{2,1,0:T(8,128)(2,1)}, u32[]{:S(2)}, u32[]{:S(2)}) collective-permute-start(bf16[8,64,384]{2,1,0:T(8,128)(2,1)} %get-tuple-element.44.rest_0_), channel_id=1, source_target_pairs={{0,1},{1,0},{2,3},{3,2},{4,5},{5,4},{6,7},{7,6},{8,9},{9,8},{10,11... | collective-permute-start | bytes 1179656 | tf_op jit(solution)/shard_map/ppermute | solution.py:623
  161.2 41.9 %collective-permute-start.8 = (bf16[8,64,384]{2,1,0:T(8,128)(2,1)}, bf16[8,64,384]{2,1,0:T(8,128)(2,1)}, u32[]{:S(2)}, u32[]{:S(2)}) collective-permute-start(bf16[8,64,384]{2,1,0:T(8,128)(2,1)} %get-tuple-element.47), channel_id=1, source_target_pairs={{0,3},{1,2},{2,1},{3,0},{4,7},{5,6},{6,5},{7,4},{8,11},{9,10},{10,... | collective-permute-start | bytes 1179656 | tf_op jit(solution)/shard_map/ppermute | solution.py:623
  161.9 67.0 %collective-permute-start.10 = (bf16[8,64,384]{2,1,0:T(8,128)(2,1)}, bf16[8,64,384]{2,1,0:T(8,128)(2,1)}, u32[]{:S(2)}, u32[]{:S(2)}) collective-permute-start(bf16[8,64,384]{2,1,0:T(8,128)(2,1)} %get-tuple-element.49), channel_id=1, source_target_pairs={{0,2},{1,3},{2,0},{3,1},{4,6},{5,7},{6,4},{7,5},{8,10},{9,11},{10,... | collective-permute-start | bytes 1179656 | tf_op jit(solution)/shard_map/ppermute | solution.py:623
  165.6 67.4 %collective-permute-start.9 = (bf16[8,64,384]{2,1,0:T(8,128)(2,1)}, bf16[8,64,384]{2,1,0:T(8,128)(2,1)}, u32[]{:S(2)}, u32[]{:S(2)}) collective-permute-start(bf16[8,64,384]{2,1,0:T(8,128)(2,1)} %get-tuple-element.45.refs_4_), channel_id=1, source_target_pairs={{0,1},{1,0},{2,3},{3,2},{4,5},{5,4},{6,7},{7,6},{8,9},{9,8},{10,11... | collective-permute-start | bytes 1179656 | tf_op jit(solution)/shard_map/ppermute | solution.py:623
  177.7 25.9 %all-to-all-start.2 = ((bf16[8,4,64,384]{3,2,1,0:T(8,128)(2,1)}), bf16[8,4,64,384]{3,2,1,0:T(8,128)(2,1)}, u32[]{:S(2)}, u32[]{:S(2)}) async-start(bf16[8,4,64,384]{3,2,1,0:T(8,128)(2,1)} %join.3.rest_0_), calls=%async_computation.2 | async-start | bytes 3145728 | tf_op jit(solution)/shard_map/all_to_all | solution.py:628
  197.2 35.7 %collective-permute-start.11 = (bf16[8,64,384]{2,1,0:T(8,128)(2,1)}, bf16[8,64,384]{2,1,0:T(8,128)(2,1)}, u32[]{:S(2)}, u32[]{:S(2)}) collective-permute-start(bf16[8,64,384]{2,1,0:T(8,128)(2,1)} %get-tuple-element.50), channel_id=1, source_target_pairs={{0,3},{1,2},{2,1},{3,0},{4,7},{5,6},{6,5},{7,4},{8,11},{9,10},{10,... | collective-permute-start | bytes 1179656 | tf_op jit(solution)/shard_map/ppermute | solution.py:623
  218.6 77.7 %all-to-all-start.4 = ((bf16[32,128,384]{2,1,0:T(8,128)(2,1)}), bf16[32,128,384]{2,1,0:T(8,128)(2,1)}, u32[]{:S(2)}, u32[]{:S(2)}) async-start(bf16[32,128,384]{2,1,0:T(8,128)(2,1)} %bitcast.30), calls=%async_computation.4 | async-start | bytes 6291456 | tf_op jit(solution)/shard_map/all_to_all | solution.py:632

commit v4 on v3

--- a/solution.py
+++ b/solution.py
@@ -681,7 +681,7 @@
 
     (field,) = fields
     marked = (marked.reshape(ways, planes, MOST, comps * BLOCK), labels[0].reshape(ways, planes, MOST, BLOCK))
-    sent3 = outward(3, (field,))
+    sent3 = outward(3, (field, metric_col))
     sent2 = outward(2, (sent3[0],), marked)
     later2, later3 = lax.optimization_barrier((sent2[EARLY:], sent3[EARLY:], arrived))[:2]
     come2 = across(tuple(sent2[1:EARLY]) + tuple(later2))

time: 305 us -> 304 us (level)
  no operation moved by 1% of the time
where the time goes in v4:
time: 304 us; the launch traced here: 302 us
  Pallas kernels  143 us (47%)
  waiting for transfers between devices  118 us (39%)
  starting transfers between devices  38 us (12%)
    all_to_all x2, waiting for transfers between devices, exchange(): return lax.all_to_all(x, AXES, split_axis=0, concat_axis=0, tiled=True)  65.9 us
    pallas_call x3, Pallas kernels, depth(): pl.pallas_call(functools.partial(depth_body, count, slab, block, len(extr...  50.1 us
    pallas_call x1, Pallas kernels, near(): pl.pallas_call(functools.partial(near_body, planes, comps, len(after), ne...  43.3 us
    ppermute x12, waiting for transfers between devices, across(): lax.ppermute(piece, 'col', [(c, c ^ k) for c in range(ways)])  37 us
    all_to_all x3, waiting for transfers between devices, along(): return lax.all_to_all(x, 'row', split_axis=0, concat_axis=0, tiled=True)  15.2 us
    ppermute x12, starting transfers between devices, across(): lax.ppermute(piece, 'col', [(c, c ^ k) for c in range(ways)])  14.4 us
    all_to_all x3, starting transfers between devices, along(): return lax.all_to_all(x, 'row', split_axis=0, concat_axis=0, tiled=True)  13.1 us
    pallas_call x2, Pallas kernels, last_apart(): pl.pallas_call(functools.partial(last_apart_body, comps, group, columns /...  11.6 us
  transfers between devices with their start and end apart: 17, of which 8 were waited for; matrix products, arithmetic and copies ran while one was open for 1% of the time, Pallas kernels for 43%

profile of v4, /device:TPU:8, one launch (start us, length us, event | category | flops | bytes accessed | tf_op | source)
XLA Modules:
  0.0 302.4 jit_solution(6244854264016667984)
XLA Ops:
  0.0 3.8 %pack.1.rest_0_ = bf16[8,4,128,384]{3,2,1,0:T(8,128)(2,1)} custom-call(bf16[192,192]{1,0:T(8,128)(2,1)} %constant.13.clone.order_ref, bf16[1536,2048]{1,0:T(8,128)(2,1)} %bitcast.19), custom_call_target="tpu_custom_call" | custom-call | flops 1 | bytes 1 | tf_op jit(solution)/shard_map/pack/pallas_call | solution.py:92
  3.8 6.0 %all-to-all-start = ((bf16[32,128,384]{2,1,0:T(8,128)(2,1)}), bf16[32,128,384]{2,1,0:T(8,128)(2,1)S(1)}, u32[]{:S(2)}, u32[]{:S(2)}) async-start(bf16[32,128,384]{2,1,0:T(8,128)(2,1)} %bitcast.29), calls=%async_computation | async-start | bytes 6291456 | tf_op jit(solution)/shard_map/all_to_all | solution.py:632
  9.8 0.0 copy-start.1
  9.8 43.3 %near.1 = (f32[64,3,8,2048]{3,2,1,0:T(8,128)}, f32[64,3,8,1024]{3,2,1,0:T(8,128)}) custom-call(bf16[1536,2048]{1,0:T(8,128)(2,1)} %bitcast.20, bf16[2048,2048]{1,0:T(8,128)(2,1)} %dx_ref.1, bf16[8,8]{1,0:T(8,128)(2,1)} %dy_ref.1, f32[1,2048]{1,0:T(1,128)} %bitcast.35, f32[1,8]{1,0:T(1,128)} %bitcast.38, bf16[8,4,128,384]{3,2,1,0:T(8,128)(2,1)} %pack.1.rest_0_), custom_call_target="tpu_custom_call" | custom-call | flops 1 | bytes 1 | tf_op jit(solution)/shard_map/near/pallas_call | solution.py:371
  53.2 1.4 copy.22.rest_5_.m_ref
  54.5 3.7 %pack_apart.2 = (bf16[8,64,384]{2,1,0:T(8,128)(2,1)}, bf16[8,64,384]{2,1,0:T(8,128)(2,1)}, bf16[8,64,384]{2,1,0:T(8,128)(2,1)}, bf16[8,64,384]{2,1,0:T(8,128)(2,1)}) custom-call(s32[1]{0:T(128)} %bitcast.me_ref, bf16[384,384]{1,0:T(8,128)(2,1)} %constant.12.clone.order_ref, bf16[1536,2048]{1,0:T(8,128)(2,1)} %bitcast.21, bf16[1536,2048]{1,0:T(8,128)(2,1)} %bitcast.22, ...), custom_call_target="tpu_custom_call" | custom-call | flops 1 | bytes 1 | tf_op jit(solution)/shard_map/pack_apart/pallas_call | solution.py:140
  58.9 0.7 copy.24.block_col
  59.6 0.7 copy.23.owner_col
  60.3 2.0 markers.1
  62.3 3.8 %pack_apart.3 = (bf16[8,224,128]{2,1,0:T(8,128)(2,1)}, bf16[8,224,128]{2,1,0:T(8,128)(2,1)}, bf16[8,224,128]{2,1,0:T(8,128)(2,1)}, bf16[8,224,128]{2,1,0:T(8,128)(2,1)}) custom-call(s32[1]{0:T(128)} %bitcast.me_ref, bf16[384,384]{1,0:T(8,128)(2,1)} %constant.12.clone.order_ref, bf16[1536,2048]{1,0:T(8,128)(2,1)} %bitcast.25, bf16[1536,2048]{1,0:T(8,128)(2,1)} %bitcast.26, ...), custom_call_target="tpu_custom_call" | custom-call | flops 1 | bytes 1 | tf_op jit(solution)/shard_map/pack_apart/pallas_call | solution.py:140
  66.1 0.3 collective-permute-start.3
  66.4 15.0 %all-to-all-done = bf16[32,128,384]{2,1,0:T(8,128)(2,1)S(1)} async-done(((bf16[32,128,384]{2,1,0:T(8,128)(2,1)}), bf16[32,128,384]{2,1,0:T(8,128)(2,1)S(1)}, u32[]{:S(2)}, u32[]{:S(2)}) %all-to-all-start) | async-done | bytes 3145760 | tf_op jit(solution)/shard_map/all_to_all | solution.py:632
  81.4 0.5 collective-permute-start.5
  81.9 3.9 %collective-permute-start = (bf16[8,64,384]{2,1,0:T(8,128)(2,1)}, bf16[8,64,384]{2,1,0:T(8,128)(2,1)}, u32[]{:S(2)}, u32[]{:S(2)}) collective-permute-start(bf16[8,64,384]{2,1,0:T(8,128)(2,1)} %get-tuple-element.31), channel_id=1, source_target_pairs={{0,1},{1,0},{2,3},{3,2},{4,5},{5,4},{6,7},{7,6},{8,9},{9,8},{10,11... | collective-permute-start | bytes 1179656 | tf_op jit(solution)/shard_map/ppermute | solution.py:623
  85.8 20.0 %depth.3.refs_4_ = bf16[8,4,128,384]{3,2,1,0:T(8,128)(2,1)} custom-call(s32[1]{0:T(128)} %bitcast.me_ref, bf16[8,4,128,384]{3,2,1,0:T(8,128)(2,1)} %bitcast.31, bf16[2048,2048]{1,0:T(8,128)(2,1)} %d_ref.5, f32[2048,1]{1,0:T(8,128)} %copy.22.rest_5_.m_ref, bf16[8,224,128]{2,1,0:T(8,128)(2,1)} %get-tuple-element.40.rest_0_.refs_0_), custom_call_target="tpu_custom_call" | custom-call | flops 1 | bytes 1 | tf_op jit(solution)/shard_map/depth/pallas_call | solution.py:254
  105.7 4.5 %all-to-all-start.1 = ((bf16[8,4,128,384]{3,2,1,0:T(8,128)(2,1)}), bf16[8,4,128,384]{3,2,1,0:T(8,128)(2,1)}, u32[]{:S(2)}, u32[]{:S(2)}) async-start(bf16[8,4,128,384]{3,2,1,0:T(8,128)(2,1)} %depth.3.refs_4_), calls=%async_computation.1 | async-start | bytes 6291456 | tf_op jit(solution)/shard_map/all_to_all | solution.py:628
  110.2 1.3 collective-permute-start.2
  111.6 17.5 %collective-permute-done.4.refs_2_ = bf16[8,224,128]{2,1,0:T(8,128)(2,1)} collective-permute-done((bf16[8,224,128]{2,1,0:T(8,128)(2,1)}, bf16[8,224,128]{2,1,0:T(8,128)(2,1)}, u32[]{:S(2)}, u32[]{:S(2)}) %collective-permute-start.4) | collective-permute-done | bytes 458784 | tf_op jit(solution)/shard_map/ppermute | solution.py:623
  129.1 10.9 %collective-permute-done.5.refs_3_ = bf16[8,224,128]{2,1,0:T(8,128)(2,1)} collective-permute-done((bf16[8,224,128]{2,1,0:T(8,128)(2,1)}, bf16[8,224,128]{2,1,0:T(8,128)(2,1)}, u32[]{:S(2)}, u32[]{:S(2)}) %collective-permute-start.5) | collective-permute-done | bytes 458784 | tf_op jit(solution)/shard_map/ppermute | solution.py:623
  140.0 2.6 join.2.rest_0_
  142.5 5.6 %all-to-all-done.1.x_ref.own_ref = bf16[8,4,128,384]{3,2,1,0:T(8,128)(2,1)} async-done(((bf16[8,4,128,384]{3,2,1,0:T(8,128)(2,1)}), bf16[8,4,128,384]{3,2,1,0:T(8,128)(2,1)}, u32[]{:S(2)}, u32[]{:S(2)}) %all-to-all-start.1) | async-done | bytes 3145760 | tf_op jit(solution)/shard_map/all_to_all | solution.py:628
  148.1 4.3 %all-to-all-start.3 = ((bf16[8,4,224,128]{3,2,1,0:T(8,128)(2,1)}), bf16[8,4,224,128]{3,2,1,0:T(8,128)(2,1)}, u32[]{:S(2)}, u32[]{:S(2)}) async-start(bf16[8,4,224,128]{3,2,1,0:T(8,128)(2,1)} %join.2.rest_0_), calls=%async_computation.3 | async-start | bytes 3670016 | tf_op jit(solution)/shard_map/all_to_all | solution.py:628
  152.5 2.3 split.2
  154.8 2.7 collective-permute-start.7
  157.5 2.3 split.3
  159.8 0.8 collective-permute-start.8
  160.5 3.6 %collective-permute-start.10 = (bf16[8,64,384]{2,1,0:T(8,128)(2,1)}, bf16[8,64,384]{2,1,0:T(8,128)(2,1)}, u32[]{:S(2)}, u32[]{:S(2)}) collective-permute-start(bf16[8,64,384]{2,1,0:T(8,128)(2,1)} %get-tuple-element.49), channel_id=1, source_target_pairs={{0,2},{1,3},{2,0},{3,1},{4,6},{5,7},{6,4},{7,5},{8,10},{9,11},{10,... | collective-permute-start | bytes 1179656 | tf_op jit(solution)/shard_map/ppermute | solution.py:623
  164.1 0.0 collective-permute-done.2.refs_3_
  164.2 0.0 collective-permute-start.9
  164.2 2.5 join.3.rest_0_
  166.6 9.7 %all-to-all-done.3.x_ref.got_ref.refs_0_ = bf16[8,4,224,128]{3,2,1,0:T(8,128)(2,1)} async-done(((bf16[8,4,224,128]{3,2,1,0:T(8,128)(2,1)}), bf16[8,4,224,128]{3,2,1,0:T(8,128)(2,1)}, u32[]{:S(2)}, u32[]{:S(2)}) %all-to-all-start.3) | async-done | bytes 1835040 | tf_op jit(solution)/shard_map/all_to_all | solution.py:628
  176.3 4.3 %all-to-all-start.2 = ((bf16[8,4,64,384]{3,2,1,0:T(8,128)(2,1)}), bf16[8,4,64,384]{3,2,1,0:T(8,128)(2,1)}, u32[]{:S(2)}, u32[]{:S(2)}) async-start(bf16[8,4,64,384]{3,2,1,0:T(8,128)(2,1)} %join.3.rest_0_), calls=%async_computation.2 | async-start | bytes 3145728 | tf_op jit(solution)/shard_map/all_to_all | solution.py:628
  180.6 15.2 %depth.4.rest_0_ = bf16[8,4,128,384]{3,2,1,0:T(8,128)(2,1)} custom-call(s32[1]{0:T(128)} %bitcast.me_ref, bf16[8,4,224,128]{3,2,1,0:T(8,128)(2,1)} %all-to-all-done.3.x_ref.got_ref.refs_0_, bf16[2048,2048]{1,0:T(8,128)(2,1)} %d_ref.5, f32[2048,1]{1,0:T(8,128)} %copy.22.rest_5_.m_ref, bf16[8,4,64,384]{3,2,1,0:T(8,128)(2,1)} %join.3.rest_0_), custom_call_target="tpu_custom_call" | custom-call | flops 1 | bytes 1 | tf_op jit(solution)/shard_map/depth/pallas_call | solution.py:254
  195.8 0.0 collective-permute-done.7.refs_1_.rest_1_
  195.8 1.3 collective-permute-start.11
  197.1 4.6 %collective-permute-done.8.refs_2_.rest_2_ = bf16[8,64,384]{2,1,0:T(8,128)(2,1)} collective-permute-done((bf16[8,64,384]{2,1,0:T(8,128)(2,1)}, bf16[8,64,384]{2,1,0:T(8,128)(2,1)}, u32[]{:S(2)}, u32[]{:S(2)}) %collective-permute-start.8) | collective-permute-done | bytes 393248 | tf_op jit(solution)/shard_map/ppermute | solution.py:623
  201.7 0.0 collective-permute-done.6.refs_0_.rest_0_
  201.7 0.6 come.1.rest_1_
  202.3 0.0 all-to-all-done.2.x_ref
  202.3 15.0 %depth.5.rest_4_ = bf16[8,4,128,384]{3,2,1,0:T(8,128)(2,1)} custom-call(s32[1]{0:T(128)} %bitcast.me_ref, bf16[8,4,64,384]{3,2,1,0:T(8,128)(2,1)} %all-to-all-done.2.x_ref, bf16[2048,2048]{1,0:T(8,128)(2,1)} %d_ref.5, f32[2048,1]{1,0:T(8,128)} %copy.22.rest_5_.m_ref, bf16[8,4,128,384]{3,2,1,0:T(8,128)(2,1)} %depth.4.rest_0_, ...), custom_call_target="tpu_custom_call", output_to_operand_aliasing={{}: (4, {})} | custom-call | flops 1 | bytes 1 | tf_op jit(solution)/shard_map/depth/pallas_call | solution.py:254
  217.2 4.5 %all-to-all-start.4 = ((bf16[32,128,384]{2,1,0:T(8,128)(2,1)}), bf16[32,128,384]{2,1,0:T(8,128)(2,1)}, u32[]{:S(2)}, u32[]{:S(2)}) async-start(bf16[32,128,384]{2,1,0:T(8,128)(2,1)} %bitcast.30), calls=%async_computation.4 | async-start | bytes 6291456 | tf_op jit(solution)/shard_map/all_to_all | solution.py:632
  221.8 5.8 %last_apart.2.rest_3_ = f32[64,3,8,2048]{3,2,1,0:T(8,128)} custom-call(s32[1]{0:T(128)} %bitcast.me_ref, bf16[256,256]{1,0:T(8,128)(2,1)} %constant.14.clone.order_ref, bf16[8,4,224,128]{3,2,1,0:T(8,128)(2,1)} %all-to-all-done.3.x_ref.got_ref.refs_0_, bf16[8,4,128,384]{3,2,1,0:T(8,128)(2,1)} %all-to-all-done.1.x_ref.own_ref, ...), custom_call_target="tpu_custom_call", output_to_operand_aliasing={{}: (7, {})} | custom-call | flops 999999995904 | bytes 1 | tf_op jit(solution)/shard_map/last_apart/pallas_call | solution.py:577
  227.6 4.0 %collective-permute-done.11.rest_2_ = bf16[8,64,384]{2,1,0:T(8,128)(2,1)} collective-permute-done((bf16[8,64,384]{2,1,0:T(8,128)(2,1)}, bf16[8,64,384]{2,1,0:T(8,128)(2,1)}, u32[]{:S(2)}, u32[]{:S(2)}) %collective-permute-start.11) | collective-permute-done | bytes 393248 | tf_op jit(solution)/shard_map/ppermute | solution.py:623
  231.5 0.0 collective-permute-done.9.rest_0_
  231.5 5.8 %last_apart.3.refs_2_.rest_4_ = f32[64,3,8,2048]{3,2,1,0:T(8,128)} custom-call(s32[1]{0:T(128)} %bitcast.me_ref, bf16[256,256]{1,0:T(8,128)(2,1)} %constant.14.clone.order_ref, bf16[8,4,224,128]{3,2,1,0:T(8,128)(2,1)} %all-to-all-done.3.x_ref.got_ref.refs_0_, bf16[8,4,128,384]{3,2,1,0:T(8,128)(2,1)} %all-to-all-done.1.x_ref.own_ref, ...), custom_call_target="tpu_custom_call", output_to_operand_aliasing={{}: (7, {})} | custom-call | flops 999999995904 | bytes 1 | tf_op jit(solution)/shard_map/last_apart/pallas_call | solution.py:577
  237.3 6.8 %mark.1 = (f32[64,3,8,1024]{3,2,1,0:T(8,128)}, f32[512,128]{1,0:T(8,128)}) custom-call(bf16[8,4,224,128]{3,2,1,0:T(8,128)(2,1)} %all-to-all-done.3.x_ref.got_ref.refs_0_, f32[64,3,8,1024]{3,2,1,0:T(8,128)} %get-tuple-element.48.refs_1_, f32[64,3,8,2048]{3,2,1,0:T(8,128)} %last_apart.3.refs_2_.rest_4_), custom_call_target="tpu_custom_call" | custom-call | flops 1 | bytes 1 | tf_op jit(solution)/shard_map/mark/pallas_call | solution.py:476
  244.1 50.9 %all-to-all-done.4 = bf16[32,128,384]{2,1,0:T(8,128)(2,1)} async-done(((bf16[32,128,384]{2,1,0:T(8,128)(2,1)}), bf16[32,128,384]{2,1,0:T(8,128)(2,1)}, u32[]{:S(2)}, u32[]{:S(2)}) %all-to-all-start.4) | async-done | bytes 3145760 | tf_op jit(solution)/shard_map/all_to_all | solution.py:632
  295.0 7.4 %last.1 = f32[64,3,8,2048]{3,2,1,0:T(8,128)} custom-call(bf16[128,128]{1,0:T(8,128)(2,1)} %constant.15.clone.order_ref, bf16[8,4,128,384]{3,2,1,0:T(8,128)(2,1)} %bitcast.16.rest_0_.rest_1_, bf16[8,4,128,384]{3,2,1,0:T(8,128)(2,1)} %bitcast.16.rest_0_.rest_1_, f32[512,128]{1,0:T(8,128)} %get-tuple-element.51.rest_2_, ...), custom_call_target="tpu_custom_call", output_to_operand_aliasing={{}: (5, {})} | custom-call | flops 1 | bytes 1 | tf_op jit(solution)/shard_map/last/pallas_call | solution.py:517
  (14 shorter events, 0.0 us)
Async XLA Ops:
  3.8 77.6 %all-to-all-start = ((bf16[32,128,384]{2,1,0:T(8,128)(2,1)}), bf16[32,128,384]{2,1,0:T(8,128)(2,1)S(1)}, u32[]{:S(2)}, u32[]{:S(2)}) async-start(bf16[32,128,384]{2,1,0:T(8,128)(2,1)} %bitcast.29), calls=%async_computation | async-start | bytes 6291456 | tf_op jit(solution)/shard_map/all_to_all | solution.py:632
  9.8 43.3 %copy-start.1 = (f32[2048]{0:T(1024)S(1)}, f32[2048]{0:T(1024)}, u32[]{:S(2)}) copy-start(f32[2048]{0:T(1024)} %param.21) | copy-start | bytes 24580
  54.5 4.3 %copy-start.3 = (s32[1,128]{1,0:T(1,128)S(1)}, s32[1,128]{1,0:T(1,128)}, u32[]{:S(2)}) copy-start(s32[1,128]{1,0:T(1,128)} %param.24) | copy-start | bytes 1540
  54.5 5.1 %copy-start.2 = (s32[1,128]{1,0:T(1,128)S(1)}, s32[1,128]{1,0:T(1,128)}, u32[]{:S(2)}) copy-start(s32[1,128]{1,0:T(1,128)} %owner_row.1) | copy-start | bytes 1540
  66.1 44.1 %collective-permute-start.3 = (bf16[8,224,128]{2,1,0:T(8,128)(2,1)}, bf16[8,224,128]{2,1,0:T(8,128)(2,1)}, u32[]{:S(2)}, u32[]{:S(2)}) collective-permute-start(bf16[8,224,128]{2,1,0:T(8,128)(2,1)} %get-tuple-element.41), channel_id=1, source_target_pairs={{0,1},{1,0},{2,3},{3,2},{4,5},{5,4},{6,7},{7,6},{8,9},{9,8},{10,11... | collective-permute-start | bytes 1376264 | tf_op jit(solution)/shard_map/ppermute | solution.py:623
  81.4 4.4 %copy-start = (bf16[32,128,384]{2,1,0:T(8,128)(2,1)}, bf16[32,128,384]{2,1,0:T(8,128)(2,1)S(1)}, u32[]{:S(2)}) copy-start(bf16[32,128,384]{2,1,0:T(8,128)(2,1)S(1)} %all-to-all-done) | copy-start | bytes 9437188
  81.4 47.7 %collective-permute-start.4 = (bf16[8,224,128]{2,1,0:T(8,128)(2,1)}, bf16[8,224,128]{2,1,0:T(8,128)(2,1)}, u32[]{:S(2)}, u32[]{:S(2)}) collective-permute-start(bf16[8,224,128]{2,1,0:T(8,128)(2,1)} %get-tuple-element.42), channel_id=1, source_target_pairs={{0,2},{1,3},{2,0},{3,1},{4,6},{5,7},{6,4},{7,5},{8,10},{9,11},{10,... | collective-permute-start | bytes 1376264 | tf_op jit(solution)/shard_map/ppermute | solution.py:623
  81.4 58.6 %collective-permute-start.5 = (bf16[8,224,128]{2,1,0:T(8,128)(2,1)}, bf16[8,224,128]{2,1,0:T(8,128)(2,1)}, u32[]{:S(2)}, u32[]{:S(2)}) collective-permute-start(bf16[8,224,128]{2,1,0:T(8,128)(2,1)} %get-tuple-element.43), channel_id=1, source_target_pairs={{0,3},{1,2},{2,1},{3,0},{4,7},{5,6},{6,5},{7,4},{8,11},{9,10},{10,... | collective-permute-start | bytes 1376264 | tf_op jit(solution)/shard_map/ppermute | solution.py:623
  81.9 77.8 %collective-permute-start = (bf16[8,64,384]{2,1,0:T(8,128)(2,1)}, bf16[8,64,384]{2,1,0:T(8,128)(2,1)}, u32[]{:S(2)}, u32[]{:S(2)}) collective-permute-start(bf16[8,64,384]{2,1,0:T(8,128)(2,1)} %get-tuple-element.31), channel_id=1, source_target_pairs={{0,1},{1,0},{2,3},{3,2},{4,5},{5,4},{6,7},{7,6},{8,9},{9,8},{10,11... | collective-permute-start | bytes 1179656 | tf_op jit(solution)/shard_map/ppermute | solution.py:623
  85.8 74.7 %collective-permute-start.1 = (bf16[8,64,384]{2,1,0:T(8,128)(2,1)}, bf16[8,64,384]{2,1,0:T(8,128)(2,1)}, u32[]{:S(2)}, u32[]{:S(2)}) collective-permute-start(bf16[8,64,384]{2,1,0:T(8,128)(2,1)} %get-tuple-element.38), channel_id=1, source_target_pairs={{0,2},{1,3},{2,0},{3,1},{4,6},{5,7},{6,4},{7,5},{8,10},{9,11},{10,... | collective-permute-start | bytes 1179656 | tf_op jit(solution)/shard_map/ppermute | solution.py:623
  105.7 42.4 %all-to-all-start.1 = ((bf16[8,4,128,384]{3,2,1,0:T(8,128)(2,1)}), bf16[8,4,128,384]{3,2,1,0:T(8,128)(2,1)}, u32[]{:S(2)}, u32[]{:S(2)}) async-start(bf16[8,4,128,384]{3,2,1,0:T(8,128)(2,1)} %depth.3.refs_4_), calls=%async_computation.1 | async-start | bytes 6291456 | tf_op jit(solution)/shard_map/all_to_all | solution.py:628
  110.2 53.9 %collective-permute-start.2 = (bf16[8,64,384]{2,1,0:T(8,128)(2,1)}, bf16[8,64,384]{2,1,0:T(8,128)(2,1)}, u32[]{:S(2)}, u32[]{:S(2)}) collective-permute-start(bf16[8,64,384]{2,1,0:T(8,128)(2,1)} %get-tuple-element.39), channel_id=1, source_target_pairs={{0,3},{1,2},{2,1},{3,0},{4,7},{5,6},{6,5},{7,4},{8,11},{9,10},{10,... | collective-permute-start | bytes 1179656 | tf_op jit(solution)/shard_map/ppermute | solution.py:623
  148.1 28.2 %all-to-all-start.3 = ((bf16[8,4,224,128]{3,2,1,0:T(8,128)(2,1)}), bf16[8,4,224,128]{3,2,1,0:T(8,128)(2,1)}, u32[]{:S(2)}, u32[]{:S(2)}) async-start(bf16[8,4,224,128]{3,2,1,0:T(8,128)(2,1)} %join.2.rest_0_), calls=%async_computation.3 | async-start | bytes 3670016 | tf_op jit(solution)/shard_map/all_to_all | solution.py:628
  154.8 41.0 %collective-permute-start.7 = (bf16[8,64,384]{2,1,0:T(8,128)(2,1)}, bf16[8,64,384]{2,1,0:T(8,128)(2,1)}, u32[]{:S(2)}, u32[]{:S(2)}) collective-permute-start(bf16[8,64,384]{2,1,0:T(8,128)(2,1)} %get-tuple-element.46), channel_id=1, source_target_pairs={{0,2},{1,3},{2,0},{3,1},{4,6},{5,7},{6,4},{7,5},{8,10},{9,11},{10,... | collective-permute-start | bytes 1179656 | tf_op jit(solution)/shard_map/ppermute | solution.py:623
  157.5 44.2 %collective-permute-start.6 = (bf16[8,64,384]{2,1,0:T(8,128)(2,1)}, bf16[8,64,384]{2,1,0:T(8,128)(2,1)}, u32[]{:S(2)}, u32[]{:S(2)}) collective-permute-start(bf16[8,64,384]{2,1,0:T(8,128)(2,1)} %get-tuple-element.44.rest_0_), channel_id=1, source_target_pairs={{0,1},{1,0},{2,3},{3,2},{4,5},{5,4},{6,7},{7,6},{8,9},{9,8},{10,11... | collective-permute-start | bytes 1179656 | tf_op jit(solution)/shard_map/ppermute | solution.py:623
  159.8 41.9 %collective-permute-start.8 = (bf16[8,64,384]{2,1,0:T(8,128)(2,1)}, bf16[8,64,384]{2,1,0:T(8,128)(2,1)}, u32[]{:S(2)}, u32[]{:S(2)}) collective-permute-start(bf16[8,64,384]{2,1,0:T(8,128)(2,1)} %get-tuple-element.47), channel_id=1, source_target_pairs={{0,3},{1,2},{2,1},{3,0},{4,7},{5,6},{6,5},{7,4},{8,11},{9,10},{10,... | collective-permute-start | bytes 1179656 | tf_op jit(solution)/shard_map/ppermute | solution.py:623
  160.5 67.0 %collective-permute-start.10 = (bf16[8,64,384]{2,1,0:T(8,128)(2,1)}, bf16[8,64,384]{2,1,0:T(8,128)(2,1)}, u32[]{:S(2)}, u32[]{:S(2)}) collective-permute-start(bf16[8,64,384]{2,1,0:T(8,128)(2,1)} %get-tuple-element.49), channel_id=1, source_target_pairs={{0,2},{1,3},{2,0},{3,1},{4,6},{5,7},{6,4},{7,5},{8,10},{9,11},{10,... | collective-permute-start | bytes 1179656 | tf_op jit(solution)/shard_map/ppermute | solution.py:623
  164.2 67.4 %collective-permute-start.9 = (bf16[8,64,384]{2,1,0:T(8,128)(2,1)}, bf16[8,64,384]{2,1,0:T(8,128)(2,1)}, u32[]{:S(2)}, u32[]{:S(2)}) collective-permute-start(bf16[8,64,384]{2,1,0:T(8,128)(2,1)} %get-tuple-element.45.refs_4_), channel_id=1, source_target_pairs={{0,1},{1,0},{2,3},{3,2},{4,5},{5,4},{6,7},{7,6},{8,9},{9,8},{10,11... | collective-permute-start | bytes 1179656 | tf_op jit(solution)/shard_map/ppermute | solution.py:623
  176.3 26.0 %all-to-all-start.2 = ((bf16[8,4,64,384]{3,2,1,0:T(8,128)(2,1)}), bf16[8,4,64,384]{3,2,1,0:T(8,128)(2,1)}, u32[]{:S(2)}, u32[]{:S(2)}) async-start(bf16[8,4,64,384]{3,2,1,0:T(8,128)(2,1)} %join.3.rest_0_), calls=%async_computation.2 | async-start | bytes 3145728 | tf_op jit(solution)/shard_map/all_to_all | solution.py:628
  195.8 35.7 %collective-permute-start.11 = (bf16[8,64,384]{2,1,0:T(8,128)(2,1)}, bf16[8,64,384]{2,1,0:T(8,128)(2,1)}, u32[]{:S(2)}, u32[]{:S(2)}) collective-permute-start(bf16[8,64,384]{2,1,0:T(8,128)(2,1)} %get-tuple-element.50), channel_id=1, source_target_pairs={{0,3},{1,2},{2,1},{3,0},{4,7},{5,6},{6,5},{7,4},{8,11},{9,10},{10,... | collective-permute-start | bytes 1179656 | tf_op jit(solution)/shard_map/ppermute | solution.py:623
  217.2 77.7 %all-to-all-start.4 = ((bf16[32,128,384]{2,1,0:T(8,128)(2,1)}), bf16[32,128,384]{2,1,0:T(8,128)(2,1)}, u32[]{:S(2)}, u32[]{:S(2)}) async-start(bf16[32,128,384]{2,1,0:T(8,128)(2,1)} %bitcast.30), calls=%async_computation.4 | async-start | bytes 6291456 | tf_op jit(solution)/shard_map/all_to_all | solution.py:632
